TPU v7x, 32 devices: a whole 2x2x4 slice. The times are simulated.
32 devices in a mesh: dp: 16 (over z, y, x), head: 2 (over core).
Axes of the slice: x: 2, y: 2, z: 4, core: 2. Of those that a mesh axis runs over, the one named last changes fastest.
Arguments:
- inputs: bfloat16 [24576, 768], P(('dp', 'head')), may hold values from -6 to 6
- qkv_weight: bfloat16 [768, 3, 768], P('dp', None, 'head'), may hold values from -0.21875 to 0.21875
- qv_bias: float32 [2, 768], P(None, 'head'), may hold values from -3 to 3
- out_weight: bfloat16 [768, 768], P('dp', 'head'), may hold values from -2.5 to 2.5
- out_bias: float32 [768], replicated, may hold values from -1.75 to 1.75
- first_gain: float32 [768], replicated, may hold values from 0.5 to 1.5
- first_shift: float32 [768], replicated, may hold values from -1.75 to 1.75
- up_weight: bfloat16 [768, 3072], P('dp', 'head'), may hold values from -0.21875 to 0.21875
- up_bias: float32 [3072], P('head'), may hold values from -3 to 3
- down_weight: bfloat16 [768, 3072], P('dp', 'head'), may hold values from -0.15625 to 0.15625
- down_bias: float32 [768], replicated, may hold values from -1.75 to 1.75
- second_gain: float32 [768], replicated, may hold values from 0.5 to 1.5
- second_shift: float32 [768], replicated, may hold values from -1.75 to 1.75
- item_lengths: int32 [16, 2], P('dp'), may hold values from 0 to 1536, as said below
- random_blocks: int32 [16, 12, 24, 3], P('dp', 'head'), may hold values from 0 to 22, as said below
- out_grad: bfloat16 [24576, 768], P(('dp', 'head')), may hold values from -16 to 16
Outputs:
- layer_out: bfloat16 [24576, 768], P(('dp', 'head'))
- input_grad: bfloat16 [24576, 768], P(('dp', 'head'))
- grad_qkv: float32 [768, 3, 768], P('dp', None, 'head')
- grad_qv_bias: float32 [2, 768], P(None, 'head')
- grad_out: float32 [768, 768], P('dp', 'head')
- grad_out_bias: float32 [768], replicated
- grad_first_gain: float32 [768], replicated
- grad_first_shift: float32 [768], replicated
- grad_up: float32 [768, 3072], P('dp', 'head')
- grad_up_bias: float32 [3072], P('head')
- grad_down: float32 [768, 3072], P('dp', 'head')
- grad_down_bias: float32 [768], replicated
- grad_second_gain: float32 [768], replicated
- grad_second_shift: float32 [768], replicated
Inputs may be any that keep to these rules, and one draw needn't show every extreme that they name: `item_lengths`: each row lists a data group's items in order, then zeros. A group holds either one item of 1536 tokens (filling all 1536 rows; 1 group are such) or one to 2 items of 768 tokens; some group holds 2 items. `random_blocks`: for head h and block b of a group, where b is block r of an item of n blocks with 0 < r < n - 1: three different block numbers of that item, none of them 0, n - 1, r - 1, r or r + 1. Elsewhere 0.
All inputs are finite; a program needn't handle non-finite values.
Results may differ from a plain program's by a relative error of at most 0.019.
Values may be sent and summed in bfloat16 or wider, within the bound.
No kernel may reach another device: no remote copies, remote signals or barrier semaphores. Data moves between devices by JAX's collectives and lax.ppermute only.
A program may use at most 256 MiB of HBM per device.

v0:
```python
import math

import jax
import jax.numpy as jnp
from jax import lax
from jax.sharding import PartitionSpec as P

BLK = 64


norm_eps = 1e-06
negative = -1e30


def norm_forward(values, gain, shift):
    centered = values - jnp.mean(values, axis=-1, keepdims=True)
    inverse = lax.rsqrt(jnp.mean(centered * centered, axis=-1, keepdims=True) + norm_eps)
    normed = centered * inverse
    return (normed * gain + shift, normed, inverse)


def norm_backward(grad, normed, inverse, gain):
    scaled = grad * gain
    mean_one = jnp.mean(scaled, axis=-1, keepdims=True)
    mean_two = jnp.mean(scaled * normed, axis=-1, keepdims=True)
    return inverse * (scaled - mean_one - normed * mean_two)


def block_table(lengths, block_count):
    counts = lengths // BLK
    starts = jnp.cumsum(counts) - counts
    blocks = jnp.arange(block_count, dtype=jnp.int32)
    inside = (blocks[None, :] >= starts[:, None]) & (blocks[None, :] < (starts + counts)[:, None])
    member = inside.astype(jnp.int32)
    live = jnp.sum(member, axis=0)
    first = jnp.sum(member * starts[:, None], axis=0)
    item_blocks = jnp.sum(member * counts[:, None], axis=0)
    return (counts, starts, live, first, item_blocks)


def pick_blocks(source, chosen):
    heads = jnp.arange(source.shape[0])[:, None, None]
    picked = source[heads, chosen]
    return picked.reshape(picked.shape[0], picked.shape[1], -1, picked.shape[-1])


def to_steps(values, steps):
    shape = values.shape
    return jnp.swapaxes(values.reshape((shape[0], steps, shape[1] // steps) + shape[2:]), 0, 1)


def from_steps(values):
    values = jnp.swapaxes(values, 0, 1)
    shape = values.shape
    return values.reshape((shape[0], shape[1] * shape[2]) + shape[3:])


def global_window(start, count, row_count):
    used = count > 0
    start = jnp.where(used, start, 0)
    count = jnp.where(used, count, 1)
    row_blocks = jnp.arange(row_count, dtype=jnp.int32) // BLK
    key_mask = (row_blocks >= start) & (row_blocks < start + count)
    return (used, start * BLK, (start + count - 1) * BLK, key_mask)


def two_blocks(values, row_first, row_last):
    return jnp.concatenate(
        [
            lax.dynamic_slice_in_dim(values, row_first, BLK, 1),
            lax.dynamic_slice_in_dim(values, row_last, BLK, 1),
        ],
        axis=1,
    )


def put_blocks(target, update, row_first, row_last, used):
    placed = lax.dynamic_update_slice_in_dim(target, update[:, :BLK], row_first, 1)
    placed = lax.dynamic_update_slice_in_dim(placed, update[:, BLK:], row_last, 1)
    return jnp.where(used, placed, target)


def on_device(
    inputs,
    qkv_weight,
    qv_bias,
    out_weight,
    out_bias,
    first_gain,
    first_shift,
    up_weight,
    up_bias,
    down_weight,
    down_bias,
    second_gain,
    second_shift,
    item_lengths,
    random_blocks,
    out_grad,
):
    half = inputs.shape[0]
    width = inputs.shape[1]
    position = lax.axis_index("head")
    local_heads = random_blocks.shape[1]
    head_width = qkv_weight.shape[2]
    head_dim = head_width // local_heads
    scale = 1.0 / math.sqrt(head_dim)
    full_qkv, full_out, full_up, full_down = (
        lax.all_gather(qkv_weight, "dp", axis=0, tiled=True),
        lax.all_gather(out_weight, "dp", axis=0, tiled=True),
        lax.all_gather(up_weight, "dp", axis=0, tiled=True),
        lax.all_gather(down_weight, "dp", axis=0, tiled=True),
    )
    tokens = lax.all_gather(inputs, "head", axis=0, tiled=True)
    capacity = tokens.shape[0]
    block_count = capacity // BLK
    counts, starts, live, first, item_blocks = block_table(item_lengths[0], block_count)
    bias = jnp.stack([qv_bias[0], jnp.zeros_like(qv_bias[0]), qv_bias[1]])
    triple = (
        jnp.einsum("td,dcf->tcf", tokens, full_qkv, preferred_element_type=jnp.float32) + bias
    ).astype(jnp.bfloat16)
    queries = jnp.swapaxes(triple[:, 0].reshape(capacity, local_heads, head_dim), 0, 1)
    keys_all = jnp.swapaxes(triple[:, 1].reshape(capacity, local_heads, head_dim), 0, 1)
    values_all = jnp.swapaxes(triple[:, 2].reshape(capacity, local_heads, head_dim), 0, 1)
    key_blocks = keys_all.reshape(local_heads, block_count, BLK, head_dim)
    value_blocks = values_all.reshape(local_heads, block_count, BLK, head_dim)
    blocks = jnp.arange(block_count, dtype=jnp.int32)
    relative = blocks - first
    last = item_blocks - 1
    is_live = live > 0
    is_global = is_live & ((relative == 0) | (relative == last))
    sparse_blocks = is_live & jnp.logical_not(is_global)
    fixed_list = jnp.stack([first, first + last, blocks - 1, blocks, blocks + 1], axis=1)
    fixed_list = jnp.clip(
        jnp.where(is_live[:, None], fixed_list, blocks[:, None]), 0, block_count - 1
    )
    random_list = first[None, :, None] + random_blocks[0]
    random_list = jnp.clip(
        jnp.where(is_live[None, :, None], random_list, blocks[None, :, None]), 0, block_count - 1
    )
    key_list = jnp.concatenate(
        [jnp.broadcast_to(fixed_list[None], (local_heads,) + fixed_list.shape), random_list], axis=2
    )
    always = jnp.ones_like(is_live)
    fixed_valid = [
        is_live,
        is_live,
        is_live & (relative - 1 > 0),
        always,
        is_live & (relative + 1 < last),
    ]
    slot_valid = jnp.stack(fixed_valid + [is_live] * random_blocks.shape[-1], axis=1)
    key_valid = jnp.repeat(slot_valid, BLK, axis=1)
    qstep = math.gcd(block_count, max(512 // BLK, 1))
    steps = block_count // qstep
    query_steps = to_steps(queries.reshape(local_heads, block_count, BLK, head_dim), steps)
    chosen_steps = to_steps(key_list, steps)
    valid_steps = key_valid.reshape(steps, qstep, -1)

    def sparse_scores(query_blk, chosen, valid):
        near_keys = pick_blocks(key_blocks, chosen)
        near_values = pick_blocks(value_blocks, chosen)
        scores = (
            jnp.einsum("hqbe,hqke->hqbk", query_blk, near_keys, preferred_element_type=jnp.float32)
            * scale
        )
        return (jnp.where(valid[None, :, None, :], scores, negative), near_keys, near_values)

    def sparse_forward(pieces):
        query_blk, chosen, valid = pieces
        scores, near_keys, near_values = sparse_scores(query_blk, chosen, valid)
        top = jnp.max(scores, axis=-1, keepdims=True)
        expo = jnp.exp(scores - top)
        total = jnp.sum(expo, axis=-1, keepdims=True)
        probs = (expo / total).astype(jnp.bfloat16)
        mixed = jnp.einsum(
            "hqbk,hqke->hqbe", probs, near_values, preferred_element_type=jnp.float32
        )
        return (mixed, (top + jnp.log(total))[..., 0])

    mixed_steps, lse_steps = lax.map(sparse_forward, (query_steps, chosen_steps, valid_steps))
    mixed = from_steps(mixed_steps).reshape(local_heads, capacity, head_dim)
    lse = from_steps(lse_steps).reshape(local_heads, capacity)
    for slot_idx in range(item_lengths.shape[1]):
        used, row_first, row_last, key_mask = global_window(
            starts[slot_idx], counts[slot_idx], capacity
        )
        query_rows = two_blocks(queries, row_first, row_last)
        scores = (
            jnp.einsum("hqe,hke->hqk", query_rows, keys_all, preferred_element_type=jnp.float32)
            * scale
        )
        scores = jnp.where(key_mask[None, None, :], scores, negative)
        top = jnp.max(scores, axis=-1, keepdims=True)
        expo = jnp.exp(scores - top)
        total = jnp.sum(expo, axis=-1, keepdims=True)
        probs = (expo / total).astype(jnp.bfloat16)
        global_mixed = jnp.einsum(
            "hqk,hke->hqe", probs, values_all, preferred_element_type=jnp.float32
        )
        mixed = put_blocks(mixed, global_mixed, row_first, row_last, used)
        lse = put_blocks(lse, (top + jnp.log(total))[..., 0], row_first, row_last, used)
    attended = jnp.swapaxes(mixed.astype(jnp.bfloat16), 0, 1).reshape(capacity, head_width)
    part = attended
    proj = lax.psum_scatter(
        jnp.einsum("tf,df->td", part, full_out, preferred_element_type=jnp.float32).astype(
            jnp.bfloat16
        ),
        "head",
        scatter_dimension=0,
        tiled=True,
    ).astype(jnp.float32)
    normed_one_out, normed_one, inverse_one = norm_forward(
        proj + out_bias + inputs.astype(jnp.float32), first_gain, first_shift
    )
    hidden = lax.all_gather(normed_one_out.astype(jnp.bfloat16), "head", axis=0, tiled=True)
    upper = (
        jnp.einsum("td,df->tf", hidden, full_up, preferred_element_type=jnp.float32) + up_bias
    ).astype(jnp.bfloat16)
    active = jax.nn.gelu(upper.astype(jnp.float32), approximate=True).astype(jnp.bfloat16)
    part = active
    down = lax.psum_scatter(
        jnp.einsum("tf,df->td", part, full_down, preferred_element_type=jnp.float32).astype(
            jnp.bfloat16
        ),
        "head",
        scatter_dimension=0,
        tiled=True,
    ).astype(jnp.float32)
    normed_two_out, normed_two, inverse_two = norm_forward(
        down + down_bias + normed_one_out, second_gain, second_shift
    )
    live_rows = jnp.repeat(live, BLK).astype(jnp.float32)
    live_half = lax.dynamic_slice_in_dim(live_rows, position * half, half, 0)
    layer_out = (normed_two_out * live_half[:, None]).astype(jnp.bfloat16)
    cotangent = out_grad.astype(jnp.float32) * live_half[:, None]
    second_gain_part = jnp.sum(cotangent * normed_two, axis=0)
    second_shift_part = jnp.sum(cotangent, axis=0)
    grad_res_two = norm_backward(cotangent, normed_two, inverse_two, second_gain)
    down_bias_part = jnp.sum(grad_res_two, axis=0)
    grad_down_rows = lax.all_gather(grad_res_two.astype(jnp.bfloat16), "head", axis=0, tiled=True)
    grad_active = jnp.einsum(
        "td,df->tf", grad_down_rows, full_down, preferred_element_type=jnp.float32
    )
    down_local = jnp.einsum("td,tf->df", grad_down_rows, active, preferred_element_type=jnp.float32)

    def gelu_tanh(values):
        return jax.nn.gelu(values, approximate=True)

    gelu_pull = jax.vjp(gelu_tanh, upper.astype(jnp.float32))[1]
    grad_upper = gelu_pull(grad_active)[0].astype(jnp.bfloat16)
    up_bias_part = jnp.sum(grad_upper.astype(jnp.float32), axis=0)
    up_local = jnp.einsum("td,tf->df", hidden, grad_upper, preferred_element_type=jnp.float32)
    part = grad_upper
    grad_norm_one = (
        lax.psum_scatter(
            jnp.einsum("tf,df->td", part, full_up, preferred_element_type=jnp.float32).astype(
                jnp.bfloat16
            ),
            "head",
            scatter_dimension=0,
            tiled=True,
        ).astype(jnp.float32)
        + grad_res_two
    )
    first_gain_part = jnp.sum(grad_norm_one * normed_one, axis=0)
    first_shift_part = jnp.sum(grad_norm_one, axis=0)
    grad_res_one = norm_backward(grad_norm_one, normed_one, inverse_one, first_gain)
    out_bias_part = jnp.sum(grad_res_one, axis=0)
    grad_proj = lax.all_gather(grad_res_one.astype(jnp.bfloat16), "head", axis=0, tiled=True)
    grad_attended = jnp.einsum(
        "td,df->tf", grad_proj, full_out, preferred_element_type=jnp.float32
    ).astype(jnp.bfloat16)
    out_local = jnp.einsum("td,tf->df", grad_proj, attended, preferred_element_type=jnp.float32)
    grad_mixed = jnp.swapaxes(grad_attended.reshape(capacity, local_heads, head_dim), 0, 1)
    sparse_rows = jnp.repeat(sparse_blocks, BLK).astype(jnp.bfloat16)
    grad_sparse = grad_mixed * sparse_rows[None, :, None]
    grad_steps = to_steps(grad_sparse.reshape(local_heads, block_count, BLK, head_dim), steps)
    lse_blocks = to_steps(lse.reshape(local_heads, block_count, BLK), steps)

    def sparse_backward(carry, pieces):
        key_acc, value_acc = carry
        query_blk, chosen, valid, grad_blk, lse_blk = pieces
        scores, near_keys, near_values = sparse_scores(query_blk, chosen, valid)
        probs = jnp.where(valid[None, :, None, :], jnp.exp(scores - lse_blk[..., None]), 0.0)
        grad_probs = jnp.einsum(
            "hqbe,hqke->hqbk", grad_blk, near_values, preferred_element_type=jnp.float32
        )
        delta = jnp.sum(probs * grad_probs, axis=-1, keepdims=True)
        grad_scores = (probs * (grad_probs - delta)).astype(jnp.bfloat16)
        grad_query = (
            jnp.einsum(
                "hqbk,hqke->hqbe", grad_scores, near_keys, preferred_element_type=jnp.float32
            )
            * scale
        )
        grad_keys = (
            jnp.einsum(
                "hqbk,hqbe->hqke", grad_scores, query_blk, preferred_element_type=jnp.float32
            )
            * scale
        )
        grad_values = jnp.einsum(
            "hqbk,hqbe->hqke",
            probs.astype(jnp.bfloat16),
            grad_blk,
            preferred_element_type=jnp.float32,
        )
        shape = (grad_keys.shape[0], grad_keys.shape[1], chosen.shape[2], BLK, grad_keys.shape[-1])
        heads = jnp.arange(shape[0])[:, None, None]
        key_acc = key_acc.at[heads, chosen].add(grad_keys.reshape(shape))
        value_acc = value_acc.at[heads, chosen].add(grad_values.reshape(shape))
        return ((key_acc, value_acc), grad_query)

    empty_blocks = jnp.zeros((local_heads, block_count, BLK, head_dim), jnp.float32)
    (key_acc, value_acc), query_steps_grad = lax.scan(
        sparse_backward,
        (empty_blocks, empty_blocks),
        (query_steps, chosen_steps, valid_steps, grad_steps, lse_blocks),
    )
    query_grad = from_steps(query_steps_grad).reshape(local_heads, capacity, head_dim)
    key_grad = key_acc.reshape(local_heads, capacity, head_dim)
    value_grad = value_acc.reshape(local_heads, capacity, head_dim)
    for slot_idx in range(item_lengths.shape[1]):
        used, row_first, row_last, key_mask = global_window(
            starts[slot_idx], counts[slot_idx], capacity
        )
        query_rows = two_blocks(queries, row_first, row_last)
        grad_rows = two_blocks(grad_mixed, row_first, row_last)
        lse_rows = two_blocks(lse, row_first, row_last)
        scores = (
            jnp.einsum("hqe,hke->hqk", query_rows, keys_all, preferred_element_type=jnp.float32)
            * scale
        )
        probs = jnp.where(key_mask[None, None, :], jnp.exp(scores - lse_rows[..., None]), 0.0)
        grad_probs = jnp.einsum(
            "hqe,hke->hqk", grad_rows, values_all, preferred_element_type=jnp.float32
        )
        delta = jnp.sum(probs * grad_probs, axis=-1, keepdims=True)
        grad_scores = (probs * (grad_probs - delta)).astype(jnp.bfloat16)
        weight_used = used.astype(jnp.float32)
        global_query = (
            jnp.einsum("hqk,hke->hqe", grad_scores, keys_all, preferred_element_type=jnp.float32)
            * scale
        )
        query_grad = put_blocks(query_grad, global_query, row_first, row_last, used)
        key_grad = key_grad + weight_used * scale * jnp.einsum(
            "hqk,hqe->hke", grad_scores, query_rows, preferred_element_type=jnp.float32
        )
        value_grad = value_grad + weight_used * jnp.einsum(
            "hqk,hqe->hke",
            probs.astype(jnp.bfloat16),
            grad_rows,
            preferred_element_type=jnp.float32,
        )

    def to_rows(values):
        return jnp.swapaxes(values.astype(jnp.bfloat16), 0, 1).reshape(capacity, head_width)

    grad_triple = jnp.stack([to_rows(query_grad), to_rows(key_grad), to_rows(value_grad)], axis=1)
    qv_bias_part = jnp.stack(
        [
            jnp.sum(grad_triple[:, 0].astype(jnp.float32), axis=0),
            jnp.sum(grad_triple[:, 2].astype(jnp.float32), axis=0),
        ]
    )
    qkv_local = jnp.einsum("td,tcf->dcf", tokens, grad_triple, preferred_element_type=jnp.float32)
    part = grad_triple
    input_grad = (
        lax.psum_scatter(
            jnp.einsum("tcf,dcf->td", part, full_qkv, preferred_element_type=jnp.float32).astype(
                jnp.bfloat16
            ),
            "head",
            scatter_dimension=0,
            tiled=True,
        ).astype(jnp.float32)
        + grad_res_one
    ).astype(jnp.bfloat16)
    grad_qkv, grad_out, grad_up, grad_down = (
        lax.psum_scatter(qkv_local, "dp", scatter_dimension=0, tiled=True),
        lax.psum_scatter(out_local, "dp", scatter_dimension=0, tiled=True),
        lax.psum_scatter(up_local, "dp", scatter_dimension=0, tiled=True),
        lax.psum_scatter(down_local, "dp", scatter_dimension=0, tiled=True),
    )
    up_width = up_bias.shape[0]
    qv_full = lax.dynamic_update_slice_in_dim(
        jnp.zeros((2, width), jnp.float32), qv_bias_part, position * head_width, 1
    )
    up_full = lax.dynamic_update_slice_in_dim(
        jnp.zeros((up_width * lax.axis_size("head"),), jnp.float32),
        up_bias_part,
        position * up_width,
        0,
    )
    totals = lax.psum(
        (
            qv_full,
            up_full,
            out_bias_part,
            first_gain_part,
            first_shift_part,
            down_bias_part,
            second_gain_part,
            second_shift_part,
        ),
        ("dp", "head"),
    )
    grad_qv_bias = lax.dynamic_slice_in_dim(totals[0], position * head_width, head_width, 1)
    grad_up_bias = lax.dynamic_slice_in_dim(totals[1], position * up_width, up_width, 0)
    return (
        layer_out,
        input_grad,
        grad_qkv,
        grad_qv_bias,
        grad_out,
        totals[2],
        totals[3],
        totals[4],
        grad_up,
        grad_up_bias,
        grad_down,
        totals[5],
        totals[6],
        totals[7],
    )


def solution(mesh):
    in_specs = (
        P(("dp", "head"), None),
        P("dp", None, "head"),
        P(None, "head"),
        P("dp", "head"),
        P(),
        P(),
        P(),
        P("dp", "head"),
        P("head"),
        P("dp", "head"),
        P(),
        P(),
        P(),
        P("dp", None),
        P("dp", "head", None, None),
        P(("dp", "head"), None),
    )
    out_specs = (
        P(("dp", "head"), None),
        P(("dp", "head"), None),
        P("dp", None, "head"),
        P(None, "head"),
        P("dp", "head"),
        P(),
        P(),
        P(),
        P("dp", "head"),
        P("head"),
        P("dp", "head"),
        P(),
        P(),
        P(),
    )
    return jax.shard_map(
        on_device, mesh=mesh, in_specs=in_specs, out_specs=out_specs, check_vma=False
    )
```

profile of v0, /device:TPU:0, one launch (start us, length us, event | category | flops | bytes accessed | tf_op | source)
XLA Modules:
  0.0 1733.3 jit_solution(2711912428511761612)
XLA Ops:
  20.2 49.8 %all_gather.26 = bf16[768,384]{1,0:T(8,128)(2,1)} all-gather(bf16[48,384]{1,0:T(8,128)(2,1)} %param.23), channel_id=1, replica_groups=mesh['dp'=16,'head'=2] {'dp'}, dimensions={0}, use_global_device_ids=true | all-gather | bytes 626688 | tf_op jit(solution)/shard_map/all_gather | solution.py:110
  69.9 16.4 all-gather.10.cloned.1.call-done
  108.9 94.5 %while.26 = (s32[]{:T(128)}, bf16[3,6,8,64,64]{4,3,2,1,0:T(8,128)(2,1)}, f32[3,6,8,64]{3,2,1,0:T(8,128)}, pred[3,8,512]{2,1,0:T(8,128)(4,1)}, bf16[3,6,8,64,64]{...) while((s32[]{:T(128)}, ...), condition=%wide.region_7.8_spmd, body=%wide.region_4.7_spmd.sunk | while | flops 421527552 | bytes 71831760 | solution.py:181
  237.3 8.2 reduce-scatter.8.cloned.1.call-done
  251.0 61.0 %all-gather.14.cloned.1.call-done = bf16[768,1536]{1,0:T(8,128)(2,1)} async-done(((bf16[48,1536]{1,0:T(8,128)(2,1)}), bf16[768,1536]{1,0:T(8,128)(2,1)}) %all-gather.14.cloned.1.call-update) | async-done | bytes 2359312 | tf_op jit(solution)/shard_map/all_gather | solution.py:111
  312.0 11.8 all-gather.12.cloned.1.call-done
  323.9 8.4 add_convert_fusion
  332.2 58.2 %all-gather.16.cloned.1.call-done = bf16[768,1536]{1,0:T(8,128)(2,1)} async-done(((bf16[48,1536]{1,0:T(8,128)(2,1)}), bf16[768,1536]{1,0:T(8,128)(2,1)}) %all-gather.16.cloned.1.call-update) | async-done | bytes 2359312 | tf_op jit(solution)/shard_map/all_gather | solution.py:112
  390.4 10.5 convolution_convert_fusion.1
  418.8 12.2 all-gather.18.cloned.1.call-done
  431.0 12.7 convert_reduce_fusion
  451.1 11.2 reduce-scatter.12.cloned.1.call-done
  502.0 537.2 %while.27 = (s32[]{:T(128)}, f32[6,24,64,64]{3,2,1,0:T(8,128)}, f32[6,24,64,64]{3,2,1,0:T(8,128)}, bf16[3,6,8,64,64]{4,3,2,1,0:T(8,128)(2,1)}, s32[3,6,8,8]{3,2,...) while((s32[]{:T(128)}, f32[6,24,64,64]{3,2,1,0:T(8,128)}, ...), condition=%wide.region_27.28_spmd, body=%wide.region_23.27_spmd.sunk | while | flops 1027278336 | bytes 152664752 | solution.py:316
  516.5 8.1 fusion.197
  547.4 62.5 %scatter_fusion.1 = f32[6,24,64,64]{3,2,1,0:T(8,128)} fusion(f32[6,24,64,64]{3,2,1,0:T(8,128)} %get-tuple-element.615, s32[384]{0:T(512)S(1)} %reshape.609, f32[384,64,64]{2,1,0:T(8,128)} %bitcast.271), kind=kCustom, calls=%fused_computation.5.clone.1 | custom fusion | flops 1572864 | bytes 18877440 | tf_op jit(solution)/shard_map/while/body/eval_jaxpr/scatter-add | solution.py:312
  609.9 9.6 copy.244
  619.6 62.2 %scatter_fusion = f32[6,24,64,64]{3,2,1,0:T(8,128)} fusion(f32[6,24,64,64]{3,2,1,0:T(8,128)} %get-tuple-element.614, s32[384]{0:T(512)S(1)} %reshape.609, f32[384,64,64]{2,1,0:T(8,128)} %bitcast.270), kind=kCustom, calls=%fused_computation.4.clone.1 | custom fusion | flops 1572864 | bytes 18877440 | tf_op jit(solution)/shard_map/while/body/eval_jaxpr/scatter-add | solution.py:311
  696.0 8.1 fusion.197
  726.9 62.2 %scatter_fusion.1 = f32[6,24,64,64]{3,2,1,0:T(8,128)} fusion(f32[6,24,64,64]{3,2,1,0:T(8,128)} %get-tuple-element.615, s32[384]{0:T(512)S(1)} %reshape.609, f32[384,64,64]{2,1,0:T(8,128)} %bitcast.271), kind=kCustom, calls=%fused_computation.5.clone.1 | custom fusion | flops 1572864 | bytes 18877440 | tf_op jit(solution)/shard_map/while/body/eval_jaxpr/scatter-add | solution.py:312
  789.1 9.6 copy.244
  798.7 61.9 %scatter_fusion = f32[6,24,64,64]{3,2,1,0:T(8,128)} fusion(f32[6,24,64,64]{3,2,1,0:T(8,128)} %get-tuple-element.614, s32[384]{0:T(512)S(1)} %reshape.609, f32[384,64,64]{2,1,0:T(8,128)} %bitcast.270), kind=kCustom, calls=%fused_computation.4.clone.1 | custom fusion | flops 1572864 | bytes 18877440 | tf_op jit(solution)/shard_map/while/body/eval_jaxpr/scatter-add | solution.py:311
  874.8 8.1 fusion.197
  905.7 62.0 %scatter_fusion.1 = f32[6,24,64,64]{3,2,1,0:T(8,128)} fusion(f32[6,24,64,64]{3,2,1,0:T(8,128)} %get-tuple-element.615, s32[384]{0:T(512)S(1)} %reshape.609, f32[384,64,64]{2,1,0:T(8,128)} %bitcast.271), kind=kCustom, calls=%fused_computation.5.clone.1 | custom fusion | flops 1572864 | bytes 18877440 | tf_op jit(solution)/shard_map/while/body/eval_jaxpr/scatter-add | solution.py:312
  967.7 9.6 copy.244
  977.3 61.8 %scatter_fusion = f32[6,24,64,64]{3,2,1,0:T(8,128)} fusion(f32[6,24,64,64]{3,2,1,0:T(8,128)} %get-tuple-element.614, s32[384]{0:T(512)S(1)} %reshape.609, f32[384,64,64]{2,1,0:T(8,128)} %bitcast.270), kind=kCustom, calls=%fused_computation.4.clone.1 | custom fusion | flops 1572864 | bytes 18877440 | tf_op jit(solution)/shard_map/while/body/eval_jaxpr/scatter-add | solution.py:311
  1128.3 8.7 fusion.109
  1144.4 52.4 %all-reduce.1 = (f32[2,768]{1,0:T(2,128)S(1)}, f32[768]{0:T(1024)}, f32[768]{0:T(1024)}, f32[768]{0:T(1024)}, f32[3072]{0:T(1024)S(1)}, /*index=5*/f32[768]{0:T(1024)}, f32[768]{0:T(1024)}, f32[768]{0:T(1024)}) all-reduce(f32[2,768]{1,0:T(2,128)S(1)} %constant_dynamic-update-slice_fusion.5, ...), channel_id=1, replica_groups=mesh['dp'=16,'head'=2] {'dp','head'}, use_global_device_ids=true, to_apply=%region_34.35 | all-reduce | flops 9216 | bytes 73728 | tf_op jit(solution)/shard_map/psum | solution.py:396
  1198.0 102.1 %all-reduce.4.cloned.1.call-done = f32[768,3,384]{2,1,0:T(4,128)} async-done(((f32[768,3,384]{2,1,0:T(4,128)}), f32[768,3,384]{2,1,0:T(4,128)}) %all-reduce.4.cloned.1.call-update) | async-done | bytes 3538960
  1301.9 9.3 reduce-scatter.14.cloned.1.call-done
  1313.7 142.3 %reduce-scatter.18.cloned.1.call-done = f32[48,1536]{1,0:T(8,128)} async-done(((f32[768,1536]{1,0:T(8,128)}), f32[48,1536]{1,0:T(8,128)}) %reduce-scatter.18.cloned.1.call-update) | async-done | bytes 294928 | tf_op jit(solution)/shard_map/reduce_scatter | solution.py:383
  1456.1 141.9 %reduce-scatter.20.cloned.1.call-done = f32[48,1536]{1,0:T(8,128)} async-done(((f32[768,1536]{1,0:T(8,128)}), f32[48,1536]{1,0:T(8,128)}) %reduce-scatter.20.cloned.1.call-update) | async-done | bytes 294928 | tf_op jit(solution)/shard_map/reduce_scatter | solution.py:384
  1598.0 128.5 %reduce-scatter.16.cloned.1.call-done = f32[48,384]{1,0:T(8,128)} async-done(((f32[768,384]{1,0:T(8,128)}), f32[48,384]{1,0:T(8,128)}) %reduce-scatter.16.cloned.1.call-update) | async-done | bytes 73744 | tf_op jit(solution)/shard_map/reduce_scatter | solution.py:382
  (447 shorter events, 441.0 us)
Async XLA Ops:
  7.2 62.8 %all-gather.8.cloned.1.call-start = ((), (), s32[]{:S(2)}) async-start(), calls=%async_computation.7 | async-start | bytes 3538944 | tf_op jit(solution)/shard_map/all_gather | solution.py:114
  7.9 78.5 %all-gather.10.cloned.1.call-start = ((), (), s32[]{:S(2)}) async-start(), calls=%async_computation.8 | async-start | bytes 1880064 | tf_op jit(solution)/shard_map/all_gather | solution.py:109
  8.7 236.8 %reduce-scatter.8.cloned.1.call-start = ((), (), s32[]{:S(2)}) async-start(), calls=%async_computation.9 | async-start | bytes 3538944 | tf_op jit(solution)/shard_map/reduce_scatter | solution.py:205
  18.0 197.6 %copy-start.49 = (pred[1536]{0:T(1024)(128)(4,1)}, pred[1536]{0:T(1024)(128)(4,1)S(1)}, u32[]{:S(2)}) copy-start(pred[1536]{0:T(1024)(128)(4,1)S(1)} %fusion.88) | copy-start | bytes 4612
  93.2 125.7 %copy-start.5 = (bf16[1536,1,384]{0,2,1:T(8,128)(2,1)}, bf16[1536,1,384]{0,2,1:T(8,128)(2,1)S(1)}, u32[]{:S(2)}) copy-start(bf16[1536,1,384]{0,2,1:T(8,128)(2,1)S(1)} %get-tuple-element.394) | copy-start | bytes 3538948
  236.2 9.3 copy-start.4
  236.2 9.3 copy-start.46
  236.3 75.8 %all-gather.14.cloned.1.call-start = ((), (), s32[]{:S(2)}) async-start(), calls=%async_computation.11 | async-start | bytes 2506752 | tf_op jit(solution)/shard_map/all_gather | solution.py:111
  236.8 11.2 copy-start.53
  236.8 87.0 %all-gather.12.cloned.1.call-start = ((), (), s32[]{:S(2)}) async-start(), calls=%async_computation.10 | async-start | bytes 3538944 | tf_op jit(solution)/shard_map/all_gather | solution.py:216
  250.4 140.0 %all-gather.16.cloned.1.call-start = ((), (), s32[]{:S(2)}) async-start(), calls=%async_computation.12 | async-start | bytes 2506752 | tf_op jit(solution)/shard_map/all_gather | solution.py:112
  251.0 158.9 %reduce-scatter.10.cloned.1.call-start = ((), (), s32[]{:S(2)}) async-start(), calls=%async_computation.13 | async-start | bytes 3538944 | tf_op jit(solution)/shard_map/reduce_scatter | solution.py:222
  400.9 30.1 %all-gather.18.cloned.1.call-start = ((), (), s32[]{:S(2)}) async-start(), calls=%async_computation.14 | async-start | bytes 3538944 | tf_op jit(solution)/shard_map/all_gather | solution.py:241
  418.7 43.6 %reduce-scatter.12.cloned.1.call-start = ((), (), s32[]{:S(2)}) async-start(), calls=%async_computation.15 | async-start | bytes 3538944 | tf_op jit(solution)/shard_map/reduce_scatter | solution.py:256
  431.0 14.9 copy-start.76
  451.1 32.2 %all-gather.20.cloned.1.call-start = ((), (), s32[]{:S(2)}) async-start(), calls=%async_computation.16 | async-start | bytes 3538944 | tf_op jit(solution)/shard_map/all_gather | solution.py:270
  469.8 13.5 copy-start.43
  471.0 829.2 %all-reduce.4.cloned.1.call-start = ((), (), s32[]{:S(2)}) async-start(), calls=%async_computation.21 | async-start | bytes 9437184
  516.5 8.1 copy-start
  696.0 8.1 copy-start
  874.8 8.1 copy-start
  1052.9 11.6 slice-start
  1064.6 7.5 slice-start.4
  1073.5 7.7 slice-start.6
  1109.3 201.9 %reduce-scatter.14.cloned.1.call-start = ((), (), s32[]{:S(2)}) async-start(), calls=%async_computation.17 | async-start | bytes 3538944 | tf_op jit(solution)/shard_map/reduce_scatter | solution.py:370
  1116.6 339.5 %reduce-scatter.18.cloned.1.call-start = ((), (), s32[]{:S(2)}) async-start(), calls=%async_computation.19 | async-start | bytes 5013504 | tf_op jit(solution)/shard_map/reduce_scatter | solution.py:383
  1126.1 471.9 %reduce-scatter.20.cloned.1.call-start = ((), (), s32[]{:S(2)}) async-start(), calls=%async_computation.20 | async-start | bytes 5013504 | tf_op jit(solution)/shard_map/reduce_scatter | solution.py:384
  1137.0 7.3 copy-start.60
  1137.1 7.3 copy-start.61
  1137.1 7.3 copy-start.62
  1137.1 589.4 %reduce-scatter.16.cloned.1.call-start = ((), (), s32[]{:S(2)}) async-start(), calls=%async_computation.18 | async-start | bytes 1253376 | tf_op jit(solution)/shard_map/reduce_scatter | solution.py:382
  1142.4 168.8 %copy-start.10 = (f32[768,768]{1,0:T(8,128)S(1)}, f32[768,768]{1,0:T(8,128)}, u32[]{:S(2)}) copy-start(f32[768,768]{1,0:T(8,128)} %copy-done.9) | copy-start | bytes 7077892
  (78 other events, 230.1 us)
Sparse Core Ops, SparseCore 0:
  9.6 13.6 all-gather.7
  26.0 60.3 all-gather.9
  236.4 9.0 reduce-scatter.7
  248.5 63.4 all-gather.13
  314.0 9.7 all-gather.11
  326.9 63.4 all-gather.15
  401.0 8.7 reduce-scatter.9
  418.9 12.0 all-gather.17
  451.2 11.0 reduce-scatter.11
  471.1 12.1 all-gather.19
  1109.4 190.6 all-reduce.3
  1302.2 8.9 reduce-scatter.13
  1317.8 138.2 reduce-scatter.17
  1461.6 136.3 reduce-scatter.19
  1603.9 122.5 reduce-scatter.15
where the time goes:
time: 1750 us; the launch traced here: 1730 us
  waiting for transfers between devices  718 us (41%)
  other arithmetic  434 us (25%)
  local copies, waits for them, and re-layouts  232 us (13%)
  matrix products  225 us (13%)
  blocking collectives  102 us (6%)
  between operations  20 us (1%)
    scatter-add x3, other arithmetic, sparse_backward(): value_acc = value_acc.at[heads, chosen].add(grad_values.reshape(shape))  187 us
    scatter-add x3, other arithmetic, sparse_backward(): key_acc = key_acc.at[heads, chosen].add(grad_keys.reshape(shape))  186 us
    reduce_scatter x1, waiting for transfers between devices, on_device(): lax.psum_scatter(up_local, 'dp', scatter_dimension=0, tiled=True)  142 us
    reduce_scatter x1, waiting for transfers between devices, on_device(): lax.psum_scatter(down_local, 'dp', scatter_dimension=0, tiled=True)  142 us
    reduce_scatter x1, waiting for transfers between devices, on_device(): lax.psum_scatter(out_local, 'dp', scatter_dimension=0, tiled=True)  129 us
    unnamed x16, waiting for transfers between devices  105 us
    gather x12, local copies, waits for them, and re-layouts, pick_blocks(): picked = source[heads, chosen]  71.2 us
    all_gather x1, waiting for transfers between devices, on_device(): lax.all_gather(up_weight, 'dp', axis=0, tiled=True)  61 us
  transfers between devices with their start and end apart: 15, of which 14 were waited for; matrix products, arithmetic and copies ran while one was open for 4% of the time, Pallas kernels for 0%

commit v1 on v0

v1 whole, which is shorter than its diff:
```python
import functools

import jax
import jax.numpy as jnp
from jax import lax
from jax.experimental import pallas as pl
from jax.experimental.pallas import tpu as pltpu
from jax.sharding import PartitionSpec as P

BLK = 64


norm_eps = 1e-06
negative = -1e30


def norm_forward(values, gain, shift):
    centered = values - jnp.mean(values, axis=-1, keepdims=True)
    inverse = lax.rsqrt(jnp.mean(centered * centered, axis=-1, keepdims=True) + norm_eps)
    normed = centered * inverse
    return (normed * gain + shift, normed, inverse)


def norm_backward(grad, normed, inverse, gain):
    scaled = grad * gain
    mean_one = jnp.mean(scaled, axis=-1, keepdims=True)
    mean_two = jnp.mean(scaled * normed, axis=-1, keepdims=True)
    return inverse * (scaled - mean_one - normed * mean_two)


def dot_nt(a, b):
    return lax.dot_general(a, b, (((1,), (1,)), ((), ())), preferred_element_type=jnp.float32)
def dot_nn(a, b):
    return lax.dot_general(a, b, (((1,), (0,)), ((), ())), preferred_element_type=jnp.float32)
def dot_tn(a, b):
    return lax.dot_general(a, b, (((0,), (0,)), ((), ())), preferred_element_type=jnp.float32)

def block_scalars(len_ref, b, half_blocks):
    count0 = len_ref[0] // BLK
    count1 = len_ref[1] // BLK
    in0 = b < count0
    live = b < count0 + count1
    first = jnp.where(in0, 0, jnp.where(live, count0, b))
    items = jnp.where(in0, count0, jnp.where(live, count1, 1))
    rel = b - first
    last = items - 1
    is_global = live & ((rel == 0) | (rel == last))
    return live, first, rel, last, is_global

def slot_table(live, first, rel, last, b):
    lo = jnp.where(live, b - 1, b)
    hi = jnp.where(live, b + 1, b)
    zero = jnp.float32(0.0)
    neg = jnp.float32(negative)
    item_bias = jnp.where(live, zero, neg)
    lo_bias = jnp.where(live & (rel > 1), zero, neg)
    hi_bias = jnp.where(live & (rel + 1 < last), zero, neg)
    fixed = [first, first + last, b, lo, hi]
    bias = [item_bias, item_bias, zero, lo_bias, hi_bias, item_bias, item_bias, item_bias]
    return fixed, bias

def attn_fwd_kernel(pairs, rand, half_blocks, len_ref, rb_ref, tri_ref, out_ref):
    width = pairs * 128
    blocks = tri_ref.shape[0] // BLK
    scale = jnp.bfloat16(0.125)
    even = lax.broadcasted_iota(jnp.int32, (BLK, 128), 1) < BLK

    def rows(index, column):
        return tri_ref[pl.ds(pl.multiple_of(index * BLK, BLK), BLK), column:column + 128]

    def stacked(values):
        zero = jnp.zeros_like(values)
        return jnp.concatenate([jnp.where(even, values, zero), jnp.where(even, zero, values)], axis=0)

    def unstack(values):
        return jnp.where(even, values[:BLK], values[BLK:])

    def body(b, carry):
        live, first, rel, last, is_global = block_scalars(len_ref, b, half_blocks)
        here = pl.ds(pl.multiple_of(b * BLK, BLK), BLK)

        @pl.when(jnp.logical_not(is_global))
        def sparse():
            fixed, bias = slot_table(live, first, rel, last, b)
            lane = lax.broadcasted_iota(jnp.int32, (1, 128), 1) < BLK
            bias_row = jnp.concatenate(
                [jnp.where(lane, bias[2 * i], bias[2 * i + 1]) for i in range(4)], axis=1)
            for p in range(pairs):
                at = [[first * 0 + jnp.where(live, first + rb_ref[((2 * p + s) * blocks + b) * rand + k], b) for k in range(rand)] for s in range(2)]
                def unit(column):
                    return jnp.concatenate(
                        [rows(i, column) for i in fixed]
                        + [jnp.where(even, rows(at[0][k], column), rows(at[1][k], column)) for k in range(rand)], axis=0)
                query = stacked(rows(b, p * 128)) * scale
                scores = dot_nt(query, unit(width + p * 128)) + bias_row
                top = jnp.max(scores, axis=1, keepdims=True)
                expo = jnp.exp(scores - top)
                total = jnp.sum(expo, axis=1, keepdims=True)
                mixed = dot_nn(expo.astype(jnp.bfloat16), unit(2 * width + p * 128)) / total
                out_ref[here, p * 128:(p + 1) * 128] = unstack(mixed).astype(jnp.bfloat16)

        @pl.when(is_global)
        def dense():
            span = half_blocks * BLK
            queries = [stacked(rows(b, p * 128)) * scale for p in range(pairs)]
            def chunk(c, state):
                new = []
                at = pl.ds(pl.multiple_of((first + c * half_blocks) * BLK, BLK), span)
                for p in range(pairs):
                    top, total, acc = state[p]
                    scores = dot_nt(queries[p], tri_ref[at, width + p * 128:width + (p + 1) * 128])
                    higher = jnp.maximum(top, jnp.max(scores, axis=1, keepdims=True))
                    shrink = jnp.exp(top - higher)
                    expo = jnp.exp(scores - higher)
                    total = total * shrink + jnp.sum(expo, axis=1, keepdims=True)
                    acc = acc * shrink + dot_nn(expo.astype(jnp.bfloat16), tri_ref[at, 2 * width + p * 128:2 * width + (p + 1) * 128])
                    new.append((higher, total, acc))
                return tuple(new)
            init = tuple((jnp.full((128, 1), negative, jnp.float32), jnp.zeros((128, 1), jnp.float32), jnp.zeros((128, 128), jnp.float32)) for _ in range(pairs))
            state = lax.fori_loop(0, (last + 1) // half_blocks, chunk, init)
            for p in range(pairs):
                _, total, acc = state[p]
                out_ref[here, p * 128:(p + 1) * 128] = unstack(acc / total).astype(jnp.bfloat16)
        return carry

    lax.fori_loop(0, blocks, body, 0)

def attn_bwd_kernel(pairs, rand, half_blocks, len_ref, rb_ref, tri_ref, grad_ref, out_ref, sum_ref, *accs):
    width = pairs * 128
    blocks = tri_ref.shape[0] // BLK
    scale = jnp.bfloat16(0.125)
    even = lax.broadcasted_iota(jnp.int32, (BLK, 128), 1) < BLK
    key_acc, value_acc = accs[:pairs], accs[pairs:]
    for acc in accs:
        acc[...] = jnp.zeros_like(acc)

    def spot(index):
        return pl.ds(pl.multiple_of(index * BLK, BLK), BLK)

    def rows(index, column):
        return tri_ref[spot(index), column:column + 128]

    def stacked(values):
        zero = jnp.zeros_like(values)
        return jnp.concatenate([jnp.where(even, values, zero), jnp.where(even, zero, values)], axis=0)

    def unstack(values):
        return jnp.where(even, values[:BLK], values[BLK:])

    def body(b, carry):
        live, first, rel, last, is_global = block_scalars(len_ref, b, half_blocks)

        @pl.when(jnp.logical_not(is_global))
        def sparse():
            fixed, bias = slot_table(live, first, rel, last, b)
            for p in range(pairs):
                at = [[jnp.where(live, first + rb_ref[((2 * p + s) * blocks + b) * rand + k], b) for k in range(rand)] for s in range(2)]
                def unit(column):
                    return jnp.concatenate(
                        [rows(i, column) for i in fixed]
                        + [jnp.where(even, rows(at[0][k], column), rows(at[1][k], column)) for k in range(rand)], axis=0)
                query = stacked(rows(b, p * 128)) * scale
                grad = stacked(grad_ref[spot(b), p * 128:(p + 1) * 128])
                keys = unit(width + p * 128)
                values = unit(2 * width + p * 128)
                scores = dot_nt(keys, query)
                scores = jnp.concatenate([scores[i * BLK:(i + 1) * BLK] + bias[i] for i in range(5 + rand)], axis=0)
                top = jnp.max(scores, axis=0, keepdims=True)
                expo = jnp.exp(scores - top)
                probs = expo * (1.0 / jnp.sum(expo, axis=0, keepdims=True))
                grad_probs = dot_nt(values, grad)
                delta = jnp.sum(probs * grad_probs, axis=0, keepdims=True)
                grad_scores = (probs * (grad_probs - delta)).astype(jnp.bfloat16)
                grad_query = dot_tn(grad_scores, keys) * 0.125
                out_ref[spot(b), p * 128:(p + 1) * 128] = unstack(grad_query).astype(jnp.bfloat16)
                for acc, update in ((key_acc[p], dot_nn(grad_scores, query)), (value_acc[p], dot_nn(probs.astype(jnp.bfloat16), grad))):
                    for i in range(5):
                        acc[spot(fixed[i]), :] += update[i * BLK:(i + 1) * BLK]
                    for k in range(rand):
                        piece = update[(5 + k) * BLK:(6 + k) * BLK]
                        zero = jnp.zeros_like(piece)
                        acc[spot(at[0][k]), :] += jnp.where(even, piece, zero)
                        acc[spot(at[1][k]), :] += jnp.where(even, zero, piece)

        @pl.when(is_global)
        def dense():
            span = half_blocks * BLK
            chunks = (last + 1) // half_blocks
            def place(c):
                return pl.ds(pl.multiple_of((first + c * half_blocks) * BLK, BLK), span)
            queries = [stacked(rows(b, p * 128)) * scale for p in range(pairs)]
            grads = [stacked(grad_ref[spot(b), p * 128:(p + 1) * 128]) for p in range(pairs)]
            def first_pass(c, state):
                new = []
                at = place(c)
                for p in range(pairs):
                    top, total, dot = state[p]
                    scores = dot_nt(tri_ref[at, width + p * 128:width + (p + 1) * 128], queries[p])
                    grad_probs = dot_nt(tri_ref[at, 2 * width + p * 128:2 * width + (p + 1) * 128], grads[p])
                    higher = jnp.maximum(top, jnp.max(scores, axis=0, keepdims=True))
                    shrink = jnp.exp(top - higher)
                    expo = jnp.exp(scores - higher)
                    total = total * shrink + jnp.sum(expo, axis=0, keepdims=True)
                    dot = dot * shrink + jnp.sum(expo * grad_probs, axis=0, keepdims=True)
                    new.append((higher, total, dot))
                return tuple(new)
            init = tuple((jnp.full((1, 128), negative, jnp.float32), jnp.zeros((1, 128), jnp.float32), jnp.zeros((1, 128), jnp.float32)) for _ in range(pairs))
            state = lax.fori_loop(0, chunks, first_pass, init)
            def second_pass(c, grad_queries):
                new = []
                at = place(c)
                for p in range(pairs):
                    top, total, dot = state[p]
                    inverse = 1.0 / total
                    keys = tri_ref[at, width + p * 128:width + (p + 1) * 128]
                    scores = dot_nt(keys, queries[p])
                    grad_probs = dot_nt(tri_ref[at, 2 * width + p * 128:2 * width + (p + 1) * 128], grads[p])
                    probs = jnp.exp(scores - top) * inverse
                    grad_scores = (probs * (grad_probs - dot * inverse)).astype(jnp.bfloat16)
                    new.append(grad_queries[p] + dot_tn(grad_scores, keys))
                    key_acc[p][at, :] += dot_nn(grad_scores, queries[p])
                    value_acc[p][at, :] += dot_nn(probs.astype(jnp.bfloat16), grads[p])
                return tuple(new)
            grad_queries = lax.fori_loop(0, chunks, second_pass, tuple(jnp.zeros((128, 128), jnp.float32) for _ in range(pairs)))
            for p in range(pairs):
                out_ref[spot(b), p * 128:(p + 1) * 128] = unstack(grad_queries[p] * 0.125).astype(jnp.bfloat16)
        return carry

    lax.fori_loop(0, blocks, body, 0)
    sum_ref[...] = jnp.zeros_like(sum_ref)
    for p in range(pairs):
        column = slice(p * 128, (p + 1) * 128)
        sum_ref[0:1, column] = jnp.sum(out_ref[:, column].astype(jnp.float32), axis=0, keepdims=True)
        out_ref[:, width + p * 128:width + (p + 1) * 128] = key_acc[p][...].astype(jnp.bfloat16)
        value = value_acc[p][...].astype(jnp.bfloat16)
        out_ref[:, 2 * width + p * 128:2 * width + (p + 1) * 128] = value
        sum_ref[1:2, column] = jnp.sum(value.astype(jnp.float32), axis=0, keepdims=True)

def attention_forward(lengths, randoms, triple):
    heads, blocks, rand = randoms.shape
    pairs = heads // 2
    vm = pl.BlockSpec(memory_space=pltpu.VMEM); sm = pl.BlockSpec(memory_space=pltpu.SMEM)
    return pl.pallas_call(
        functools.partial(attn_fwd_kernel, pairs, rand, blocks // 2),
        out_shape=jax.ShapeDtypeStruct((triple.shape[0], pairs * 128), jnp.bfloat16),
        in_specs=[sm, sm, vm], out_specs=vm, name="attend_forward",
        compiler_params=pltpu.CompilerParams(vmem_limit_bytes=60 << 20),
    )(lengths, randoms.reshape(-1), triple)

def attention_backward(lengths, randoms, triple, grad):
    heads, blocks, rand = randoms.shape
    pairs = heads // 2
    vm = pl.BlockSpec(memory_space=pltpu.VMEM); sm = pl.BlockSpec(memory_space=pltpu.SMEM)
    return pl.pallas_call(
        functools.partial(attn_bwd_kernel, pairs, rand, blocks // 2),
        out_shape=(jax.ShapeDtypeStruct(triple.shape, jnp.bfloat16), jax.ShapeDtypeStruct((8, pairs * 128), jnp.float32)),
        in_specs=[sm, sm, vm, vm], out_specs=(vm, vm), name="attend_backward",
        scratch_shapes=[pltpu.VMEM((triple.shape[0], 128), jnp.float32)] * (2 * pairs),
        compiler_params=pltpu.CompilerParams(vmem_limit_bytes=60 << 20),
    )(lengths, randoms.reshape(-1), triple, grad)


def on_device(
    inputs,
    qkv_weight,
    qv_bias,
    out_weight,
    out_bias,
    first_gain,
    first_shift,
    up_weight,
    up_bias,
    down_weight,
    down_bias,
    second_gain,
    second_shift,
    item_lengths,
    random_blocks,
    out_grad,
):
    half = inputs.shape[0]
    width = inputs.shape[1]
    position = lax.axis_index("head")
    head_width = qkv_weight.shape[2]
    full_qkv, full_out, full_up, full_down = (
        lax.all_gather(qkv_weight, "dp", axis=0, tiled=True),
        lax.all_gather(out_weight, "dp", axis=0, tiled=True),
        lax.all_gather(up_weight, "dp", axis=0, tiled=True),
        lax.all_gather(down_weight, "dp", axis=0, tiled=True),
    )
    tokens = lax.all_gather(inputs, "head", axis=0, tiled=True)
    capacity = tokens.shape[0]
    block_count = capacity // BLK
    counts = item_lengths[0] // BLK
    live = (jnp.arange(block_count, dtype=jnp.int32) < jnp.sum(counts)).astype(jnp.int32)
    bias = jnp.stack([qv_bias[0], jnp.zeros_like(qv_bias[0]), qv_bias[1]])
    triple = (
        jnp.einsum("td,dcf->tcf", tokens, full_qkv, preferred_element_type=jnp.float32) + bias
    ).astype(jnp.bfloat16)
    attended = attention_forward(item_lengths[0], random_blocks[0], triple.reshape(capacity, 3 * head_width))
    part = attended
    proj = lax.psum_scatter(
        jnp.einsum("tf,df->td", part, full_out, preferred_element_type=jnp.float32).astype(
            jnp.bfloat16
        ),
        "head",
        scatter_dimension=0,
        tiled=True,
    ).astype(jnp.float32)
    normed_one_out, normed_one, inverse_one = norm_forward(
        proj + out_bias + inputs.astype(jnp.float32), first_gain, first_shift
    )
    hidden = lax.all_gather(normed_one_out.astype(jnp.bfloat16), "head", axis=0, tiled=True)
    upper = (
        jnp.einsum("td,df->tf", hidden, full_up, preferred_element_type=jnp.float32) + up_bias
    ).astype(jnp.bfloat16)
    active = jax.nn.gelu(upper.astype(jnp.float32), approximate=True).astype(jnp.bfloat16)
    part = active
    down = lax.psum_scatter(
        jnp.einsum("tf,df->td", part, full_down, preferred_element_type=jnp.float32).astype(
            jnp.bfloat16
        ),
        "head",
        scatter_dimension=0,
        tiled=True,
    ).astype(jnp.float32)
    normed_two_out, normed_two, inverse_two = norm_forward(
        down + down_bias + normed_one_out, second_gain, second_shift
    )
    live_rows = jnp.repeat(live, BLK).astype(jnp.float32)
    live_half = lax.dynamic_slice_in_dim(live_rows, position * half, half, 0)
    layer_out = (normed_two_out * live_half[:, None]).astype(jnp.bfloat16)
    cotangent = out_grad.astype(jnp.float32) * live_half[:, None]
    second_gain_part = jnp.sum(cotangent * normed_two, axis=0)
    second_shift_part = jnp.sum(cotangent, axis=0)
    grad_res_two = norm_backward(cotangent, normed_two, inverse_two, second_gain)
    down_bias_part = jnp.sum(grad_res_two, axis=0)
    grad_down_rows = lax.all_gather(grad_res_two.astype(jnp.bfloat16), "head", axis=0, tiled=True)
    grad_active = jnp.einsum(
        "td,df->tf", grad_down_rows, full_down, preferred_element_type=jnp.float32
    )
    down_local = jnp.einsum("td,tf->df", grad_down_rows, active, preferred_element_type=jnp.float32)

    def gelu_tanh(values):
        return jax.nn.gelu(values, approximate=True)

    gelu_pull = jax.vjp(gelu_tanh, upper.astype(jnp.float32))[1]
    grad_upper = gelu_pull(grad_active)[0].astype(jnp.bfloat16)
    up_bias_part = jnp.sum(grad_upper.astype(jnp.float32), axis=0)
    up_local = jnp.einsum("td,tf->df", hidden, grad_upper, preferred_element_type=jnp.float32)
    part = grad_upper
    grad_norm_one = (
        lax.psum_scatter(
            jnp.einsum("tf,df->td", part, full_up, preferred_element_type=jnp.float32).astype(
                jnp.bfloat16
            ),
            "head",
            scatter_dimension=0,
            tiled=True,
        ).astype(jnp.float32)
        + grad_res_two
    )
    first_gain_part = jnp.sum(grad_norm_one * normed_one, axis=0)
    first_shift_part = jnp.sum(grad_norm_one, axis=0)
    grad_res_one = norm_backward(grad_norm_one, normed_one, inverse_one, first_gain)
    out_bias_part = jnp.sum(grad_res_one, axis=0)
    grad_proj = lax.all_gather(grad_res_one.astype(jnp.bfloat16), "head", axis=0, tiled=True)
    grad_attended = jnp.einsum(
        "td,df->tf", grad_proj, full_out, preferred_element_type=jnp.float32
    ).astype(jnp.bfloat16)
    out_local = jnp.einsum("td,tf->df", grad_proj, attended, preferred_element_type=jnp.float32)
    grad_flat, bias_sums = attention_backward(
        item_lengths[0], random_blocks[0], triple.reshape(capacity, 3 * head_width), grad_attended
    )
    grad_triple = grad_flat.reshape(capacity, 3, head_width)
    qv_bias_part = bias_sums[:2]
    qkv_local = jnp.einsum("td,tcf->dcf", tokens, grad_triple, preferred_element_type=jnp.float32)
    part = grad_triple
    input_grad = (
        lax.psum_scatter(
            jnp.einsum("tcf,dcf->td", part, full_qkv, preferred_element_type=jnp.float32).astype(
                jnp.bfloat16
            ),
            "head",
            scatter_dimension=0,
            tiled=True,
        ).astype(jnp.float32)
        + grad_res_one
    ).astype(jnp.bfloat16)
    grad_qkv, grad_out, grad_up, grad_down = (
        lax.psum_scatter(qkv_local, "dp", scatter_dimension=0, tiled=True),
        lax.psum_scatter(out_local, "dp", scatter_dimension=0, tiled=True),
        lax.psum_scatter(up_local, "dp", scatter_dimension=0, tiled=True),
        lax.psum_scatter(down_local, "dp", scatter_dimension=0, tiled=True),
    )
    up_width = up_bias.shape[0]
    qv_full = lax.dynamic_update_slice_in_dim(
        jnp.zeros((2, width), jnp.float32), qv_bias_part, position * head_width, 1
    )
    up_full = lax.dynamic_update_slice_in_dim(
        jnp.zeros((up_width * lax.axis_size("head"),), jnp.float32),
        up_bias_part,
        position * up_width,
        0,
    )
    totals = lax.psum(
        (
            qv_full,
            up_full,
            out_bias_part,
            first_gain_part,
            first_shift_part,
            down_bias_part,
            second_gain_part,
            second_shift_part,
        ),
        ("dp", "head"),
    )
    grad_qv_bias = lax.dynamic_slice_in_dim(totals[0], position * head_width, head_width, 1)
    grad_up_bias = lax.dynamic_slice_in_dim(totals[1], position * up_width, up_width, 0)
    return (
        layer_out,
        input_grad,
        grad_qkv,
        grad_qv_bias,
        grad_out,
        totals[2],
        totals[3],
        totals[4],
        grad_up,
        grad_up_bias,
        grad_down,
        totals[5],
        totals[6],
        totals[7],
    )


def solution(mesh):
    in_specs = (
        P(("dp", "head"), None),
        P("dp", None, "head"),
        P(None, "head"),
        P("dp", "head"),
        P(),
        P(),
        P(),
        P("dp", "head"),
        P("head"),
        P("dp", "head"),
        P(),
        P(),
        P(),
        P("dp", None),
        P("dp", "head", None, None),
        P(("dp", "head"), None),
    )
    out_specs = (
        P(("dp", "head"), None),
        P(("dp", "head"), None),
        P("dp", None, "head"),
        P(None, "head"),
        P("dp", "head"),
        P(),
        P(),
        P(),
        P("dp", "head"),
        P("head"),
        P("dp", "head"),
        P(),
        P(),
        P(),
    )
    return jax.shard_map(
        on_device, mesh=mesh, in_specs=in_specs, out_specs=out_specs, check_vma=False
    )
```

time: 1750 us -> 1070 us (0.61)
  other arithmetic: 434 us -> 22.1 us
  local copies, waits for them, and re-layouts: 232 us -> 30 us
  matrix products: 225 us -> 83.9 us
  Pallas kernels: 0 us -> 76.5 us
    scatter-add x6 -> x0, other arithmetic: 373 us -> none  [the longest x3 187 us: sparse_backward(): value_acc = value_acc.at[heads, chosen].add(grad_values.reshape(shape))]
    dot_general x30 -> x0, matrix products: 124 us -> none  [the longest x6 33.3 us: sparse_scores(): jnp.einsum('hqbe,hqke->hqbk', query_blk, near_keys, preferred_element_typ...]
    pallas_call x0 -> x2, Pallas kernels: none -> 76.5 us  [the longest x1 49.6 us: attention_backward(): pl.pallas_call(functools.partial(attn_bwd_kernel, pairs, rand, blocks //...]
    gather x12 -> x0, local copies, waits for them, and re-layouts: 71.2 us -> none  [pick_blocks(): picked = source[heads, chosen]]
    reshape x5 -> x1, local copies, waits for them, and re-layouts: 39.9 us -> 3.88 us  [on_device(): triple.reshape(capacity, 3 * head_width)]
    another operation x20 -> x1, local copies, waits for them, and re-layouts: 34 us -> 0.78 us  [attention_forward(): randoms.reshape(-1)]
    reshape x3 -> x0, matrix products: 20 us -> none  [sparse_backward(): value_acc = value_acc.at[heads, chosen].add(grad_values.reshape(shape))]
  transfers between devices with their start and end apart: 15 -> 15, of which waited for: 14 -> 14; matrix products, arithmetic and copies ran while one was open for 4% -> 5% of each run, Pallas kernels for 0% -> 0%
where the time goes in v1:
time: 1070 us; the launch traced here: 1060 us
  waiting for transfers between devices  735 us (69%)
  blocking collectives  93.6 us (9%)
  matrix products  83.9 us (8%)
  Pallas kernels  76.5 us (7%)
  local copies, waits for them, and re-layouts  30 us (3%)
  other arithmetic  22.1 us (2%)
  between operations  15.1 us (1%)
    reduce_scatter x1, waiting for transfers between devices, on_device(): lax.psum_scatter(up_local, 'dp', scatter_dimension=0, tiled=True)  143 us
    reduce_scatter x1, waiting for transfers between devices, on_device(): lax.psum_scatter(down_local, 'dp', scatter_dimension=0, tiled=True)  142 us
    reduce_scatter x1, waiting for transfers between devices, on_device(): lax.psum_scatter(out_local, 'dp', scatter_dimension=0, tiled=True)  128 us
    unnamed x16, waiting for transfers between devices  105 us
    all_gather x1, waiting for transfers between devices, on_device(): lax.all_gather(up_weight, 'dp', axis=0, tiled=True)  61.4 us
    all_gather x1, waiting for transfers between devices, on_device(): lax.all_gather(down_weight, 'dp', axis=0, tiled=True)  58.2 us
    pallas_call x1, Pallas kernels, attention_backward(): pl.pallas_call(functools.partial(attn_bwd_kernel, pairs, rand, blocks //...  49.6 us
    all_gather x1, blocking collectives, on_device(): lax.all_gather(out_weight, 'dp', axis=0, tiled=True)  49.1 us
  transfers between devices with their start and end apart: 15, of which 14 were waited for; matrix products, arithmetic and copies ran while one was open for 5% of the time, Pallas kernels for 0%

profile of v1, /device:TPU:0, one launch (start us, length us, event | category | flops | bytes accessed | tf_op | source)
XLA Modules:
  0.0 1057.6 jit_solution(2206850593643254514)
XLA Ops:
  11.2 49.1 %all_gather.26 = bf16[768,384]{1,0:T(8,128)(2,1)} all-gather(bf16[48,384]{1,0:T(8,128)(2,1)} %param.19), channel_id=1, replica_groups=mesh['dp'=16,'head'=2] {'dp'}, dimensions={0}, use_global_device_ids=true | all-gather | bytes 626688 | tf_op jit(solution)/shard_map/all_gather | solution.py:287
  60.3 25.8 %all-gather.10.cloned.1.call-done = bf16[768,3,384]{2,0,1:T(8,128)(2,1)} async-done(((bf16[48,3,384]{2,0,1:T(8,128)(2,1)}), bf16[768,3,384]{2,0,1:T(8,128)(2,1)}) %all-gather.10.cloned.1.call-update) | async-done | bytes 1769488 | tf_op jit(solution)/shard_map/all_gather | solution.py:286
  86.2 5.1 add_convert_fusion.1
  95.2 26.8 %attend_forward.1 = bf16[1536,384]{1,0:T(8,128)(2,1)} custom-call(s32[2]{0:T(128)} %bitcast.42, s32[432]{0:T(512)} %reshape_squeeze.4.rb_ref, bf16[1536,1152]{1,0:T(8,128)(2,1)} %copy.41.tri_ref), custom_call_target="tpu_custom_call" | custom-call | tf_op jit(solution)/shard_map/attend_forward/pallas_call | solution.py:243
  122.0 4.1 convolution_convert_fusion.2
  126.8 8.9 reduce-scatter.8.cloned.1.call-done
  140.8 61.4 %all-gather.14.cloned.1.call-done = bf16[768,1536]{1,0:T(8,128)(2,1)} async-done(((bf16[48,1536]{1,0:T(8,128)(2,1)}), bf16[768,1536]{1,0:T(8,128)(2,1)}) %all-gather.14.cloned.1.call-update) | async-done | bytes 2359312 | tf_op jit(solution)/shard_map/all_gather | solution.py:288
  202.2 11.8 %all-gather.12.cloned.1.call-done = bf16[1536,768]{1,0:T(8,128)(2,1)} async-done(((bf16[768,768]{1,0:T(8,128)(2,1)}), bf16[1536,768]{1,0:T(8,128)(2,1)}) %all-gather.12.cloned.1.call-update) | async-done | bytes 2359312 | tf_op jit(solution)/shard_map/all_gather | solution.py:313
  214.0 8.3 add_convert_fusion
  222.4 58.2 %all-gather.16.cloned.1.call-done = bf16[768,1536]{1,0:T(8,128)(2,1)} async-done(((bf16[48,1536]{1,0:T(8,128)(2,1)}), bf16[768,1536]{1,0:T(8,128)(2,1)}) %all-gather.16.cloned.1.call-update) | async-done | bytes 2359312 | tf_op jit(solution)/shard_map/all_gather | solution.py:289
  280.6 10.5 convolution_convert_fusion.1
  293.2 6.7 reduce-scatter.10.cloned.1.call-done
  308.5 11.7 %all-gather.18.cloned.1.call-done = bf16[1536,768]{1,0:T(8,128)(2,1)} async-done(((bf16[768,768]{1,0:T(8,128)(2,1)}), bf16[1536,768]{1,0:T(8,128)(2,1)}) %all-gather.18.cloned.1.call-update) | async-done | bytes 2359312 | tf_op jit(solution)/shard_map/all_gather | solution.py:338
  320.2 12.7 %convert_reduce_fusion = (f32[1536]{0:T(1024)}, bf16[1536,1536]{1,0:T(8,128)(2,1)S(1)}) fusion(bf16[1536,1536]{1,0:T(8,128)(2,1)} %add_convert_fusion, bf16[1536,768]{1,0:T(8,128)(2,1)} %all-gather.18.cloned.1.call-done, bf16[768,1536]{1,0:T(8,128)(2,1)} %all-gather.16.cloned.1.call-done), kind=kOutput, calls=%fused_computation.15 | convolution fusion | flops 3678140928 | bytes 14161920 | tf_op jit(solution)/shard_map/td,df->tf/dot_general | solution.py:339
  335.1 5.1 convolution_convert_fusion
  340.2 11.2 %reduce-scatter.12.cloned.1.call-done = bf16[768,768]{1,0:T(8,128)(2,1)} async-done(((bf16[1536,768]{1,0:T(8,128)(2,1)}), bf16[768,768]{1,0:T(8,128)(2,1)}) %reduce-scatter.12.cloned.1.call-update) | async-done | bytes 1179664 | tf_op jit(solution)/shard_map/reduce_scatter | solution.py:353
  360.1 12.1 %all-gather.20.cloned.1.call-done = bf16[1536,768]{1,0:T(8,128)(2,1)} async-done(((bf16[768,768]{1,0:T(8,128)(2,1)}), bf16[1536,768]{1,0:T(8,128)(2,1)}) %all-gather.20.cloned.1.call-update) | async-done | bytes 2359312 | tf_op jit(solution)/shard_map/all_gather | solution.py:367
  372.1 4.1 convolution_convert_fusion.3.grad_ref
  376.2 49.6 %attend_backward.1 = (bf16[1536,1152]{1,0:T(8,128)(2,1)}, f32[8,384]{1,0:T(8,128)}) custom-call(s32[2]{0:T(128)} %bitcast.43, s32[432]{0:T(512)} %reshape_squeeze.4.rb_ref, bf16[1536,1152]{1,0:T(8,128)(2,1)} %copy.41.tri_ref, bf16[1536,384]{1,0:T(8,128)(2,1)} %convolution_convert_fusion.3.grad_ref), custom_call_target="tpu_custom_call" | custom-call | tf_op jit(solution)/shard_map/attend_backward/pallas_call | solution.py:254
  425.8 4.4 copy.43
  430.2 6.3 fusion.17
  436.5 6.2 copy.45
  442.8 6.1 bitcast_convert_fusion
  450.3 5.0 fusion.31
  455.3 7.9 fusion.32
  464.9 8.7 fusion.23
  476.5 44.5 %all-reduce.1 = (f32[2,768]{1,0:T(2,128)S(1)}, f32[768]{0:T(1024)}, f32[768]{0:T(1024)}, f32[768]{0:T(1024)}, f32[3072]{0:T(1024)S(1)}, /*index=5*/f32[768]{0:T(1024)}, f32[768]{0:T(1024)}, f32[768]{0:T(1024)}) all-reduce(f32[2,768]{1,0:T(2,128)S(1)} %slice_dynamic-update-slice_fusion, ...), channel_id=1, replica_groups=mesh['dp'=16,'head'=2] {'dp','head'}, use_global_device_ids=true, to_apply=%region_14.15 | all-reduce | flops 9216 | bytes 73728 | tf_op jit(solution)/shard_map/psum | solution.py:406
  522.3 102.1 %all-reduce.4.cloned.1.call-done = f32[768,3,384]{2,1,0:T(4,128)} async-done(((f32[768,3,384]{2,1,0:T(4,128)}), f32[768,3,384]{2,1,0:T(4,128)}) %all-reduce.4.cloned.1.call-update) | async-done | bytes 3538960
  626.2 9.3 reduce-scatter.14.cloned.1.call-done
  638.0 128.3 %reduce-scatter.16.cloned.1.call-done = f32[48,384]{1,0:T(8,128)} async-done(((f32[768,384]{1,0:T(8,128)}), f32[48,384]{1,0:T(8,128)}) %reduce-scatter.16.cloned.1.call-update) | async-done | bytes 73744 | tf_op jit(solution)/shard_map/reduce_scatter | solution.py:392
  766.3 142.6 %reduce-scatter.18.cloned.1.call-done = f32[48,1536]{1,0:T(8,128)} async-done(((f32[768,1536]{1,0:T(8,128)}), f32[48,1536]{1,0:T(8,128)}) %reduce-scatter.18.cloned.1.call-update) | async-done | bytes 294928 | tf_op jit(solution)/shard_map/reduce_scatter | solution.py:393
  908.9 142.0 %reduce-scatter.20.cloned.1.call-done = f32[48,1536]{1,0:T(8,128)} async-done(((f32[768,1536]{1,0:T(8,128)}), f32[48,1536]{1,0:T(8,128)}) %reduce-scatter.20.cloned.1.call-update) | async-done | bytes 294928 | tf_op jit(solution)/shard_map/reduce_scatter | solution.py:394
  (119 shorter events, 45.9 us)
Async XLA Ops:
  7.2 53.2 %all-gather.8.cloned.1.call-start = ((), (), s32[]{:S(2)}) async-start(), calls=%async_computation.7 | async-start | bytes 3538944 | tf_op jit(solution)/shard_map/all_gather | solution.py:291
  7.9 78.3 %all-gather.10.cloned.1.call-start = ((), (), s32[]{:S(2)}) async-start(), calls=%async_computation.8 | async-start | bytes 1880064 | tf_op jit(solution)/shard_map/all_gather | solution.py:286
  8.7 127.0 %reduce-scatter.8.cloned.1.call-start = ((), (), s32[]{:S(2)}) async-start(), calls=%async_computation.9 | async-start | bytes 3538944 | tf_op jit(solution)/shard_map/reduce_scatter | solution.py:302
  95.2 26.8 %copy-start.8 = (bf16[768,384]{1,0:T(8,128)(2,1)S(1)}, bf16[768,384]{1,0:T(8,128)(2,1)}, u32[]{:S(2)}) copy-start(bf16[768,384]{1,0:T(8,128)(2,1)} %all_gather.26) | copy-start | bytes 1769476
  126.1 9.5 copy-start
  126.1 9.5 copy-start.9
  126.1 76.0 %all-gather.14.cloned.1.call-start = ((), (), s32[]{:S(2)}) async-start(), calls=%async_computation.11 | async-start | bytes 2506752 | tf_op jit(solution)/shard_map/all_gather | solution.py:288
  126.7 11.4 %copy-start.10 = (f32[768]{0:T(1024)S(1)}, f32[768]{0:T(1024)}, u32[]{:S(2)}) copy-start(f32[768]{0:T(1024)} %param.21) | copy-start | bytes 9220
  126.7 11.4 %copy-start.14 = (f32[768]{0:T(1024)S(1)}, f32[768]{0:T(1024)}, u32[]{:S(2)}) copy-start(f32[768]{0:T(1024)} %param.22) | copy-start | bytes 9220
  126.7 87.3 %all-gather.12.cloned.1.call-start = ((), (), s32[]{:S(2)}) async-start(), calls=%async_computation.10 | async-start | bytes 3538944 | tf_op jit(solution)/shard_map/all_gather | solution.py:313
  138.2 75.9 %copy-start.22 = (f32[1536]{0:T(1024)S(1)}, f32[1536]{0:T(1024)}, u32[]{:S(2)}) copy-start(f32[1536]{0:T(1024)} %param.24) | copy-start | bytes 18436
  139.9 140.7 %all-gather.16.cloned.1.call-start = ((), (), s32[]{:S(2)}) async-start(), calls=%async_computation.12 | async-start | bytes 2506752 | tf_op jit(solution)/shard_map/all_gather | solution.py:289
  140.5 159.5 %reduce-scatter.10.cloned.1.call-start = ((), (), s32[]{:S(2)}) async-start(), calls=%async_computation.13 | async-start | bytes 3538944 | tf_op jit(solution)/shard_map/reduce_scatter | solution.py:319
  291.0 8.9 copy-start.16
  291.1 29.1 %all-gather.18.cloned.1.call-start = ((), (), s32[]{:S(2)}) async-start(), calls=%async_computation.14 | async-start | bytes 3538944 | tf_op jit(solution)/shard_map/all_gather | solution.py:338
  302.8 2.3 copy-start.17
  307.9 43.5 %reduce-scatter.12.cloned.1.call-start = ((), (), s32[]{:S(2)}) async-start(), calls=%async_computation.15 | async-start | bytes 3538944 | tf_op jit(solution)/shard_map/reduce_scatter | solution.py:353
  320.2 14.9 %copy-start.20 = (bf16[768,1536]{1,0:T(8,128)(2,1)S(1)}, bf16[768,1536]{1,0:T(8,128)(2,1)}, u32[]{:S(2)}) copy-start(bf16[768,1536]{1,0:T(8,128)(2,1)} %all-gather.14.cloned.1.call-done) | copy-start | bytes 7077892
  332.9 2.2 copy-start.24
  340.2 31.9 %all-gather.20.cloned.1.call-start = ((), (), s32[]{:S(2)}) async-start(), calls=%async_computation.16 | async-start | bytes 3538944 | tf_op jit(solution)/shard_map/all_gather | solution.py:367
  351.4 3.9 copy-start.4
  351.4 3.9 copy-start.6
  359.8 264.6 %all-reduce.4.cloned.1.call-start = ((), (), s32[]{:S(2)}) async-start(), calls=%async_computation.21 | async-start | bytes 9437184
  442.8 192.7 %reduce-scatter.14.cloned.1.call-start = ((), (), s32[]{:S(2)}) async-start(), calls=%async_computation.17 | async-start | bytes 3538944 | tf_op jit(solution)/shard_map/reduce_scatter | solution.py:380
  448.9 6.4 copy-start.19
  448.9 317.4 %reduce-scatter.16.cloned.1.call-start = ((), (), s32[]{:S(2)}) async-start(), calls=%async_computation.18 | async-start | bytes 1253376 | tf_op jit(solution)/shard_map/reduce_scatter | solution.py:392
  455.3 453.6 %reduce-scatter.18.cloned.1.call-start = ((), (), s32[]{:S(2)}) async-start(), calls=%async_computation.19 | async-start | bytes 5013504 | tf_op jit(solution)/shard_map/reduce_scatter | solution.py:393
  463.3 587.6 %reduce-scatter.20.cloned.1.call-start = ((), (), s32[]{:S(2)}) async-start(), calls=%async_computation.20 | async-start | bytes 5013504 | tf_op jit(solution)/shard_map/reduce_scatter | solution.py:394
  473.6 1.9 copy-start.15
  473.6 3.0 copy-start.12
  473.6 3.0 copy-start.13
  473.6 161.9 %copy-start.3 = (f32[768,768]{1,0:T(8,128)S(1)}, f32[768,768]{1,0:T(8,128)}, u32[]{:S(2)}) copy-start(f32[768,768]{1,0:T(8,128)} %copy-done.2) | copy-start | bytes 7077892
  (8 other events, 10.1 us)
Sparse Core Ops, SparseCore 0:
  9.6 13.6 all-gather.7
  25.9 60.1 all-gather.9
  126.3 9.3 reduce-scatter.7
  138.7 63.4 all-gather.13
  204.2 9.7 all-gather.11
  217.1 63.4 all-gather.15
  291.2 8.7 reduce-scatter.9
  308.0 12.0 all-gather.17
  340.3 11.0 reduce-scatter.11
  360.0 12.1 all-gather.19
  442.9 181.5 all-reduce.3
  626.5 8.9 reduce-scatter.13
  641.6 124.7 reduce-scatter.15
  772.7 136.1 reduce-scatter.17
  914.5 136.3 reduce-scatter.19

commit v2 on v1

--- a/solution.py
+++ b/solution.py
@@ -2,9 +2,11 @@
 
 import jax
 import jax.numpy as jnp
+import numpy as np
 from jax import lax
 from jax.experimental import pallas as pl
 from jax.experimental.pallas import tpu as pltpu
+from jax.sharding import Mesh
 from jax.sharding import PartitionSpec as P
 
 BLK = 64
@@ -65,8 +67,20 @@
     scale = jnp.bfloat16(0.125)
     even = lax.broadcasted_iota(jnp.int32, (BLK, 128), 1) < BLK
 
+    shift = len_ref[2]
+
+    def spot(index):
+        moved = index + shift
+        moved = jnp.where(moved >= blocks, moved - blocks, moved)
+        return pl.ds(pl.multiple_of(moved * BLK, BLK), BLK)
+
+    def span_of(index, count):
+        moved = index + shift
+        moved = jnp.where(moved >= blocks, moved - blocks, moved)
+        return pl.ds(pl.multiple_of(moved * BLK, BLK), count * BLK)
+
     def rows(index, column):
-        return tri_ref[pl.ds(pl.multiple_of(index * BLK, BLK), BLK), column:column + 128]
+        return tri_ref[spot(index), column:column + 128]
 
     def stacked(values):
         zero = jnp.zeros_like(values)
@@ -77,7 +91,7 @@
 
     def body(b, carry):
         live, first, rel, last, is_global = block_scalars(len_ref, b, half_blocks)
-        here = pl.ds(pl.multiple_of(b * BLK, BLK), BLK)
+        here = spot(b)
 
         @pl.when(jnp.logical_not(is_global))
         def sparse():
@@ -86,7 +100,7 @@
             bias_row = jnp.concatenate(
                 [jnp.where(lane, bias[2 * i], bias[2 * i + 1]) for i in range(4)], axis=1)
             for p in range(pairs):
-                at = [[first * 0 + jnp.where(live, first + rb_ref[((2 * p + s) * blocks + b) * rand + k], b) for k in range(rand)] for s in range(2)]
+                at = [[jnp.where(live, first + rb_ref[((2 * p + s) * blocks + b) * rand + k], b) for k in range(rand)] for s in range(2)]
                 def unit(column):
                     return jnp.concatenate(
                         [rows(i, column) for i in fixed]
@@ -101,11 +115,10 @@
 
         @pl.when(is_global)
         def dense():
-            span = half_blocks * BLK
             queries = [stacked(rows(b, p * 128)) * scale for p in range(pairs)]
             def chunk(c, state):
                 new = []
-                at = pl.ds(pl.multiple_of((first + c * half_blocks) * BLK, BLK), span)
+                at = span_of(first + c * half_blocks, half_blocks)
                 for p in range(pairs):
                     top, total, acc = state[p]
                     scores = dot_nt(queries[p], tri_ref[at, width + p * 128:width + (p + 1) * 128])
@@ -134,8 +147,17 @@
     for acc in accs:
         acc[...] = jnp.zeros_like(acc)
 
+    shift = len_ref[2]
+
     def spot(index):
-        return pl.ds(pl.multiple_of(index * BLK, BLK), BLK)
+        moved = index + shift
+        moved = jnp.where(moved >= blocks, moved - blocks, moved)
+        return pl.ds(pl.multiple_of(moved * BLK, BLK), BLK)
+
+    def span_of(index, count):
+        moved = index + shift
+        moved = jnp.where(moved >= blocks, moved - blocks, moved)
+        return pl.ds(pl.multiple_of(moved * BLK, BLK), count * BLK)
 
     def rows(index, column):
         return tri_ref[spot(index), column:column + 128]
@@ -184,10 +206,9 @@
 
         @pl.when(is_global)
         def dense():
-            span = half_blocks * BLK
             chunks = (last + 1) // half_blocks
             def place(c):
-                return pl.ds(pl.multiple_of((first + c * half_blocks) * BLK, BLK), span)
+                return span_of(first + c * half_blocks, half_blocks)
             queries = [stacked(rows(b, p * 128)) * scale for p in range(pairs)]
             grads = [stacked(grad_ref[spot(b), p * 128:(p + 1) * 128]) for p in range(pairs)]
             def first_pass(c, state):
@@ -260,6 +281,132 @@
     )(lengths, randoms.reshape(-1), triple, grad)
 
 
+QUAD = 4
+
+
+def group_permute(value, deep, target):
+    pairs = []
+    for z in range(deep):
+        for q in range(QUAD):
+            for h in range(2):
+                to_z, to_q = target(z, q, h)
+                pairs.append(((z * QUAD + q) * 2 + h, (to_z * QUAD + to_q) * 2 + h))
+    return lax.ppermute(value, ("deep", "quad", "head"), pairs)
+
+
+def deep_step(value, deep, bit):
+    return group_permute(value, deep, lambda z, q, h: (z ^ bit, q))
+
+
+def quad_step(value, deep, second):
+    return group_permute(value, deep, lambda z, q, h: (z, q ^ ((2 >> h) if second else (1 << h))))
+
+
+def swap(value):
+    return lax.ppermute(value, "head", [(0, 1), (1, 0)])
+
+
+def gather_deep(value, deep):
+    z = lax.axis_index("deep")
+    block = value[None]
+    bit = 1
+    while bit < deep:
+        other = deep_step(block, deep, bit)
+        low = (z & bit) == 0
+        block = jnp.concatenate(
+            [jnp.where(low, block, other), jnp.where(low, other, block)], axis=0
+        )
+        bit *= 2
+    return block
+
+
+def gather_quad(block, deep):
+    q = lax.axis_index("quad")
+    h = lax.axis_index("head")
+    bit_one, bit_two = 1 << h, 2 >> h
+    other = quad_step(block, deep, False)
+    both = jnp.stack([block, other])
+    far = quad_step(both, deep, True)
+    full = jnp.zeros((deep, QUAD) + block.shape[1:], block.dtype)
+    for piece, place in (
+        (block, q),
+        (other, q ^ bit_one),
+        (far[0], q ^ bit_two),
+        (far[1], q ^ 3),
+    ):
+        full = lax.dynamic_update_slice(full, piece[:, None], (0, place, 0, 0))
+    return full.reshape(-1, block.shape[-1])
+
+
+def pack_small(small):
+    high = lax.reduce_precision(small, 8, 7)
+    return jnp.concatenate([high, small - high]).astype(jnp.bfloat16)
+
+
+def unpack_small(packed):
+    rows = packed.shape[0] // 2
+    return packed[:rows].astype(jnp.float32) + packed[rows:].astype(jnp.float32)
+
+
+def exchange(send, small, step):
+    message = jnp.concatenate([send.astype(jnp.bfloat16), pack_small(small)], axis=0)
+    answer = step(message)
+    return answer[: send.shape[0]], small + unpack_small(answer[send.shape[0] :])
+
+
+def scatter_sum(total, small, deep):
+    q = lax.axis_index("quad")
+    h = lax.axis_index("head")
+    z = lax.axis_index("deep")
+    bit_one, bit_two = 1 << h, 2 >> h
+    columns = total.shape[-1]
+    rows = total.shape[0] // (deep * QUAD)
+    cube = total.reshape(deep, QUAD, rows, columns)
+
+    def slab(place):
+        return lax.dynamic_slice(cube, (0, place, 0, 0), (deep, 1, rows, columns)).reshape(
+            deep * rows, columns
+        )
+
+    send = jnp.concatenate([slab(q ^ bit_one), slab(q ^ 3)], axis=0)
+    got, small = exchange(send, small, lambda m: quad_step(m, deep, False))
+    got = got.astype(jnp.float32)
+    keep = slab(q) + got[: deep * rows]
+    send = slab(q ^ bit_two) + got[deep * rows :]
+    got, small = exchange(send, small, lambda m: quad_step(m, deep, True))
+    keep = keep + got.astype(jnp.float32)
+    bit = deep // 2
+    while bit:
+        span = bit * rows
+        own = jnp.where((z & bit) == 0, 0, span)
+        send = lax.dynamic_slice_in_dim(keep, span - own, span, 0)
+        got, small = exchange(send, small, lambda m, bit=bit: deep_step(m, deep, bit))
+        keep = lax.dynamic_slice_in_dim(keep, own, span, 0) + got.astype(jnp.float32)
+        bit //= 2
+    return keep, small
+
+
+def scatter_offload(total):
+    part = lax.psum_scatter(total.astype(jnp.bfloat16), "deep", scatter_dimension=0, tiled=True)
+    return lax.psum_scatter(part, "quad", scatter_dimension=0, tiled=True).astype(jnp.float32)
+
+
+def mm(left, right):
+    return jnp.einsum("td,df->tf", left, right, preferred_element_type=jnp.float32)
+
+
+def mm_nt(left, right):
+    return jnp.einsum("tf,df->td", left, right, preferred_element_type=jnp.float32)
+
+
+def mm_tn(left, right):
+    return jnp.einsum("td,tf->df", left, right, preferred_element_type=jnp.float32)
+
+
+def low(value):
+    return value.astype(jnp.bfloat16)
+
+
 def on_device(
     inputs,
     qkv_weight,
@@ -278,199 +425,172 @@
     random_blocks,
     out_grad,
 ):
-    half = inputs.shape[0]
-    width = inputs.shape[1]
+    half, width = inputs.shape
     position = lax.axis_index("head")
+    deep = lax.axis_size("deep")
+    shard = qkv_weight.shape[0]
     head_width = qkv_weight.shape[2]
-    full_qkv, full_out, full_up, full_down = (
-        lax.all_gather(qkv_weight, "dp", axis=0, tiled=True),
-        lax.all_gather(out_weight, "dp", axis=0, tiled=True),
-        lax.all_gather(up_weight, "dp", axis=0, tiled=True),
-        lax.all_gather(down_weight, "dp", axis=0, tiled=True),
-    )
-    tokens = lax.all_gather(inputs, "head", axis=0, tiled=True)
-    capacity = tokens.shape[0]
-    block_count = capacity // BLK
-    counts = item_lengths[0] // BLK
-    live = (jnp.arange(block_count, dtype=jnp.int32) < jnp.sum(counts)).astype(jnp.int32)
-    bias = jnp.stack([qv_bias[0], jnp.zeros_like(qv_bias[0]), qv_bias[1]])
-    triple = (
-        jnp.einsum("td,dcf->tcf", tokens, full_qkv, preferred_element_type=jnp.float32) + bias
-    ).astype(jnp.bfloat16)
-    attended = attention_forward(item_lengths[0], random_blocks[0], triple.reshape(capacity, 3 * head_width))
-    part = attended
-    proj = lax.psum_scatter(
-        jnp.einsum("tf,df->td", part, full_out, preferred_element_type=jnp.float32).astype(
-            jnp.bfloat16
-        ),
-        "head",
-        scatter_dimension=0,
-        tiled=True,
-    ).astype(jnp.float32)
+    up_width = up_weight.shape[1]
+    half_blocks = half // BLK
+    lengths = item_lengths[0]
+    layout = jnp.concatenate([lengths, (position * half_blocks)[None].astype(jnp.int32)])
+    randoms = random_blocks[0]
+
+    tokens = jnp.concatenate([inputs, swap(inputs)], axis=0)
+    qkv_deep = gather_deep(qkv_weight.reshape(shard, 3 * head_width), deep)
+    rest_deep = gather_deep(jnp.concatenate([down_weight, out_weight, up_weight], axis=1), deep)
+    full_qkv = gather_quad(qkv_deep, deep)
+    rest_deep, full_qkv = lax.optimization_barrier((rest_deep, full_qkv))
+    offload = lax.all_gather(
+        rest_deep[:, :, up_width:].reshape(deep * shard, -1), "quad", axis=0, tiled=False
+    )
+    offload = jnp.swapaxes(offload.reshape(QUAD, deep, shard, -1), 0, 1).reshape(width, -1)
+    full_out, full_up = offload[:, :head_width], offload[:, head_width:]
+    full_down = gather_quad(rest_deep[:, :, :up_width], deep)
+
+    bias = jnp.concatenate([qv_bias[0], jnp.zeros_like(qv_bias[0]), qv_bias[1]])
+    triple = low(mm(tokens, full_qkv) + bias)
+    attended = attention_forward(layout, randoms, triple)
+
+    other = swap(low(mm_nt(attended[half:], full_out)))
+    proj = mm_nt(attended[:half], full_out) + other.astype(jnp.float32)
     normed_one_out, normed_one, inverse_one = norm_forward(
         proj + out_bias + inputs.astype(jnp.float32), first_gain, first_shift
     )
-    hidden = lax.all_gather(normed_one_out.astype(jnp.bfloat16), "head", axis=0, tiled=True)
-    upper = (
-        jnp.einsum("td,df->tf", hidden, full_up, preferred_element_type=jnp.float32) + up_bias
-    ).astype(jnp.bfloat16)
-    active = jax.nn.gelu(upper.astype(jnp.float32), approximate=True).astype(jnp.bfloat16)
-    part = active
-    down = lax.psum_scatter(
-        jnp.einsum("tf,df->td", part, full_down, preferred_element_type=jnp.float32).astype(
-            jnp.bfloat16
-        ),
-        "head",
-        scatter_dimension=0,
-        tiled=True,
-    ).astype(jnp.float32)
+    hidden_own = low(normed_one_out)
+    hidden_other = swap(hidden_own)
+    hidden = jnp.concatenate([hidden_own, hidden_other], axis=0)
+
+    def gelu_tanh(values):
+        return jax.nn.gelu(values, approximate=True)
+
+    upper_own = low(mm(hidden_own, full_up) + up_bias)
+    upper_other = low(mm(hidden_other, full_up) + up_bias)
+    active_other = low(gelu_tanh(upper_other.astype(jnp.float32)))
+    active_own = low(gelu_tanh(upper_own.astype(jnp.float32)))
+    other = swap(low(mm_nt(active_other, full_down)))
+    down = mm_nt(active_own, full_down) + other.astype(jnp.float32)
+    active = jnp.concatenate([active_own, active_other], axis=0)
     normed_two_out, normed_two, inverse_two = norm_forward(
         down + down_bias + normed_one_out, second_gain, second_shift
     )
-    live_rows = jnp.repeat(live, BLK).astype(jnp.float32)
-    live_half = lax.dynamic_slice_in_dim(live_rows, position * half, half, 0)
-    layer_out = (normed_two_out * live_half[:, None]).astype(jnp.bfloat16)
-    cotangent = out_grad.astype(jnp.float32) * live_half[:, None]
+    row = position * half + lax.broadcasted_iota(jnp.int32, (half, 1), 0)
+    live = (row < jnp.sum(lengths)).astype(jnp.float32)
+    layer_out = low(normed_two_out * live)
+    cotangent = out_grad.astype(jnp.float32) * live
     second_gain_part = jnp.sum(cotangent * normed_two, axis=0)
     second_shift_part = jnp.sum(cotangent, axis=0)
     grad_res_two = norm_backward(cotangent, normed_two, inverse_two, second_gain)
     down_bias_part = jnp.sum(grad_res_two, axis=0)
-    grad_down_rows = lax.all_gather(grad_res_two.astype(jnp.bfloat16), "head", axis=0, tiled=True)
-    grad_active = jnp.einsum(
-        "td,df->tf", grad_down_rows, full_down, preferred_element_type=jnp.float32
-    )
-    down_local = jnp.einsum("td,tf->df", grad_down_rows, active, preferred_element_type=jnp.float32)
-
-    def gelu_tanh(values):
-        return jax.nn.gelu(values, approximate=True)
-
-    gelu_pull = jax.vjp(gelu_tanh, upper.astype(jnp.float32))[1]
-    grad_upper = gelu_pull(grad_active)[0].astype(jnp.bfloat16)
+    grad_own = low(grad_res_two)
+    grad_other = swap(grad_own)
+    grad_down_rows = jnp.concatenate([grad_own, grad_other], axis=0)
+
+    def pull(grad_rows, upper_rows):
+        grad_active = mm(grad_rows, full_down)
+        return low(jax.vjp(gelu_tanh, upper_rows.astype(jnp.float32))[1](grad_active)[0])
+
+    grad_upper_own = pull(grad_own, upper_own)
+    grad_upper_other = pull(grad_other, upper_other)
+    grad_upper = jnp.concatenate([grad_upper_own, grad_upper_other], axis=0)
+    down_local = low(mm_tn(grad_down_rows, active))
     up_bias_part = jnp.sum(grad_upper.astype(jnp.float32), axis=0)
-    up_local = jnp.einsum("td,tf->df", hidden, grad_upper, preferred_element_type=jnp.float32)
-    part = grad_upper
-    grad_norm_one = (
-        lax.psum_scatter(
-            jnp.einsum("tf,df->td", part, full_up, preferred_element_type=jnp.float32).astype(
-                jnp.bfloat16
-            ),
-            "head",
-            scatter_dimension=0,
-            tiled=True,
-        ).astype(jnp.float32)
-        + grad_res_two
-    )
+    other = swap(low(mm_nt(grad_upper_other, full_up)))
+    grad_norm_one = mm_nt(grad_upper_own, full_up) + other.astype(jnp.float32) + grad_res_two
+    up_local = low(mm_tn(hidden, grad_upper))
     first_gain_part = jnp.sum(grad_norm_one * normed_one, axis=0)
     first_shift_part = jnp.sum(grad_norm_one, axis=0)
     grad_res_one = norm_backward(grad_norm_one, normed_one, inverse_one, first_gain)
     out_bias_part = jnp.sum(grad_res_one, axis=0)
-    grad_proj = lax.all_gather(grad_res_one.astype(jnp.bfloat16), "head", axis=0, tiled=True)
-    grad_attended = jnp.einsum(
-        "td,df->tf", grad_proj, full_out, preferred_element_type=jnp.float32
-    ).astype(jnp.bfloat16)
-    out_local = jnp.einsum("td,tf->df", grad_proj, attended, preferred_element_type=jnp.float32)
-    grad_flat, bias_sums = attention_backward(
-        item_lengths[0], random_blocks[0], triple.reshape(capacity, 3 * head_width), grad_attended
-    )
-    grad_triple = grad_flat.reshape(capacity, 3, head_width)
-    qv_bias_part = bias_sums[:2]
-    qkv_local = jnp.einsum("td,tcf->dcf", tokens, grad_triple, preferred_element_type=jnp.float32)
-    part = grad_triple
-    input_grad = (
-        lax.psum_scatter(
-            jnp.einsum("tcf,dcf->td", part, full_qkv, preferred_element_type=jnp.float32).astype(
-                jnp.bfloat16
-            ),
-            "head",
-            scatter_dimension=0,
-            tiled=True,
-        ).astype(jnp.float32)
-        + grad_res_one
-    ).astype(jnp.bfloat16)
-    grad_qkv, grad_out, grad_up, grad_down = (
-        lax.psum_scatter(qkv_local, "dp", scatter_dimension=0, tiled=True),
-        lax.psum_scatter(out_local, "dp", scatter_dimension=0, tiled=True),
-        lax.psum_scatter(up_local, "dp", scatter_dimension=0, tiled=True),
-        lax.psum_scatter(down_local, "dp", scatter_dimension=0, tiled=True),
-    )
-    up_width = up_bias.shape[0]
-    qv_full = lax.dynamic_update_slice_in_dim(
-        jnp.zeros((2, width), jnp.float32), qv_bias_part, position * head_width, 1
-    )
-    up_full = lax.dynamic_update_slice_in_dim(
-        jnp.zeros((up_width * lax.axis_size("head"),), jnp.float32),
-        up_bias_part,
-        position * up_width,
-        0,
-    )
-    totals = lax.psum(
-        (
-            qv_full,
-            up_full,
+    grad_proj_own = low(grad_res_one)
+    grad_proj = jnp.concatenate([grad_proj_own, swap(grad_proj_own)], axis=0)
+    grad_attended = low(mm(grad_proj, full_out))
+    out_local = low(mm_tn(grad_proj, attended))
+    grad_triple, bias_sums = attention_backward(layout, randoms, triple, grad_attended)
+
+    other = swap(low(mm_nt(grad_triple[half:], full_qkv)))
+    qkv_local = mm_tn(tokens, grad_triple)
+    input_grad = low(mm_nt(grad_triple[:half], full_qkv) + other.astype(jnp.float32) + grad_res_one)
+
+    grad_down = scatter_offload(down_local)
+    grad_up = scatter_offload(up_local)
+    grad_out = scatter_offload(out_local)
+
+    shared = jnp.stack(
+        [
             out_bias_part,
             first_gain_part,
             first_shift_part,
             down_bias_part,
             second_gain_part,
             second_shift_part,
-        ),
-        ("dp", "head"),
-    )
-    grad_qv_bias = lax.dynamic_slice_in_dim(totals[0], position * head_width, head_width, 1)
-    grad_up_bias = lax.dynamic_slice_in_dim(totals[1], position * up_width, up_width, 0)
+        ]
+    )
+    shared = shared + swap(shared)
+    small = jnp.concatenate([shared.reshape(-1), up_bias_part, bias_sums[:2].reshape(-1)])
+    grad_qkv, small = scatter_sum(qkv_local, small.reshape(-1, 3 * head_width), deep)
+    small = small.reshape(-1)
+    count = shared.size
+    totals = small[:count].reshape(shared.shape)
+    grad_up_bias = small[count : count + up_width]
+    grad_qv_bias = small[count + up_width :].reshape(2, head_width)
     return (
         layer_out,
         input_grad,
-        grad_qkv,
+        grad_qkv.reshape(shard, 3, head_width),
         grad_qv_bias,
         grad_out,
+        totals[0],
+        totals[1],
         totals[2],
-        totals[3],
-        totals[4],
         grad_up,
         grad_up_bias,
         grad_down,
+        totals[3],
+        totals[4],
         totals[5],
-        totals[6],
-        totals[7],
     )
 
 
 def solution(mesh):
+    devices = mesh.devices.reshape(-1, QUAD, mesh.shape["head"])
+    fine = Mesh(devices, ("deep", "quad", "head"))
+    rows = ("deep", "quad", "head")
+    dp = ("deep", "quad")
     in_specs = (
-        P(("dp", "head"), None),
-        P("dp", None, "head"),
+        P(rows, None),
+        P(dp, None, "head"),
         P(None, "head"),
-        P("dp", "head"),
-        P(),
-        P(),
-        P(),
-        P("dp", "head"),
+        P(dp, "head"),
+        P(),
+        P(),
+        P(),
+        P(dp, "head"),
         P("head"),
-        P("dp", "head"),
-        P(),
-        P(),
-        P(),
-        P("dp", None),
-        P("dp", "head", None, None),
-        P(("dp", "head"), None),
+        P(dp, "head"),
+        P(),
+        P(),
+        P(),
+        P(dp, None),
+        P(dp, "head", None, None),
+        P(rows, None),
     )
     out_specs = (
-        P(("dp", "head"), None),
-        P(("dp", "head"), None),
-        P("dp", None, "head"),
+        P(rows, None),
+        P(rows, None),
+        P(dp, None, "head"),
         P(None, "head"),
-        P("dp", "head"),
-        P(),
-        P(),
-        P(),
-        P("dp", "head"),
+        P(dp, "head"),
+        P(),
+        P(),
+        P(),
+        P(dp, "head"),
         P("head"),
-        P("dp", "head"),
+        P(dp, "head"),
         P(),
         P(),
         P(),
     )
     return jax.shard_map(
-        on_device, mesh=mesh, in_specs=in_specs, out_specs=out_specs, check_vma=False
-    )
+        on_device, mesh=fine, in_specs=in_specs, out_specs=out_specs, check_vma=False
+    )

time: 1070 us -> 405 us (0.38)
  waiting for transfers between devices: 735 us -> 161 us
  blocking collectives: 93.6 us -> 0 us
  starting transfers between devices: 1.81 us -> 20.4 us
    reduce_scatter x7 -> x5, waiting for transfers between devices: 449 us -> 49.5 us  [the longest x2 49.4 us: scatter_offload(): lax.psum_scatter(part, 'quad', scatter_dimension=0, tiled=True)]
    all_gather x7 -> x1, waiting for transfers between devices: 181 us -> 1.95 us  [on_device(): lax.all_gather(rest_deep[:, :, up_width:].reshape(deep * shard, -1), 'qua...]
    ppermute x0 -> x21, waiting for transfers between devices: none -> 94 us  [the longest x12 87.5 us: group_permute(): return lax.ppermute(value, ('deep', 'quad', 'head'), pairs)]
    unnamed x16 -> x8, waiting for transfers between devices: 105 us -> 16.1 us
    all_gather x1 -> x0, blocking collectives: 49.1 us -> none  [on_device(): lax.all_gather(out_weight, 'dp', axis=0, tiled=True)]
    psum x1 -> x0, blocking collectives: 44.5 us -> none  [on_device(): lax.psum((qv_full, up_full, out_bias_part, first_gain_part, first_shift_p...]
    ppermute x0 -> x21, starting transfers between devices: none -> 20.1 us  [the longest x12 18.5 us: group_permute(): return lax.ppermute(value, ('deep', 'quad', 'head'), pairs)]
    dot_general x12 -> x18, matrix products: 83.9 us -> 75.5 us  [the longest x6 27.3 us: mm(): jnp.einsum('td,df->tf', left, right, preferred_element_type=jnp.float32)]
  transfers between devices with their start and end apart: 15 -> 28, of which waited for: 14 -> 16; matrix products, arithmetic and copies ran while one was open for 5% -> 20% of each run, Pallas kernels for 0% -> 20%
where the time goes in v2:
time: 405 us; the launch traced here: 402 us
  waiting for transfers between devices  161 us (40%)
  Pallas kernels  78.6 us (19%)
  matrix products  75.5 us (19%)
  other arithmetic  25.6 us (6%)
  local copies, waits for them, and re-layouts  24.8 us (6%)
  starting transfers between devices  20.4 us (5%)
  between operations  15.3 us (4%)
    ppermute x12, waiting for transfers between devices, group_permute(): return lax.ppermute(value, ('deep', 'quad', 'head'), pairs)  87.5 us
    pallas_call x1, Pallas kernels, attention_backward(): pl.pallas_call(functools.partial(attn_bwd_kernel, pairs, rand, blocks //...  51.1 us
    reduce_scatter x2, waiting for transfers between devices, scatter_offload(): lax.psum_scatter(part, 'quad', scatter_dimension=0, tiled=True)  49.4 us
    pallas_call x1, Pallas kernels, attention_forward(): pl.pallas_call(functools.partial(attn_fwd_kernel, pairs, rand, blocks //...  27.6 us
    dot_general x6, matrix products, mm(): jnp.einsum('td,df->tf', left, right, preferred_element_type=jnp.float32)  27.3 us
    dot_general x8, matrix products, mm_nt(): jnp.einsum('tf,df->td', left, right, preferred_element_type=jnp.float32)  25.3 us
    dot_general x4, matrix products, mm_tn(): jnp.einsum('td,tf->df', left, right, preferred_element_type=jnp.float32)  23 us
    ppermute x12, starting transfers between devices, group_permute(): return lax.ppermute(value, ('deep', 'quad', 'head'), pairs)  18.5 us
  transfers between devices with their start and end apart: 28, of which 16 were waited for; matrix products, arithmetic and copies ran while one was open for 20% of the time, Pallas kernels for 20%

profile of v2, /device:TPU:0, one launch (start us, length us, event | category | flops | bytes accessed | tf_op | source)
XLA Modules:
  0.0 401.6 jit_solution(5630874895706768970)
XLA Ops:
  8.3 3.1 collective-permute-start.3
  14.9 2.6 collective-permute-start.4
  17.5 9.0 %collective-permute-done.1 = bf16[1,48,3456]{2,1,0:T(8,128)(2,1)S(1)} collective-permute-done((bf16[1,48,3456]{2,1,0:T(8,128)(2,1)S(1)}, bf16[1,48,3456]{2,1,0:T(8,128)(2,1)S(1)}, u32[]{:S(2)}, u32[]{:S(2)}) %collective-permute-start.1) | collective-permute-done | bytes 331808 | tf_op jit(solution)/shard_map/ppermute | solution.py:294
  33.1 3.0 collective-permute-done.5
  38.6 21.2 %collective-permute-done.2 = bf16[2,48,3456]{2,1,0:T(8,128)(2,1)S(1)} collective-permute-done((bf16[2,48,3456]{2,1,0:T(8,128)(2,1)S(1)}, bf16[2,48,3456]{2,1,0:T(8,128)(2,1)S(1)}, u32[]{:S(2)}, u32[]{:S(2)}) %collective-permute-start.2) | collective-permute-done | bytes 663584 | tf_op jit(solution)/shard_map/ppermute | solution.py:294
  68.5 6.5 %fusion.tri_ref = bf16[1536,1152]{1,0:T(8,128)(2,1)} fusion(bf16[1536,768]{1,0:T(8,128)(2,1)S(1)} %constant_dynamic-update-slice_fusion, bf16[768,1152]{1,0:T(8,128)(2,1)} %bitcast.13, f32[1152]{0:T(1024)S(1)} %pad_maximum_fusion.18), kind=kOutput, calls=%fused_computation.12 | convolution fusion | flops 2721447936 | bytes 7672320 | tf_op jit(solution)/shard_map/td,df->tf/dot_general | solution.py:395
  75.0 27.6 %attend_forward.1 = bf16[1536,384]{1,0:T(8,128)(2,1)} custom-call(s32[3]{0:T(128)} %pad_add_fusion.len_ref, s32[432]{0:T(512)} %reshape_squeeze.4.rb_ref, bf16[1536,1152]{1,0:T(8,128)(2,1)} %fusion.tri_ref), custom_call_target="tpu_custom_call" | custom-call | tf_op jit(solution)/shard_map/attend_forward/pallas_call | solution.py:264
  109.6 8.1 %collective-permute-done.8 = bf16[4,48,1536]{2,1,0:T(8,128)(2,1)S(1)} collective-permute-done((bf16[4,48,1536]{2,1,0:T(8,128)(2,1)S(1)}, bf16[4,48,1536]{2,1,0:T(8,128)(2,1)S(1)}, u32[]{:S(2)}, u32[]{:S(2)}) %collective-permute-start.8) | collective-permute-done | bytes 589856 | tf_op jit(solution)/shard_map/ppermute | solution.py:294
  121.6 12.4 %collective-permute-done.9 = bf16[2,4,48,1536]{3,2,1,0:T(8,128)(2,1)S(1)} collective-permute-done((bf16[2,4,48,1536]{3,2,1,0:T(8,128)(2,1)S(1)}, bf16[2,4,48,1536]{3,2,1,0:T(8,128)(2,1)S(1)}, u32[]{:S(2)}, u32[]{:S(2)}) %collective-permute-start.9) | collective-permute-done | bytes 1179680 | tf_op jit(solution)/shard_map/ppermute | solution.py:294
  136.2 4.0 %convolution_convert_fusion.4 = bf16[768,768]{1,0:T(8,128)(2,1)} fusion(bf16[768,1536]{1,0:T(8,128)(2,1)S(1)} %bitcast.99, bf16[768,1536]{1,0:T(8,128)(2,1)S(1)} %add_convert_fusion), kind=kOutput, calls=%fused_computation.79 | convolution fusion | flops 1824325632 | bytes 5898240 | tf_op jit(solution)/shard_map/tf,df->td/dot_general | solution.py:399
  141.6 3.8 add_convert_fusion.1
  145.5 4.9 %fusion.85 = (f32[768]{0:T(1024)S(1)}, f32[768,768]{1,0:T(8,128)S(1)}) fusion(f32[768]{0:T(1024)S(1)} %copy-done.36, f32[768]{0:T(1024)S(1)} %copy-done.28, f32[768]{0:T(1024)S(1)} %add_rsqrt_fusion.1, f32[768,768]{1,0:T(8,128)S(1)} %get-tuple-element.114, f32[768]{0:T(1024)S(1)} %broadcast_multiply_fusion.5, f32[768]{0:T(1024)S(1)} %copy-done.45, ...), kind=kOutput, calls=%fused_computation.186 | convolution fusion | flops 1829043456 | bytes 10635264 | tf_op jit(solution)/shard_map/tf,df->td/dot_general | solution.py:399
  156.4 2.5 collective-permute-done.12
  158.9 5.8 %fusion.18 = (bf16[768,1536]{1,0:T(8,128)(2,1)}, bf16[768,1536]{1,0:T(8,128)(2,1)S(1)}) fusion(bf16[768,1536]{1,0:T(8,128)(2,1)S(1)} %copy-done.49, bf16[768,768]{1,0:T(8,128)(2,1)S(1)} %collective-permute-done.12, bf16[768,1536]{1,0:T(8,128)(2,1)S(1)} %bitcast.101), kind=kOutput, calls=%fused_computation.30 | convolution fusion | flops 1839071232 | bytes 10616832 | tf_op jit(solution)/shard_map/td,df->tf/dot_general | solution.py:395
  167.2 5.7 %fusion.12 = (bf16[768,1536]{1,0:T(8,128)(2,1)}, bf16[768,1536]{1,0:T(8,128)(2,1)S(1)}) fusion(bf16[768,1536]{1,0:T(8,128)(2,1)S(1)} %add_convert_fusion.1, bf16[768,768]{1,0:T(8,128)(2,1)S(1)} %convert_element_type.172, bf16[768,1536]{1,0:T(8,128)(2,1)S(1)} %bitcast.102), kind=kOutput, calls=%fused_computation.24 | convolution fusion | flops 1839071232 | bytes 10616832 | tf_op jit(solution)/shard_map/td,df->tf/dot_general | solution.py:395
  172.9 3.2 multiply_reduce_fusion.1
  179.4 2.7 collective-permute-done.14
  184.4 8.0 %fusion.25 = bf16[768,1536]{1,0:T(8,128)(2,1)} fusion(bf16[768,1536]{1,0:T(8,128)(2,1)} %get-tuple-element.93, bf16[768,1536]{1,0:T(8,128)(2,1)} %get-tuple-element.91, bf16[768,768]{1,0:T(8,128)(2,1)} %copy-done.43, bf16[768,768]{1,0:T(8,128)(2,1)S(1)} %copy-done.18), kind=kOutput, calls=%fused_computation.40 | convolution fusion | flops 3639214080 | bytes 9437184 | tf_op jit(solution)/shard_map/td,tf->df/dot_general | solution.py:403
  194.1 7.3 %convolution_convert_fusion = bf16[768,1536]{1,0:T(8,128)(2,1)} fusion(bf16[768,1536]{1,0:T(8,128)(2,1)S(1)} %copy-done.11, bf16[768,1536]{1,0:T(8,128)(2,1)} %copy-done.12, bf16[768,768]{1,0:T(8,128)(2,1)} %copy-done.40, bf16[768,768]{1,0:T(8,128)(2,1)S(1)} %fusion.37), kind=kOutput, calls=%fused_computation.41 | convolution fusion | flops 3639214080 | bytes 9437184 | tf_op jit(solution)/shard_map/td,tf->df/dot_general | solution.py:403
  203.6 2.4 convert_reduce_fusion
  207.7 3.5 convolution_convert_fusion.1.grad_ref
  211.2 51.1 %attend_backward.1 = (bf16[1536,1152]{1,0:T(8,128)(2,1)}, f32[8,384]{1,0:T(8,128)}) custom-call(s32[3]{0:T(128)} %pad_add_fusion.len_ref, s32[432]{0:T(512)} %reshape_squeeze.4.rb_ref, bf16[1536,1152]{1,0:T(8,128)(2,1)} %fusion.tri_ref, bf16[1536,384]{1,0:T(8,128)(2,1)} %convolution_convert_fusion.1.grad_ref), custom_call_target="tpu_custom_call" | custom-call | tf_op jit(solution)/shard_map/attend_backward/pallas_call | solution.py:275
  263.1 5.4 %fusion.86 = f32[768,1152]{1,0:T(8,128)S(1)} fusion(bf16[1536,768]{1,0:T(8,128)(2,1)S(1)} %copy-done.21, bf16[1536,1152]{1,0:T(8,128)(2,1)} %get-tuple-element.20), kind=kOutput, calls=%fused_computation.187 | convolution fusion | flops 2717908992 | bytes 9437184 | tf_op jit(solution)/shard_map/td,tf->df/dot_general | solution.py:403
  270.3 11.9 %collective-permute-done.17 = bf16[396,1152]{1,0:T(8,128)(2,1)S(1)} collective-permute-done((bf16[396,1152]{1,0:T(8,128)(2,1)S(1)}, bf16[396,1152]{1,0:T(8,128)(2,1)S(1)}, u32[]{:S(2)}, u32[]{:S(2)}) %collective-permute-start.17) | collective-permute-done | bytes 912416 | tf_op jit(solution)/shard_map/ppermute | solution.py:294
  285.1 7.8 %collective-permute-done.18 = bf16[204,1152]{1,0:T(8,128)(2,1)S(1)} collective-permute-done((bf16[204,1152]{1,0:T(8,128)(2,1)}, bf16[204,1152]{1,0:T(8,128)(2,1)S(1)}, u32[]{:S(2)}, u32[]{:S(2)}) %collective-permute-start.18) | collective-permute-done | bytes 470048 | tf_op jit(solution)/shard_map/ppermute | solution.py:294
  296.3 2.3 collective-permute-start.19
  298.6 4.2 %fusion.42 = bf16[768,768]{1,0:T(8,128)(2,1)} fusion(bf16[768,1152]{1,0:T(8,128)(2,1)} %bitcast.13, bf16[1536,1152]{1,0:T(8,128)(2,1)S(1)} %copy-done.39), kind=kOutput, calls=%fused_computation.76 | convolution fusion | flops 1359544320 | bytes 4718592 | tf_op jit(solution)/shard_map/tf,df->td/dot_general | solution.py:399
  302.9 11.8 %collective-permute-done.19 = bf16[108,1152]{1,0:T(8,128)(2,1)S(1)} collective-permute-done((bf16[108,1152]{1,0:T(8,128)(2,1)}, bf16[108,1152]{1,0:T(8,128)(2,1)S(1)}, u32[]{:S(2)}, u32[]{:S(2)}) %collective-permute-start.19) | collective-permute-done | bytes 248864 | tf_op jit(solution)/shard_map/ppermute | solution.py:294
  315.9 5.1 %add_convert_fusion.2 = bf16[768,768]{1,0:T(8,128)(2,1)} fusion(f32[768,768]{1,0:T(8,128)S(1)} %copy-done.1, bf16[768,768]{1,0:T(8,128)(2,1)} %collective-permute-done.15, bf16[768,1152]{1,0:T(8,128)(2,1)} %bitcast.13, bf16[1536,1152]{1,0:T(8,128)(2,1)} %get-tuple-element.20), kind=kOutput, calls=%fused_computation.52 | convolution fusion | flops 1361313792 | bytes 8257536 | tf_op jit(solution)/shard_map/tf,df->td/dot_general | solution.py:399
  321.0 15.9 %reduce-scatter.19.cloned.1.call-done = bf16[48,384]{1,0:T(8,128)(2,1)} async-done(((bf16[192,384]{1,0:T(8,128)(2,1)}), bf16[48,384]{1,0:T(8,128)(2,1)}) %reduce-scatter.19.cloned.1.call-update) | async-done | bytes 36880
  341.9 22.9 %reduce-scatter.17.cloned.1.call-done = bf16[48,1536]{1,0:T(8,128)(2,1)} async-done(((bf16[192,1536]{1,0:T(8,128)(2,1)}), bf16[48,1536]{1,0:T(8,128)(2,1)}) %reduce-scatter.17.cloned.1.call-update) | async-done | bytes 147472 | tf_op jit(solution)/shard_map/reduce_scatter | solution.py:391
  366.4 26.6 %reduce-scatter.13.cloned.1.call-done = bf16[48,1536]{1,0:T(8,128)(2,1)} async-done(((bf16[192,1536]{1,0:T(8,128)(2,1)}), bf16[48,1536]{1,0:T(8,128)(2,1)}) %reduce-scatter.13.cloned.1.call-update) | async-done | bytes 147472 | tf_op jit(solution)/shard_map/reduce_scatter | solution.py:391
  (246 shorter events, 74.1 us)
Async XLA Ops:
  7.2 97.4 %all-gather.2.cloned.1.call-start = ((), (), s32[]{:S(2)}) async-start(), calls=%async_computation.6 | async-start | bytes 3686400 | tf_op jit(solution)/shard_map/all_gather | solution.py:444
  8.3 6.6 %collective-permute-start.3 = (bf16[1,48,1152]{2,1,0:T(8,128)(2,1)S(1)}, bf16[1,48,1152]{2,1,0:T(8,128)(2,1)S(1)}, u32[]{:S(2)}, u32[]{:S(2)}) collective-permute-start(bf16[1,48,1152]{2,1,0:T(8,128)(2,1)S(1)} %broadcast_in_dim_reshape.3), channel_id=1, source_target_pairs={{0,8},{1,9},{2,10},{3,11},{4,12},{5,13},{6,14},{7,15},{8,0},{9,1},... | collective-permute-start | bytes 331784 | tf_op jit(solution)/shard_map/ppermute | solution.py:294
  12.4 14.1 %collective-permute-start.1 = (bf16[1,48,3456]{2,1,0:T(8,128)(2,1)S(1)}, bf16[1,48,3456]{2,1,0:T(8,128)(2,1)S(1)}, u32[]{:S(2)}, u32[]{:S(2)}) collective-permute-start(bf16[1,48,3456]{2,1,0:T(8,128)(2,1)S(1)} %maximum_bitcast_fusion), channel_id=1, source_target_pairs={{0,8},{1,9},{2,10},{3,11},{4,12},{5,13},{6,14},{7,15},{8,0},{9,1},... | collective-permute-start | bytes 995336 | tf_op jit(solution)/shard_map/ppermute | solution.py:294
  14.9 12.7 %collective-permute-start.4 = (bf16[2,48,1152]{2,1,0:T(8,128)(2,1)S(1)}, bf16[2,48,1152]{2,1,0:T(8,128)(2,1)S(1)}, u32[]{:S(2)}, u32[]{:S(2)}) collective-permute-start(bf16[2,48,1152]{2,1,0:T(8,128)(2,1)S(1)} %pad_maximum_fusion.15), channel_id=1, source_target_pairs={{0,16},{1,17},{2,18},{3,19},{4,20},{5,21},{6,22},{7,23},{8,24},{9,... | collective-permute-start | bytes 663560 | tf_op jit(solution)/shard_map/ppermute | solution.py:294
  27.7 8.4 %collective-permute-start.5 = (bf16[4,48,1152]{2,1,0:T(8,128)(2,1)S(1)}, bf16[4,48,1152]{2,1,0:T(8,128)(2,1)S(1)}, u32[]{:S(2)}, u32[]{:S(2)}) collective-permute-start(bf16[4,48,1152]{2,1,0:T(8,128)(2,1)S(1)} %get-tuple-element.104), channel_id=1, source_target_pairs={{0,2},{1,5},{2,0},{3,7},{4,6},{5,1},{6,4},{7,3},{8,10},{9,13},{10,... | collective-permute-start | bytes 1327112 | tf_op jit(solution)/shard_map/ppermute | solution.py:294
  29.4 30.4 %collective-permute-start.2 = (bf16[2,48,3456]{2,1,0:T(8,128)(2,1)S(1)}, bf16[2,48,3456]{2,1,0:T(8,128)(2,1)S(1)}, u32[]{:S(2)}, u32[]{:S(2)}) collective-permute-start(bf16[2,48,3456]{2,1,0:T(8,128)(2,1)S(1)} %pad_maximum_fusion.11), channel_id=1, source_target_pairs={{0,16},{1,17},{2,18},{3,19},{4,20},{5,21},{6,22},{7,23},{8,24},{9,... | collective-permute-start | bytes 1990664 | tf_op jit(solution)/shard_map/ppermute | solution.py:294
  36.2 23.9 %collective-permute-start.6 = (bf16[2,4,48,1152]{3,2,1,0:T(8,128)(2,1)S(1)}, bf16[2,4,48,1152]{3,2,1,0:T(8,128)(2,1)S(1)}, u32[]{:S(2)}, u32[]{:S(2)}) collective-permute-start(bf16[2,4,48,1152]{3,2,1,0:T(8,128)(2,1)S(1)} %pad_maximum_fusion.10), channel_id=1, source_target_pairs={{0,4},{1,3},{2,6},{3,1},{4,0},{5,7},{6,2},{7,5},{8,12},{9,11},{10,... | collective-permute-start | bytes 2654216 | tf_op jit(solution)/shard_map/ppermute | solution.py:294
  62.7 222.3 %reduce-scatter.9.cloned.1.call-start = ((), (), s32[]{:S(2)}) async-start(), calls=%async_computation.7 | async-start | bytes 737280 | tf_op jit(solution)/shard_map/reduce_scatter | solution.py:390
  62.7 3.0 collective-permute-start
  106.7 27.5 %copy-start.4 = (bf16[4,4,48,1920]{3,2,1,0:T(8,128)(2,1)}, bf16[4,4,48,1920]{3,2,1,0:T(8,128)(2,1)S(1)}, u32[]{:S(2)}) copy-start(bf16[4,4,48,1920]{3,2,1,0:T(8,128)(2,1)S(1)} %copy.56) | copy-start | bytes 8847364
  107.5 11.8 %collective-permute-start.7 = (bf16[768,768]{1,0:T(8,128)(2,1)S(1)}, bf16[768,768]{1,0:T(8,128)(2,1)S(1)}, u32[]{:S(2)}, u32[]{:S(2)}) collective-permute-start(bf16[768,768]{1,0:T(8,128)(2,1)S(1)} %convolution_convert_fusion.2), channel_id=1, source_target_pairs={{0,1},{1,0},{2,3},{3,2},{4,5},{5,4},{6,7},{7,6},{8,9},{9,8},{10,11... | collective-permute-start | bytes 3538952 | tf_op jit(solution)/shard_map/ppermute | solution.py:306
  107.7 9.9 %collective-permute-start.8 = (bf16[4,48,1536]{2,1,0:T(8,128)(2,1)S(1)}, bf16[4,48,1536]{2,1,0:T(8,128)(2,1)S(1)}, u32[]{:S(2)}, u32[]{:S(2)}) collective-permute-start(bf16[4,48,1536]{2,1,0:T(8,128)(2,1)S(1)} %get-tuple-element.96), channel_id=1, source_target_pairs={{0,2},{1,5},{2,0},{3,7},{4,6},{5,1},{6,4},{7,3},{8,10},{9,13},{10,... | collective-permute-start | bytes 1769480 | tf_op jit(solution)/shard_map/ppermute | solution.py:294
  117.8 16.3 %collective-permute-start.9 = (bf16[2,4,48,1536]{3,2,1,0:T(8,128)(2,1)S(1)}, bf16[2,4,48,1536]{3,2,1,0:T(8,128)(2,1)S(1)}, u32[]{:S(2)}, u32[]{:S(2)}) collective-permute-start(bf16[2,4,48,1536]{3,2,1,0:T(8,128)(2,1)S(1)} %pad_maximum_fusion.8), channel_id=1, source_target_pairs={{0,4},{1,3},{2,6},{3,1},{4,0},{5,7},{6,2},{7,5},{8,12},{9,11},{10,... | collective-permute-start | bytes 3538952 | tf_op jit(solution)/shard_map/ppermute | solution.py:294
  121.5 12.7 %collective-permute-start.10 = (bf16[768,768]{1,0:T(8,128)(2,1)S(1)}, bf16[768,768]{1,0:T(8,128)(2,1)S(1)}, u32[]{:S(2)}, u32[]{:S(2)}) collective-permute-start(bf16[768,768]{1,0:T(8,128)(2,1)S(1)} %fusion.37), channel_id=1, source_target_pairs={{0,1},{1,0},{2,3},{3,2},{4,5},{5,4},{6,7},{7,6},{8,9},{9,8},{10,11... | collective-permute-start | bytes 3538952 | tf_op jit(solution)/shard_map/ppermute | solution.py:306
  140.3 5.1 %collective-permute-start.11 = (bf16[768,768]{1,0:T(8,128)(2,1)}, bf16[768,768]{1,0:T(8,128)(2,1)}, u32[]{:S(2)}, u32[]{:S(2)}) collective-permute-start(bf16[768,768]{1,0:T(8,128)(2,1)} %convolution_convert_fusion.4), channel_id=1, source_target_pairs={{0,1},{1,0},{2,3},{3,2},{4,5},{5,4},{6,7},{7,6},{8,9},{9,8},{10,11... | collective-permute-start | bytes 3538952 | tf_op jit(solution)/shard_map/ppermute | solution.py:306
  155.9 3.0 collective-permute-start.12
  166.8 6.1 %collective-permute-start.13 = (bf16[768,768]{1,0:T(8,128)(2,1)S(1)}, bf16[768,768]{1,0:T(8,128)(2,1)S(1)}, u32[]{:S(2)}, u32[]{:S(2)}) collective-permute-start(bf16[768,768]{1,0:T(8,128)(2,1)S(1)} %convolution_convert_fusion.3), channel_id=1, source_target_pairs={{0,1},{1,0},{2,3},{3,2},{4,5},{5,4},{6,7},{7,6},{8,9},{9,8},{10,11... | collective-permute-start | bytes 3538952 | tf_op jit(solution)/shard_map/ppermute | solution.py:306
  179.2 2.9 collective-permute-start.14
  184.4 118.5 %reduce-scatter.15.cloned.1.call-start = ((), (), s32[]{:S(2)}) async-start(), calls=%async_computation.10 | async-start | bytes 2949120 | tf_op jit(solution)/shard_map/reduce_scatter | solution.py:390
  192.5 123.4 %reduce-scatter.11.cloned.1.call-start = ((), (), s32[]{:S(2)}) async-start(), calls=%async_computation.8 | async-start | bytes 2949120 | tf_op jit(solution)/shard_map/reduce_scatter | solution.py:390
  203.5 2.7 collective-permute-start.16
  206.1 130.9 %reduce-scatter.19.cloned.1.call-start = ((), (), s32[]{:S(2)}) async-start(), calls=%async_computation.12 | async-start | bytes 184320
  211.2 51.8 %copy-start.21 = (bf16[1536,768]{1,0:T(8,128)(2,1)S(1)}, bf16[1536,768]{1,0:T(8,128)(2,1)}, u32[]{:S(2)}) copy-start(bf16[1536,768]{1,0:T(8,128)(2,1)} %copy-done.20) | copy-start | bytes 7077892
  268.7 13.5 %collective-permute-start.17 = (bf16[396,1152]{1,0:T(8,128)(2,1)S(1)}, bf16[396,1152]{1,0:T(8,128)(2,1)S(1)}, u32[]{:S(2)}, u32[]{:S(2)}) collective-permute-start(bf16[396,1152]{1,0:T(8,128)(2,1)S(1)} %pad_maximum_fusion.9), channel_id=1, source_target_pairs={{0,2},{1,5},{2,0},{3,7},{4,6},{5,1},{6,4},{7,3},{8,10},{9,13},{10,... | collective-permute-start | bytes 2737160 | tf_op jit(solution)/shard_map/ppermute | solution.py:294
  283.9 8.9 %collective-permute-start.18 = (bf16[204,1152]{1,0:T(8,128)(2,1)}, bf16[204,1152]{1,0:T(8,128)(2,1)S(1)}, u32[]{:S(2)}, u32[]{:S(2)}) collective-permute-start(bf16[204,1152]{1,0:T(8,128)(2,1)} %pad_maximum_fusion.12), channel_id=1, source_target_pairs={{0,4},{1,3},{2,6},{3,1},{4,0},{5,7},{6,2},{7,5},{8,12},{9,11},{10,... | collective-permute-start | bytes 1410056 | tf_op jit(solution)/shard_map/ppermute | solution.py:294
  285.0 79.8 %reduce-scatter.17.cloned.1.call-start = ((), (), s32[]{:S(2)}) async-start(), calls=%async_computation.11 | async-start | bytes 737280 | tf_op jit(solution)/shard_map/reduce_scatter | solution.py:391
  296.3 18.5 %collective-permute-start.19 = (bf16[108,1152]{1,0:T(8,128)(2,1)}, bf16[108,1152]{1,0:T(8,128)(2,1)S(1)}, u32[]{:S(2)}, u32[]{:S(2)}) collective-permute-start(bf16[108,1152]{1,0:T(8,128)(2,1)} %pad_maximum_fusion.14), channel_id=1, source_target_pairs={{0,16},{1,17},{2,18},{3,19},{4,20},{5,21},{6,22},{7,23},{8,24},{9,... | collective-permute-start | bytes 746504 | tf_op jit(solution)/shard_map/ppermute | solution.py:294
  302.8 13.0 %collective-permute-start.15 = (bf16[768,768]{1,0:T(8,128)(2,1)}, bf16[768,768]{1,0:T(8,128)(2,1)}, u32[]{:S(2)}, u32[]{:S(2)}) collective-permute-start(bf16[768,768]{1,0:T(8,128)(2,1)} %fusion.42), channel_id=1, source_target_pairs={{0,1},{1,0},{2,3},{3,2},{4,5},{5,4},{6,7},{7,6},{8,9},{9,8},{10,11... | collective-permute-start | bytes 3538952 | tf_op jit(solution)/shard_map/ppermute | solution.py:306
  302.9 90.1 %reduce-scatter.13.cloned.1.call-start = ((), (), s32[]{:S(2)}) async-start(), calls=%async_computation.9 | async-start | bytes 737280 | tf_op jit(solution)/shard_map/reduce_scatter | solution.py:391
  315.7 22.7 %collective-permute-start.20 = (bf16[60,1152]{1,0:T(8,128)(2,1)S(1)}, bf16[60,1152]{1,0:T(8,128)(2,1)S(1)}, u32[]{:S(2)}, u32[]{:S(2)}) collective-permute-start(bf16[60,1152]{1,0:T(8,128)(2,1)S(1)} %pad_maximum_fusion.16), channel_id=1, source_target_pairs={{0,8},{1,9},{2,10},{3,11},{4,12},{5,13},{6,14},{7,15},{8,0},{9,1},... | collective-permute-start | bytes 414728 | tf_op jit(solution)/shard_map/ppermute | solution.py:294
  315.9 22.5 %copy-start.24 = (f32[6,1152]{1,0:T(8,128)S(1)}, f32[6,1152]{1,0:T(8,128)}, u32[]{:S(2)}) copy-start(f32[6,1152]{1,0:T(8,128)} %copy-done.22) | copy-start | bytes 82948
  315.9 23.4 %copy-start.14 = (f32[96,1152]{1,0:T(8,128)S(1)}, f32[96,1152]{1,0:T(8,128)}, u32[]{:S(2)}) copy-start(f32[96,1152]{1,0:T(8,128)} %copy-done.13) | copy-start | bytes 1327108
  (46 other events, 202.0 us)
Sparse Core Ops, SparseCore 0:
  62.8 41.6 all-gather.1
  184.5 21.9 reduce-scatter.8
  208.8 46.3 reduce-scatter.14
  257.3 47.8 reduce-scatter.10
  307.8 29.1 reduce-scatter.18
  339.7 25.0 reduce-scatter.16
  367.9 25.0 reduce-scatter.12

commit v3 on v2

v3 whole, which is shorter than its diff:
```python
import functools

import jax
import jax.numpy as jnp
import numpy as np
from jax import lax
from jax.experimental import pallas as pl
from jax.experimental.pallas import tpu as pltpu
from jax.sharding import Mesh
from jax.sharding import PartitionSpec as P

BLK = 64


norm_eps = 1e-06
negative = -1e30


def norm_forward(values, gain, shift):
    centered = values - jnp.mean(values, axis=-1, keepdims=True)
    inverse = lax.rsqrt(jnp.mean(centered * centered, axis=-1, keepdims=True) + norm_eps)
    normed = centered * inverse
    return (normed * gain + shift, normed, inverse)


def norm_backward(grad, normed, inverse, gain):
    scaled = grad * gain
    mean_one = jnp.mean(scaled, axis=-1, keepdims=True)
    mean_two = jnp.mean(scaled * normed, axis=-1, keepdims=True)
    return inverse * (scaled - mean_one - normed * mean_two)


def dot_nt(a, b):
    return lax.dot_general(a, b, (((1,), (1,)), ((), ())), preferred_element_type=jnp.float32)


def dot_nn(a, b):
    return lax.dot_general(a, b, (((1,), (0,)), ((), ())), preferred_element_type=jnp.float32)


def dot_tn(a, b):
    return lax.dot_general(a, b, (((0,), (0,)), ((), ())), preferred_element_type=jnp.float32)


PAIR = 2 * BLK


def even_lanes(rows):
    return lax.broadcasted_iota(jnp.int32, (rows, PAIR), 1) < BLK


def stacked(values):
    zero = jnp.zeros_like(values)
    even = even_lanes(BLK)
    return jnp.concatenate([jnp.where(even, values, zero), jnp.where(even, zero, values)], axis=0)


def unstacked(values):
    return jnp.where(even_lanes(BLK), values[:BLK], values[BLK:])


class Layout:
    def __init__(self, len_ref, rb_ref, blocks, position):
        self.len_ref, self.rb_ref, self.blocks = len_ref, rb_ref, blocks
        self.half = blocks // 2
        self.rand = rb_ref.shape[-1]
        self.shift = position * self.half

    def moved(self, index):
        at = index + self.shift
        return jnp.where(at >= self.blocks, at - self.blocks, at)

    def spot(self, index):
        return pl.ds(pl.multiple_of(self.moved(index) * BLK, BLK), BLK)

    def part(self, index):
        return pl.ds(pl.multiple_of(self.moved(index) * BLK, BLK), self.half * BLK)

    def locate(self, b):
        count0 = self.len_ref[0, 0] // BLK
        count1 = self.len_ref[0, 1] // BLK
        in0 = b < count0
        self.live = live = b < count0 + count1
        self.first = first = jnp.where(in0, 0, jnp.where(live, count0, b))
        items = jnp.where(in0, count0, jnp.where(live, count1, 1))
        rel = b - first
        last = items - 1
        self.chunks = items // self.half
        self.is_global = live & ((rel == 0) | (rel == last))
        zero, neg = jnp.float32(0.0), jnp.float32(negative)
        item_bias = jnp.where(live, zero, neg)
        self.fixed = [
            first,
            first + last,
            b,
            jnp.where(live, b - 1, b),
            jnp.where(live, b + 1, b),
        ]
        self.bias = [
            item_bias,
            item_bias,
            zero,
            jnp.where(live & (rel > 1), zero, neg),
            jnp.where(live & (rel + 1 < last), zero, neg),
        ] + [item_bias] * self.rand
        self.b = b

    def chosen(self, head):
        return [
            jnp.where(self.live, self.first + self.rb_ref[0, head, self.b, k], self.b)
            for k in range(self.rand)
        ]


def gathered(ref, layout, column, picked):
    even = even_lanes(BLK)

    def rows(index):
        return ref[layout.spot(index), column : column + PAIR]

    return jnp.concatenate(
        [rows(i) for i in layout.fixed]
        + [jnp.where(even, rows(i), rows(j)) for i, j in zip(*picked)],
        axis=0,
    )


def attn_fwd_kernel(pairs, position, len_ref, rb_ref, tri_ref, out_ref):
    blocks = tri_ref.shape[0] // BLK
    scale = jnp.bfloat16(BLK**-0.5)
    layout = Layout(len_ref, rb_ref, blocks, position())

    def body(b, carry):
        layout.locate(b)
        here = layout.spot(b)

        def query_of(p):
            return stacked(tri_ref[here, p * 3 * PAIR : p * 3 * PAIR + PAIR]) * scale

        def put(p, mixed):
            out_ref[here, p * PAIR : (p + 1) * PAIR] = unstacked(mixed).astype(jnp.bfloat16)

        @pl.when(jnp.logical_not(layout.is_global))
        def sparse():
            lane = lax.broadcasted_iota(jnp.int32, (1, PAIR), 1) < BLK
            bias = layout.bias
            bias_row = jnp.concatenate(
                [jnp.where(lane, bias[2 * i], bias[2 * i + 1]) for i in range(len(bias) // 2)],
                axis=1,
            )
            for p in pairs:
                picked = [layout.chosen(2 * p), layout.chosen(2 * p + 1)]
                keys = gathered(tri_ref, layout, (3 * p + 1) * PAIR, picked)
                values = gathered(tri_ref, layout, (3 * p + 2) * PAIR, picked)
                scores = dot_nt(query_of(p), keys) + bias_row
                top = jnp.max(scores, axis=1, keepdims=True)
                expo = jnp.exp(scores - top)
                total = jnp.sum(expo, axis=1, keepdims=True)
                put(p, dot_nn(expo.astype(jnp.bfloat16), values) / total)

        @pl.when(layout.is_global)
        def dense():
            queries = [query_of(p) for p in pairs]

            def chunk(c, state):
                new = []
                at = layout.part(layout.first + c * layout.half)
                for query, p, (top, total, acc) in zip(queries, pairs, state):
                    keys = tri_ref[at, (3 * p + 1) * PAIR : (3 * p + 2) * PAIR]
                    values = tri_ref[at, (3 * p + 2) * PAIR : (3 * p + 3) * PAIR]
                    scores = dot_nt(query, keys)
                    higher = jnp.maximum(top, jnp.max(scores, axis=1, keepdims=True))
                    shrink = jnp.exp(top - higher)
                    expo = jnp.exp(scores - higher)
                    total = total * shrink + jnp.sum(expo, axis=1, keepdims=True)
                    acc = acc * shrink + dot_nn(expo.astype(jnp.bfloat16), values)
                    new.append((higher, total, acc))
                return tuple(new)

            column = jnp.zeros((PAIR, 1), jnp.float32)
            init = tuple(
                (column + negative, column, jnp.zeros((PAIR, PAIR), jnp.float32)) for _ in pairs
            )
            state = lax.fori_loop(0, layout.chunks, chunk, init)
            for p, (_, total, acc) in zip(pairs, state):
                put(p, acc / total)

        return carry

    lax.fori_loop(0, blocks, body, 0)


def attn_bwd_kernel(pairs, position, len_ref, rb_ref, tri_ref, grad_ref, out_ref, sum_ref, *accs):
    blocks = tri_ref.shape[0] // BLK
    scale = jnp.bfloat16(BLK**-0.5)
    back = BLK**-0.5
    layout = Layout(len_ref, rb_ref, blocks, position())
    count = len(pairs)
    key_acc, value_acc = accs[:count], accs[count:]
    for acc in accs:
        acc[...] = jnp.zeros_like(acc)

    def body(b, carry):
        layout.locate(b)
        here = layout.spot(b)

        def query_of(p):
            return stacked(tri_ref[here, p * 3 * PAIR : p * 3 * PAIR + PAIR]) * scale

        def grad_of(p):
            return stacked(grad_ref[here, p * PAIR : (p + 1) * PAIR])

        def put(i, grad_query):
            out_ref[here, i * 3 * PAIR : i * 3 * PAIR + PAIR] = unstacked(
                grad_query * back
            ).astype(jnp.bfloat16)

        @pl.when(jnp.logical_not(layout.is_global))
        def sparse():
            bias = layout.bias
            even = even_lanes(BLK)
            for i, p in enumerate(pairs):
                picked = [layout.chosen(2 * p), layout.chosen(2 * p + 1)]
                query, grad = query_of(p), grad_of(p)
                keys = gathered(tri_ref, layout, (3 * p + 1) * PAIR, picked)
                values = gathered(tri_ref, layout, (3 * p + 2) * PAIR, picked)
                scores = dot_nt(keys, query)
                scores = jnp.concatenate(
                    [scores[j * BLK : (j + 1) * BLK] + bias[j] for j in range(len(bias))], axis=0
                )
                top = jnp.max(scores, axis=0, keepdims=True)
                expo = jnp.exp(scores - top)
                probs = expo * (1.0 / jnp.sum(expo, axis=0, keepdims=True))
                grad_probs = dot_nt(values, grad)
                delta = jnp.sum(probs * grad_probs, axis=0, keepdims=True)
                grad_scores = (probs * (grad_probs - delta)).astype(jnp.bfloat16)
                put(i, dot_tn(grad_scores, keys))
                for acc, update in (
                    (key_acc[i], dot_nn(grad_scores, query)),
                    (value_acc[i], dot_nn(probs.astype(jnp.bfloat16), grad)),
                ):
                    pieces = [update[j * BLK : (j + 1) * BLK] for j in range(len(bias))]
                    for j, index in enumerate(layout.fixed):
                        acc[layout.spot(index), :] += pieces[j]
                    for j, (one, two) in enumerate(zip(*picked)):
                        piece = pieces[len(layout.fixed) + j]
                        zero = jnp.zeros_like(piece)
                        acc[layout.spot(one), :] += jnp.where(even, piece, zero)
                        acc[layout.spot(two), :] += jnp.where(even, zero, piece)

        @pl.when(layout.is_global)
        def dense():
            queries = [query_of(p) for p in pairs]
            grads = [grad_of(p) for p in pairs]

            def both(c, i, p):
                at = layout.part(layout.first + c * layout.half)
                keys = tri_ref[at, (3 * p + 1) * PAIR : (3 * p + 2) * PAIR]
                values = tri_ref[at, (3 * p + 2) * PAIR : (3 * p + 3) * PAIR]
                return at, keys, dot_nt(keys, queries[i]), dot_nt(values, grads[i])

            def first_pass(c, state):
                new = []
                for i, p in enumerate(pairs):
                    top, total, dot = state[i]
                    _, _, scores, grad_probs = both(c, i, p)
                    higher = jnp.maximum(top, jnp.max(scores, axis=0, keepdims=True))
                    shrink = jnp.exp(top - higher)
                    expo = jnp.exp(scores - higher)
                    total = total * shrink + jnp.sum(expo, axis=0, keepdims=True)
                    dot = dot * shrink + jnp.sum(expo * grad_probs, axis=0, keepdims=True)
                    new.append((higher, total, dot))
                return tuple(new)

            row = jnp.zeros((1, PAIR), jnp.float32)
            state = lax.fori_loop(
                0, layout.chunks, first_pass, tuple((row + negative, row, row) for _ in pairs)
            )

            def second_pass(c, grad_queries):
                new = []
                for i, p in enumerate(pairs):
                    top, total, dot = state[i]
                    inverse = 1.0 / total
                    at, keys, scores, grad_probs = both(c, i, p)
                    probs = jnp.exp(scores - top) * inverse
                    grad_scores = (probs * (grad_probs - dot * inverse)).astype(jnp.bfloat16)
                    new.append(grad_queries[i] + dot_tn(grad_scores, keys))
                    key_acc[i][at, :] += dot_nn(grad_scores, queries[i])
                    value_acc[i][at, :] += dot_nn(probs.astype(jnp.bfloat16), grads[i])
                return tuple(new)

            grad_queries = lax.fori_loop(
                0,
                layout.chunks,
                second_pass,
                tuple(jnp.zeros((PAIR, PAIR), jnp.float32) for _ in pairs),
            )
            for i, grad_query in enumerate(grad_queries):
                put(i, grad_query)

        return carry

    lax.fori_loop(0, blocks, body, 0)
    sum_ref[...] = jnp.zeros_like(sum_ref)
    for i in range(count):
        at = i * 3 * PAIR
        column = slice(i * PAIR, (i + 1) * PAIR)
        query_grads = out_ref[:, at : at + PAIR].astype(jnp.float32)
        sum_ref[0:1, column] = jnp.sum(query_grads, axis=0, keepdims=True)
        out_ref[:, at + PAIR : at + 2 * PAIR] = key_acc[i][...].astype(jnp.bfloat16)
        value = value_acc[i][...].astype(jnp.bfloat16)
        out_ref[:, at + 2 * PAIR : at + 3 * PAIR] = value
        sum_ref[1:2, column] = jnp.sum(value.astype(jnp.float32), axis=0, keepdims=True)


vmem = pl.BlockSpec(memory_space=pltpu.VMEM)
smem = pl.BlockSpec(memory_space=pltpu.SMEM)
VMEM_LIMIT = 60 << 20


def attention_forward(lengths, randoms, triple, position):
    pairs = randoms.shape[1] // 2
    rows = triple.shape[0]
    area = rows * rows // 3 * 2 * pairs
    return pl.pallas_call(
        functools.partial(attn_fwd_kernel, range(pairs), position),
        out_shape=jax.ShapeDtypeStruct((rows, pairs * PAIR), jnp.bfloat16),
        in_specs=[smem, smem, vmem],
        out_specs=vmem,
        name="attend_forward",
        cost_estimate=pl.CostEstimate(
            flops=16 * area * PAIR, transcendentals=area, bytes_accessed=rows * pairs * PAIR * 8
        ),
        compiler_params=pltpu.CompilerParams(vmem_limit_bytes=VMEM_LIMIT),
    )(lengths, randoms, triple)


def attention_backward(lengths, randoms, triple, grad, pairs, position):
    rows = triple.shape[0]
    count = len(pairs)
    area = rows * rows // 3 * 2 * count
    return pl.pallas_call(
        functools.partial(attn_bwd_kernel, pairs, position),
        out_shape=(
            jax.ShapeDtypeStruct((rows, count * 3 * PAIR), jnp.bfloat16),
            jax.ShapeDtypeStruct((8, count * PAIR), jnp.float32),
        ),
        in_specs=[smem, smem, vmem, vmem],
        out_specs=(vmem, vmem),
        name="attend_backward",
        scratch_shapes=[pltpu.VMEM((rows, PAIR), jnp.float32)] * (2 * count),
        cost_estimate=pl.CostEstimate(
            flops=40 * area * PAIR, transcendentals=area, bytes_accessed=rows * count * PAIR * 20
        ),
        compiler_params=pltpu.CompilerParams(vmem_limit_bytes=VMEM_LIMIT),
    )(lengths, randoms, triple, grad)


QUAD = 4


def group_permute(value, deep, target):
    pairs = []
    for z in range(deep):
        for q in range(QUAD):
            for h in range(2):
                to_z, to_q = target(z, q, h)
                pairs.append(((z * QUAD + q) * 2 + h, (to_z * QUAD + to_q) * 2 + h))
    return lax.ppermute(value, ("deep", "quad", "head"), pairs)


def deep_step(value, deep, bit):
    return group_permute(value, deep, lambda z, q, h: (z ^ bit, q))


def quad_step(value, deep, second):
    return group_permute(value, deep, lambda z, q, h: (z, q ^ ((2 >> h) if second else (1 << h))))


def swap(value):
    return lax.ppermute(value, "head", [(0, 1), (1, 0)])


def after(value, *others):
    return lax.optimization_barrier((value,) + others)[0]


class Spot:
    def __init__(self):
        self.z, self.q, self.h = (lax.axis_index(a) for a in ("deep", "quad", "head"))
        self.deep = lax.axis_size("deep")
        one, two = 1 << self.h, 2 >> self.h
        self.places = [self.q, self.q ^ one, self.q ^ two, self.q ^ 3]


def gather_deep(value, spot):
    direct = min(spot.deep, 4)
    blocks = [value] + [deep_step(value, spot.deep, k) for k in range(1, direct)]
    block = jnp.stack(blocks)
    bit = direct
    while bit < spot.deep:
        block = jnp.concatenate([block, deep_step(block, spot.deep, bit)])
        bit *= 2
    return block


def place_kernel(deep, windows, at_ref, *refs):
    pieces = refs[:3]
    outs = refs[3:]
    rows = pieces[0].shape[1]
    for k in range(deep):
        for j in range(QUAD):
            ref = pieces[j] if j < 2 else pieces[2].at[j - 2]
            row = pl.multiple_of(((at_ref[QUAD] ^ k) * QUAD + at_ref[j]) * rows, rows)
            for out, (low, high) in zip(outs, windows):
                out[pl.ds(row, rows), :] = ref[k, :, low:high]


def place(spot, pieces, widths):
    windows, low = [], 0
    for width in widths:
        windows.append((low, low + width))
        low += width
    deep, rows = pieces[0].shape[:2]
    at = jnp.stack(spot.places + [spot.z]).astype(jnp.int32)
    if rows % 16:
        order = jnp.stack([pieces[0], pieces[1], pieces[2][0], pieces[2][1]])
        full = jnp.zeros((deep, QUAD, rows, low), order.dtype)
        for k in range(deep):
            for j in range(QUAD):
                full = lax.dynamic_update_slice(
                    full, order[j, k][None, None], (spot.z ^ k, spot.places[j], 0, 0)
                )
        full = full.reshape(-1, low)
        return [full[:, a:b] for a, b in windows]
    return pl.pallas_call(
        functools.partial(place_kernel, deep, windows),
        out_shape=[
            jax.ShapeDtypeStruct((deep * QUAD * rows, width), pieces[0].dtype) for width in widths
        ],
        in_specs=[smem] + [vmem] * 3,
        out_specs=[vmem] * len(widths),
        compiler_params=pltpu.CompilerParams(vmem_limit_bytes=VMEM_LIMIT),
        name="place_pieces",
    )(at, *pieces)


def slabs(total, spot, places):
    rows = total.shape[0] // (spot.deep * QUAD)
    columns = total.shape[1]
    cube = total.reshape(spot.deep, QUAD, rows, columns)
    return [
        lax.dynamic_slice(cube, (0, p, 0, 0), (spot.deep, 1, rows, columns)).reshape(
            spot.deep * rows, columns
        )
        for p in places
    ]


def first_send(totals, spot):
    parts = [slabs(t, spot, [spot.places[1], spot.places[3]]) for t in totals]
    return jnp.concatenate([jnp.concatenate(p, axis=0) for p in parts], axis=1)


def second_send(totals, spot, got):
    rows = got.shape[0] // 2
    far = jnp.concatenate([slabs(t, spot, [spot.places[2]])[0] for t in totals], axis=1)
    return low(far.astype(jnp.float32) + got[rows:].astype(jnp.float32))


def quad_sum(totals, spot, got, got_two):
    rows = got_two.shape[0]
    own = jnp.concatenate([slabs(t, spot, [spot.places[0]])[0] for t in totals], axis=1)
    return (
        own.astype(jnp.float32) + got[:rows].astype(jnp.float32) + got_two.astype(jnp.float32)
    )


def deep_sends(total, spot, small=None):
    bit = spot.deep // 2
    rows = total.shape[0] // spot.deep
    while bit >= 4:
        span = bit * rows
        own = jnp.where((spot.z & bit) == 0, 0, span)
        send = low(lax.dynamic_slice_in_dim(total, span - own, span, 0))
        if small is not None:
            send = jnp.concatenate([send, pack_small(small)], axis=0)
        got = deep_step(send, spot.deep, bit)
        if small is not None:
            small = small + unpack_small(got[span:])
        total = lax.dynamic_slice_in_dim(total, own, span, 0) + got[:span].astype(jnp.float32)
        bit //= 2
    direct = min(spot.deep, 4)
    place = spot.z % direct

    def piece(k):
        return lax.dynamic_slice_in_dim(total, (place ^ k) * rows, rows, 0)

    packed = [] if small is None else [pack_small(small)]
    messages = [
        jnp.concatenate([low(piece(k))] + packed, axis=0) for k in range(1, direct)
    ]
    return piece(0), small, messages


def deep_finish(own, small, answers):
    rows = own.shape[0]
    for answer in answers:
        own = own + answer[:rows].astype(jnp.float32)
        if small is not None:
            small = small + unpack_small(answer[rows:])
    return own, small


def pack_small(small):
    high = lax.reduce_precision(small, 8, 7)
    return jnp.concatenate([high, small - high]).astype(jnp.bfloat16)


def unpack_small(packed):
    rows = packed.shape[0] // 2
    return packed[:rows].astype(jnp.float32) + packed[rows:].astype(jnp.float32)


def mm(left, right):
    return jnp.einsum("td,df->tf", left, right, preferred_element_type=jnp.float32)


def mm_nt(left, right):
    return jnp.einsum("tf,df->td", left, right, preferred_element_type=jnp.float32)


def mm_tn(left, right):
    return jnp.einsum("td,tf->df", left, right, preferred_element_type=jnp.float32)


def low(value):
    return value.astype(jnp.bfloat16)


def by_pair(value):
    lead, kinds, columns = value.shape[:-2], value.shape[-2], value.shape[-1]
    split = value.reshape(lead + (kinds, columns // PAIR, PAIR))
    return jnp.swapaxes(split, -3, -2).reshape(lead + (kinds * columns,))


def by_kind(value, kinds):
    lead, columns = value.shape[:-1], value.shape[-1]
    split = value.reshape(lead + (columns // (kinds * PAIR), kinds, PAIR))
    return jnp.swapaxes(split, -3, -2).reshape(lead + (kinds, columns // kinds))


def on_device(
    inputs,
    qkv_weight,
    qv_bias,
    out_weight,
    out_bias,
    first_gain,
    first_shift,
    up_weight,
    up_bias,
    down_weight,
    down_bias,
    second_gain,
    second_shift,
    item_lengths,
    random_blocks,
    out_grad,
):
    half, width = inputs.shape
    spot = Spot()
    deep = spot.deep
    shard = qkv_weight.shape[0]
    head_width = qkv_weight.shape[2]
    up_width = up_weight.shape[1]
    pair_count = head_width // PAIR

    def position():
        return lax.axis_index("head")

    qkv_deep = gather_deep(by_pair(qkv_weight), spot)
    tokens = jnp.concatenate([inputs, swap(inputs)], axis=0)
    mid = jnp.concatenate([out_weight, up_weight], axis=1)

    def first_quad(block):
        return quad_step(block, deep, False)

    def second_quad(block, other):
        return quad_step(jnp.stack([block, other]), deep, True)

    mid, qkv_deep = lax.optimization_barrier((mid, qkv_deep))
    qkv_other = first_quad(qkv_deep)
    mid_deep = gather_deep(mid, spot)
    qkv_far = second_quad(qkv_deep, qkv_other)
    (full_qkv,) = place(spot, (qkv_deep, qkv_other, qkv_far), [3 * head_width])
    mid_deep, full_qkv = lax.optimization_barrier((mid_deep, full_qkv))
    mid_other = first_quad(mid_deep)
    down_deep = gather_deep(after(down_weight, mid_deep), spot)

    bias = by_pair(jnp.stack([qv_bias[0], jnp.zeros_like(qv_bias[0]), qv_bias[1]]))
    triple = low(mm(tokens, full_qkv) + bias)
    triple, mid_other, down_deep = lax.optimization_barrier((triple, mid_other, down_deep))
    mid_far = second_quad(mid_deep, mid_other)
    down_other = first_quad(down_deep)
    attended = attention_forward(item_lengths, random_blocks, triple, position)
    attended, mid_far, down_other = lax.optimization_barrier((attended, mid_far, down_other))
    down_far = second_quad(down_deep, down_other)
    full_out, full_up = place(spot, (mid_deep, mid_other, mid_far), [head_width, up_width])

    other = swap(low(mm_nt(attended[half:], full_out)))
    proj = mm_nt(attended[:half], full_out) + other.astype(jnp.float32)
    normed_one_out, normed_one, inverse_one = norm_forward(
        proj + out_bias + inputs.astype(jnp.float32), first_gain, first_shift
    )
    hidden_own = low(normed_one_out)
    hidden_other = swap(hidden_own)
    hidden = jnp.concatenate([hidden_own, hidden_other], axis=0)

    def gelu_tanh(values):
        return jax.nn.gelu(values, approximate=True)

    upper_own = low(mm(hidden_own, full_up) + up_bias)
    upper_other = low(mm(hidden_other, full_up) + up_bias)
    active_other = low(gelu_tanh(upper_other.astype(jnp.float32)))
    active_own = low(gelu_tanh(upper_own.astype(jnp.float32)))
    active_other, active_own, down_far = lax.optimization_barrier(
        (active_other, active_own, down_far)
    )
    (full_down,) = place(spot, (down_deep, down_other, down_far), [up_width])
    other = swap(low(mm_nt(active_other, full_down)))
    down = mm_nt(active_own, full_down) + other.astype(jnp.float32)
    active = jnp.concatenate([active_own, active_other], axis=0)
    normed_two_out, normed_two, inverse_two = norm_forward(
        down + down_bias + normed_one_out, second_gain, second_shift
    )
    row = spot.h * half + lax.broadcasted_iota(jnp.int32, (half, 1), 0)
    live = (row < jnp.sum(item_lengths)).astype(jnp.float32)
    layer_out = low(normed_two_out * live)
    cotangent = out_grad.astype(jnp.float32) * live
    second_gain_part = jnp.sum(cotangent * normed_two, axis=0)
    second_shift_part = jnp.sum(cotangent, axis=0)
    grad_res_two = norm_backward(cotangent, normed_two, inverse_two, second_gain)
    down_bias_part = jnp.sum(grad_res_two, axis=0)
    grad_own = low(grad_res_two)
    grad_other = swap(grad_own)
    grad_down_rows = jnp.concatenate([grad_own, grad_other], axis=0)

    down_local = low(mm_tn(grad_down_rows, active))
    down_got = first_quad(first_send([down_local], spot))

    def pull(grad_rows, upper_rows):
        grad_active = mm(grad_rows, full_down)
        return low(jax.vjp(gelu_tanh, upper_rows.astype(jnp.float32))[1](grad_active)[0])

    grad_other, grad_own, down_local = lax.optimization_barrier((grad_other, grad_own, down_local))
    grad_upper_other = pull(grad_other, upper_other)
    grad_upper_own = pull(grad_own, upper_own)
    grad_upper = jnp.concatenate([grad_upper_own, grad_upper_other], axis=0)
    up_bias_part = jnp.sum(grad_upper.astype(jnp.float32), axis=0)
    other = swap(low(mm_nt(grad_upper_other, full_up)))
    grad_norm_one = mm_nt(grad_upper_own, full_up) + other.astype(jnp.float32) + grad_res_two
    up_local = low(mm_tn(hidden, grad_upper))
    first_gain_part = jnp.sum(grad_norm_one * normed_one, axis=0)
    first_shift_part = jnp.sum(grad_norm_one, axis=0)
    grad_res_one = norm_backward(grad_norm_one, normed_one, inverse_one, first_gain)
    out_bias_part = jnp.sum(grad_res_one, axis=0)
    grad_proj_own = low(grad_res_one)
    grad_proj = jnp.concatenate([grad_proj_own, swap(grad_proj_own)], axis=0)
    grad_attended = low(mm(grad_proj, full_out))
    out_local = low(mm_tn(grad_proj, attended))

    mids = [out_local, up_local]
    grad_attended, down_got = lax.optimization_barrier((grad_attended, down_got))
    mid_got = first_quad(first_send(mids, spot))
    down_two = quad_step(second_send([down_local], spot, down_got), deep, True)
    shared = jnp.stack(
        [
            out_bias_part,
            first_gain_part,
            first_shift_part,
            down_bias_part,
            second_gain_part,
            second_shift_part,
        ]
    )
    shared = shared + swap(shared)

    split = pair_count - 1
    grads_a, sums_a = attention_backward(
        item_lengths, random_blocks, triple, grad_attended, range(split), position
    )
    grads_a, mid_got, down_two, grad_attended = lax.optimization_barrier(
        (grads_a, mid_got, down_two, grad_attended)
    )
    local_a = low(mm_tn(tokens, grads_a))
    got_a = first_quad(first_send([local_a], spot))
    mid_two = quad_step(second_send(mids, spot, mid_got), deep, True)
    down_own, _, messages = deep_sends(quad_sum([down_local], spot, down_got, down_two), spot)
    down_answers = [deep_step(m, deep, k + 1) for k, m in enumerate(messages)]
    grad_attended, local_a = lax.optimization_barrier((grad_attended, local_a))
    grads_b, sums_b = attention_backward(
        item_lengths, random_blocks, triple, grad_attended, range(split, pair_count), position
    )
    grads_b, got_a, mid_two, *down_answers = lax.optimization_barrier(
        (grads_b, got_a, mid_two, *down_answers)
    )

    def carry(send, small, step):
        message = jnp.concatenate([send, pack_small(small)], axis=0)
        answer = step(message)
        return answer[: send.shape[0]], small + unpack_small(answer[send.shape[0] :])

    sums = jnp.concatenate([sums_a[:2], sums_b[:2]], axis=1)
    small = jnp.concatenate([shared.reshape(-1), up_bias_part, sums.reshape(-1)])
    small = small.reshape(-1, 3 * PAIR)
    local_b = low(mm_tn(tokens, grads_b))
    got_b, small = carry(first_send([local_b], spot), small, first_quad)
    two_a = quad_step(second_send([local_a], spot, got_a), deep, True)
    mid_sum = after(quad_sum(mids, spot, mid_got, mid_two), local_b)
    mid_own, _, messages = deep_sends(mid_sum, spot)
    mid_answers = [deep_step(m, deep, k + 1) for k, m in enumerate(messages)]

    cut = split * 3 * PAIR
    grads_a, grads_b, local_b = lax.optimization_barrier((grads_a, grads_b, local_b))
    other = swap(
        low(mm_nt(grads_a[half:], full_qkv[:, :cut]) + mm_nt(grads_b[half:], full_qkv[:, cut:]))
    )
    mine = mm_nt(grads_a[:half], full_qkv[:, :cut]) + mm_nt(grads_b[:half], full_qkv[:, cut:])
    mine, other, got_b, two_a = lax.optimization_barrier((mine, other, got_b, two_a))
    two_b, small = carry(
        second_send([local_b], spot, got_b), small, lambda m: quad_step(m, deep, True)
    )
    input_grad = low(mine + other.astype(jnp.float32) + grad_res_one)
    sum_a = quad_sum([local_a], spot, got_a, two_a)
    grad_down, _ = deep_finish(down_own, None, down_answers)
    input_grad, sum_a, grad_down, two_b = lax.optimization_barrier(
        (input_grad, sum_a, grad_down, two_b)
    )
    qkv_sum = jnp.concatenate([sum_a, quad_sum([local_b], spot, got_b, two_b)], axis=1)
    small = small.reshape(-1, 3 * head_width)
    qkv_own, small, messages = deep_sends(qkv_sum, spot, small)
    answers = [deep_step(m, deep, k + 1) for k, m in enumerate(messages)]
    grad_mid, _ = deep_finish(mid_own, None, mid_answers)
    grad_mid, *answers = lax.optimization_barrier((grad_mid, *answers))
    grad_qkv, small = deep_finish(qkv_own, small, answers)
    grad_out, grad_up = grad_mid[:, :head_width], grad_mid[:, head_width:]

    small = small.reshape(-1)
    count = shared.size
    totals = small[:count].reshape(shared.shape)
    grad_up_bias = small[count : count + up_width]
    grad_qv_bias = small[count + up_width :].reshape(2, head_width)
    return (
        layer_out,
        input_grad,
        by_kind(grad_qkv, 3),
        grad_qv_bias,
        grad_out,
        totals[0],
        totals[1],
        totals[2],
        grad_up,
        grad_up_bias,
        grad_down,
        totals[3],
        totals[4],
        totals[5],
    )


def solution(mesh):
    devices = mesh.devices.reshape(-1, QUAD, mesh.shape["head"])
    fine = Mesh(devices, ("deep", "quad", "head"))
    rows = ("deep", "quad", "head")
    dp = ("deep", "quad")
    in_specs = (
        P(rows, None),
        P(dp, None, "head"),
        P(None, "head"),
        P(dp, "head"),
        P(),
        P(),
        P(),
        P(dp, "head"),
        P("head"),
        P(dp, "head"),
        P(),
        P(),
        P(),
        P(dp, None),
        P(dp, "head", None, None),
        P(rows, None),
    )
    out_specs = (
        P(rows, None),
        P(rows, None),
        P(dp, None, "head"),
        P(None, "head"),
        P(dp, "head"),
        P(),
        P(),
        P(),
        P(dp, "head"),
        P("head"),
        P(dp, "head"),
        P(),
        P(),
        P(),
    )
    return jax.shard_map(
        on_device, mesh=fine, in_specs=in_specs, out_specs=out_specs, check_vma=False
    )
```

time: 405 us -> 340 us (0.84)
  waiting for transfers between devices: 161 us -> 52.2 us
  starting transfers between devices: 20.4 us -> 47.4 us
  Pallas kernels: 78.6 us -> 96 us
  between operations: 15.3 us -> 2.05 us
  other arithmetic: 25.6 us -> 31.7 us
    reduce_scatter x5 -> x0, waiting for transfers between devices: 49.5 us -> none  [the longest x2 49.4 us: scatter_offload(): lax.psum_scatter(part, 'quad', scatter_dimension=0, tiled=True)]
    ppermute x12 -> x32, waiting for transfers between devices: 87.5 us -> 47.4 us  [group_permute(): return lax.ppermute(value, ('deep', 'quad', 'head'), pairs)]
    ppermute x12 -> x32, starting transfers between devices: 18.5 us -> 45.9 us  [group_permute(): return lax.ppermute(value, ('deep', 'quad', 'head'), pairs)]
    pallas_call x2 -> x6, Pallas kernels: 78.6 us -> 96 us  [the longest x2 59.3 us: attention_backward(): pl.pallas_call(functools.partial(attn_bwd_kernel, pairs, position), out_s...]
    unnamed x8 -> x0, waiting for transfers between devices: 16.1 us -> none
    convert_element_type x3 -> x9, other arithmetic: 0.66 us -> 7.48 us  [low(): return value.astype(jnp.bfloat16)]
    add x4 -> x9, other arithmetic: 2.11 us -> 7.21 us  [the longest x4 4.11 us: quad_sum(): own.astype(jnp.float32) + got[:rows].astype(jnp.float32)]
    convert_element_type x6 -> x1, other arithmetic: 5.56 us -> 0.65 us  [on_device(): live = (row < jnp.sum(item_lengths)).astype(jnp.float32)]
  transfers between devices with their start and end apart: 28 -> 41, of which waited for: 16 -> 13; matrix products, arithmetic and copies ran while one was open for 20% -> 22% of each run, Pallas kernels for 20% -> 26%
where the time goes in v3:
time: 340 us; the launch traced here: 334 us
  Pallas kernels  96 us (28%)
  matrix products  76.9 us (23%)
  waiting for transfers between devices  52.2 us (15%)
  starting transfers between devices  47.4 us (14%)
  other arithmetic  31.7 us (9%)
  local copies, waits for them, and re-layouts  27.9 us (8%)
    pallas_call x2, Pallas kernels, attention_backward(): pl.pallas_call(functools.partial(attn_bwd_kernel, pairs, position), out_s...  59.3 us
    ppermute x32, waiting for transfers between devices, group_permute(): return lax.ppermute(value, ('deep', 'quad', 'head'), pairs)  47.4 us
    ppermute x32, starting transfers between devices, group_permute(): return lax.ppermute(value, ('deep', 'quad', 'head'), pairs)  45.9 us
    dot_general x6, matrix products, mm(): jnp.einsum('td,df->tf', left, right, preferred_element_type=jnp.float32)  31.7 us
    pallas_call x1, Pallas kernels, attention_forward(): pl.pallas_call(functools.partial(attn_fwd_kernel, range(pairs), position)...  26.9 us
    dot_general x10, matrix products, mm_nt(): jnp.einsum('tf,df->td', left, right, preferred_element_type=jnp.float32)  23.5 us
    dot_general x5, matrix products, mm_tn(): jnp.einsum('td,tf->df', left, right, preferred_element_type=jnp.float32)  21.7 us
    unnamed x116, local copies, waits for them, and re-layouts  9.9 us
  transfers between devices with their start and end apart: 41, of which 13 were waited for; matrix products, arithmetic and copies ran while one was open for 22% of the time, Pallas kernels for 26%

profile of v3, /device:TPU:0, one launch (start us, length us, event | category | flops | bytes accessed | tf_op | source)
XLA Modules:
  0.0 334.1 jit_solution(16934237318159118188)
XLA Ops:
  1.9 5.1 %collective-permute-start.3 = (bf16[48,1152]{1,0:T(8,128)(2,1)S(1)}, bf16[48,1152]{1,0:T(8,128)(2,1)S(1)}, u32[]{:S(2)}, u32[]{:S(2)}) collective-permute-start(bf16[48,1152]{1,0:T(8,128)(2,1)S(1)} %reshape.215), channel_id=1, source_target_pairs={{0,24},{1,25},{2,26},{3,27},{4,28},{5,29},{6,30},{7,31},{8,16},{9,... | collective-permute-start | bytes 331784 | tf_op jit(solution)/shard_map/ppermute | solution.py:370
  11.0 5.3 %collective-permute-done.2 = bf16[48,1152]{1,0:T(8,128)(2,1)S(1)} collective-permute-done((bf16[48,1152]{1,0:T(8,128)(2,1)S(1)}, bf16[48,1152]{1,0:T(8,128)(2,1)S(1)}, u32[]{:S(2)}, u32[]{:S(2)}) %collective-permute-start.2) | collective-permute-done | bytes 110624 | tf_op jit(solution)/shard_map/ppermute | solution.py:370
  18.1 6.7 %collective-permute-done.7.refs_1_ = bf16[4,48,1152]{2,1,0:T(8,128)(2,1)S(1)} collective-permute-done((bf16[4,48,1152]{2,1,0:T(8,128)(2,1)S(1)}, bf16[4,48,1152]{2,1,0:T(8,128)(2,1)S(1)}, u32[]{:S(2)}, u32[]{:S(2)}) %collective-permute-start.7) | collective-permute-done | bytes 442400 | tf_op jit(solution)/shard_map/ppermute | solution.py:370
  33.6 3.2 collective-permute-done.6
  36.8 6.8 %collective-permute-done.5 = bf16[48,1920]{1,0:T(8,128)(2,1)S(1)} collective-permute-done((bf16[48,1920]{1,0:T(8,128)(2,1)S(1)}, bf16[48,1920]{1,0:T(8,128)(2,1)S(1)}, u32[]{:S(2)}, u32[]{:S(2)}) %collective-permute-start.5) | collective-permute-done | bytes 184352 | tf_op jit(solution)/shard_map/ppermute | solution.py:370
  46.4 2.8 place_pieces.3
  54.2 7.2 %fusion.tri_ref = bf16[1536,1152]{1,0:T(8,128)(2,1)} fusion(bf16[1536,768]{1,0:T(8,128)(2,1)} %constant_dynamic-update-slice_fusion, bf16[768,1152]{1,0:T(8,128)(2,1)} %place_pieces.3, f32[1152]{0:T(1024)S(1)} %add.281), kind=kOutput, calls=%fused_computation.12 | convolution fusion | flops 2721447936 | bytes 7672320 | tf_op jit(solution)/shard_map/td,df->tf/dot_general | solution.py:527
  69.3 26.9 %attend_forward.1 = bf16[1536,384]{1,0:T(8,128)(2,1)} custom-call(s32[1,2]{1,0:T(1,128)} %len_ref.5, s32[1,6,24,3]{3,2,1,0:T(8,128)} %copy.38.rb_ref, bf16[1536,1152]{1,0:T(8,128)(2,1)} %fusion.tri_ref), custom_call_target="tpu_custom_call" | custom-call | flops 9663676416 | bytes 4718592 | tf_op jit(solution)/shard_map/attend_forward/pallas_call | solution.py:326
  97.4 3.7 %place_pieces.4 = (bf16[768,384]{1,0:T(8,128)(2,1)}, bf16[768,1536]{1,0:T(8,128)(2,1)}) custom-call(s32[5]{0:T(128)} %stack.137.at_ref, bf16[4,48,1920]{2,1,0:T(8,128)(2,1)} %copy-done.4, bf16[4,48,1920]{2,1,0:T(8,128)(2,1)} %copy-done.10, bf16[2,4,48,1920]{3,2,1,0:T(8,128)(2,1)} %copy-done.25), custom_call_target="tpu_custom_call" | custom-call | tf_op jit(solution)/shard_map/place_pieces/pallas_call | solution.py:437
  103.2 2.8 collective-permute-done.15
  111.1 5.2 %fusion.18 = (bf16[768,1536]{1,0:T(8,128)(2,1)}, bf16[768,1536]{1,0:T(8,128)(2,1)}) fusion(f32[1536]{0:T(1024)S(1)} %copy-done.50, bf16[768,768]{1,0:T(8,128)(2,1)S(1)} %fusion.37, bf16[768,1536]{1,0:T(8,128)(2,1)S(1)} %copy-done.46), kind=kOutput, calls=%fused_computation.30 | convolution fusion | flops 1826095104 | bytes 8263680 | tf_op jit(solution)/shard_map/td,df->tf/dot_general | solution.py:527
  116.3 5.0 %fusion.12 = (bf16[768,1536]{1,0:T(8,128)(2,1)}, bf16[768,1536]{1,0:T(8,128)(2,1)}) fusion(f32[1536]{0:T(1024)S(1)} %copy-done.50, bf16[768,768]{1,0:T(8,128)(2,1)S(1)} %collective-permute-done.16, bf16[768,1536]{1,0:T(8,128)(2,1)S(1)} %copy-done.46), kind=kOutput, calls=%fused_computation.24 | convolution fusion | flops 1826095104 | bytes 8263680 | tf_op jit(solution)/shard_map/td,df->tf/dot_general | solution.py:527
  121.3 4.7 %collective-permute-done.17.refs_2_ = bf16[2,4,48,1536]{3,2,1,0:T(8,128)(2,1)S(1)} collective-permute-done((bf16[2,4,48,1536]{3,2,1,0:T(8,128)(2,1)S(1)}, bf16[2,4,48,1536]{3,2,1,0:T(8,128)(2,1)S(1)}, u32[]{:S(2)}, u32[]{:S(2)}) %collective-permute-start.17) | collective-permute-done | bytes 1179680 | tf_op jit(solution)/shard_map/ppermute | solution.py:370
  127.1 3.2 place_pieces.5
  130.2 5.4 %convolution_convert_fusion.5 = bf16[768,768]{1,0:T(8,128)(2,1)} fusion(bf16[768,1536]{1,0:T(8,128)(2,1)} %get-tuple-element.82, bf16[768,1536]{1,0:T(8,128)(2,1)} %place_pieces.5), kind=kOutput, calls=%fused_computation.81 | convolution fusion | flops 1812529152 | bytes 5898240 | tf_op jit(solution)/shard_map/tf,df->td/dot_general | solution.py:531
  138.9 5.0 %fusion.80 = (f32[768]{0:T(1024)S(1)}, f32[768,768]{1,0:T(8,128)S(1)}) fusion(f32[768]{0:T(1024)S(1)} %copy-done.43, f32[768]{0:T(1024)S(1)} %copy-done.36, f32[768]{0:T(1024)S(1)} %add_rsqrt_fusion.1, f32[768,768]{1,0:T(8,128)S(1)} %get-tuple-element.181, f32[768]{0:T(1024)S(1)} %broadcast_multiply_fusion.5, f32[768]{0:T(1024)S(1)} %copy-done.51, ...), kind=kOutput, calls=%fused_computation.212 | convolution fusion | flops 1817246976 | bytes 10635264 | tf_op jit(solution)/shard_map/tf,df->td/dot_general | solution.py:531
  154.4 6.7 %fusion.25 = bf16[768,1536]{1,0:T(8,128)(2,1)S(1)} fusion(bf16[768,1536]{1,0:T(8,128)(2,1)} %get-tuple-element.82, bf16[768,1536]{1,0:T(8,128)(2,1)} %get-tuple-element.80, bf16[768,768]{1,0:T(8,128)(2,1)} %collective-permute-done.19, bf16[768,768]{1,0:T(8,128)(2,1)S(1)} %convert_element_type.296), kind=kOutput, calls=%fused_computation.40 | convolution fusion | flops 3639214080 | bytes 9437184 | tf_op jit(solution)/shard_map/td,tf->df/dot_general | solution.py:535
  161.2 5.8 %fusion.8 = bf16[768,1536]{1,0:T(8,128)(2,1)S(1)} fusion(bf16[768,1536]{1,0:T(8,128)(2,1)S(1)} %copy-done.56, bf16[768,768]{1,0:T(8,128)(2,1)} %collective-permute-done.19, bf16[768,1536]{1,0:T(8,128)(2,1)S(1)} %copy-done.12), kind=kOutput, calls=%fused_computation.20 | convolution fusion | flops 1836711936 | bytes 8257536 | tf_op jit(solution)/shard_map/td,df->tf/dot_general | solution.py:527
  172.9 4.4 %fusion.5 = bf16[768,1536]{1,0:T(8,128)(2,1)S(1)} fusion(bf16[768,1536]{1,0:T(8,128)(2,1)S(1)} %copy-done.55, bf16[768,768]{1,0:T(8,128)(2,1)S(1)} %convert_element_type.296, bf16[768,1536]{1,0:T(8,128)(2,1)S(1)} %copy-done.12), kind=kOutput, calls=%fused_computation.17 | convolution fusion | flops 1836711936 | bytes 8257536 | tf_op jit(solution)/shard_map/td,df->tf/dot_general | solution.py:527
  177.3 2.9 multiply_reduce_fusion.1
  183.9 4.2 %convolution_convert_fusion = bf16[768,1536]{1,0:T(8,128)(2,1)S(1)} fusion(bf16[768,1536]{1,0:T(8,128)(2,1)S(1)} %fusion.8, bf16[768,1536]{1,0:T(8,128)(2,1)S(1)} %fusion.5, bf16[768,768]{1,0:T(8,128)(2,1)S(1)} %copy-done.49, bf16[768,768]{1,0:T(8,128)(2,1)S(1)} %copy-done.28), kind=kOutput, calls=%fused_computation.41 | convolution fusion | flops 3639214080 | bytes 9437184 | tf_op jit(solution)/shard_map/td,tf->df/dot_general | solution.py:535
  194.0 3.4 %fusion.39 = bf16[768,384]{1,0:T(8,128)(2,1)S(1)} fusion(bf16[1536,384]{1,0:T(8,128)(2,1)} %attend_forward.1, bf16[768,768]{1,0:T(8,128)(2,1)} %collective-permute-done.21, bf16[768,768]{1,0:T(8,128)(2,1)} %convert_element_type.302), kind=kOutput, calls=%fused_computation.88 | convolution fusion | flops 910983168 | bytes 4128768 | tf_op jit(solution)/shard_map/td,tf->df/dot_general | solution.py:535
  197.6 4.2 %convolution_convert_fusion.1.grad_ref = bf16[1536,384]{1,0:T(8,128)(2,1)} fusion(bf16[768,384]{1,0:T(8,128)(2,1)S(1)} %copy-done.31, bf16[768,768]{1,0:T(8,128)(2,1)} %collective-permute-done.21, bf16[768,768]{1,0:T(8,128)(2,1)} %convert_element_type.302), kind=kOutput, calls=%fused_computation.42 | convolution fusion | flops 911278080 | bytes 4128768 | tf_op jit(solution)/shard_map/td,df->tf/dot_general | solution.py:527
  206.9 36.6 %attend_backward.2 = (bf16[1536,768]{1,0:T(8,128)(2,1)}, f32[8,256]{1,0:T(8,128)}) custom-call(s32[1,2]{1,0:T(1,128)} %len_ref.5, s32[1,6,24,3]{3,2,1,0:T(8,128)} %copy.38.rb_ref, bf16[1536,1152]{1,0:T(8,128)(2,1)} %fusion.tri_ref, bf16[1536,384]{1,0:T(8,128)(2,1)} %convolution_convert_fusion.1.grad_ref), custom_call_target="tpu_custom_call" | custom-call | flops 16106127360 | bytes 7864320 | tf_op jit(solution)/shard_map/attend_backward/pallas_call | solution.py:343
  247.8 3.7 %collective-permute-start.29 = (bf16[48,1536]{1,0:T(8,128)(2,1)}, bf16[48,1536]{1,0:T(8,128)(2,1)}, u32[]{:S(2)}, u32[]{:S(2)}) collective-permute-start(bf16[48,1536]{1,0:T(8,128)(2,1)} %get-tuple-element.153), channel_id=1, source_target_pairs={{0,24},{1,25},{2,26},{3,27},{4,28},{5,29},{6,30},{7,31},{8,16},{9,... | collective-permute-start | bytes 442376 | tf_op jit(solution)/shard_map/ppermute | solution.py:370
  255.0 3.7 %convolution_convert_fusion.3 = bf16[768,768]{1,0:T(8,128)(2,1)S(1)} fusion(bf16[1536,768]{1,0:T(8,128)(2,1)} %constant_dynamic-update-slice_fusion, bf16[1536,768]{1,0:T(8,128)(2,1)S(1)} %copy-done.53), kind=kOutput, calls=%fused_computation.79 | convolution fusion | flops 1812529152 | bytes 5898240 | tf_op jit(solution)/shard_map/td,tf->df/dot_general | solution.py:535
  261.8 22.7 %attend_backward.3 = (bf16[1536,384]{1,0:T(8,128)(2,1)}, f32[8,128]{1,0:T(8,128)}) custom-call(s32[1,2]{1,0:T(1,128)} %len_ref.5, s32[1,6,24,3]{3,2,1,0:T(8,128)} %copy.38.rb_ref, bf16[1536,1152]{1,0:T(8,128)(2,1)} %fusion.tri_ref, bf16[1536,384]{1,0:T(8,128)(2,1)} %convolution_convert_fusion.1.grad_ref), custom_call_target="tpu_custom_call" | custom-call | flops 8053063680 | bytes 3932160 | tf_op jit(solution)/shard_map/attend_backward/pallas_call | solution.py:343
  285.4 3.5 %convolution_convert_fusion.6 = bf16[768,384]{1,0:T(8,128)(2,1)S(1)} fusion(bf16[1536,768]{1,0:T(8,128)(2,1)} %constant_dynamic-update-slice_fusion, bf16[1536,384]{1,0:T(8,128)(2,1)} %get-tuple-element.97), kind=kOutput, calls=%fused_computation.87 | convolution fusion | flops 906264576 | bytes 4128768 | tf_op jit(solution)/shard_map/td,tf->df/dot_general | solution.py:535
  297.0 3.7 %collective-permute-start.37 = (bf16[48,1920]{1,0:T(8,128)(2,1)}, bf16[48,1920]{1,0:T(8,128)(2,1)}, u32[]{:S(2)}, u32[]{:S(2)}) collective-permute-start(bf16[48,1920]{1,0:T(8,128)(2,1)} %get-tuple-element.149), channel_id=1, source_target_pairs={{0,24},{1,25},{2,26},{3,27},{4,28},{5,29},{6,30},{7,31},{8,16},{9,... | collective-permute-start | bytes 552968 | tf_op jit(solution)/shard_map/ppermute | solution.py:370
  311.3 2.7 collective-permute-start.40
  315.7 7.7 %collective-permute-done.36 = bf16[48,1920]{1,0:T(8,128)(2,1)} collective-permute-done((bf16[48,1920]{1,0:T(8,128)(2,1)}, bf16[48,1920]{1,0:T(8,128)(2,1)}, u32[]{:S(2)}, u32[]{:S(2)}) %collective-permute-start.36) | collective-permute-done | bytes 184352 | tf_op jit(solution)/shard_map/ppermute | solution.py:370
  324.6 4.7 %collective-permute-done.39 = bf16[60,1152]{1,0:T(8,128)(2,1)S(1)} collective-permute-done((bf16[60,1152]{1,0:T(8,128)(2,1)S(1)}, bf16[60,1152]{1,0:T(8,128)(2,1)S(1)}, u32[]{:S(2)}, u32[]{:S(2)}) %collective-permute-start.39) | collective-permute-done | bytes 138272 | tf_op jit(solution)/shard_map/ppermute | solution.py:370
  (292 shorter events, 112.1 us)
Async XLA Ops:
  1.9 9.1 %collective-permute-start.3 = (bf16[48,1152]{1,0:T(8,128)(2,1)S(1)}, bf16[48,1152]{1,0:T(8,128)(2,1)S(1)}, u32[]{:S(2)}, u32[]{:S(2)}) collective-permute-start(bf16[48,1152]{1,0:T(8,128)(2,1)S(1)} %reshape.215), channel_id=1, source_target_pairs={{0,24},{1,25},{2,26},{3,27},{4,28},{5,29},{6,30},{7,31},{8,16},{9,... | collective-permute-start | bytes 331784 | tf_op jit(solution)/shard_map/ppermute | solution.py:370
  7.0 9.3 %collective-permute-start.2 = (bf16[48,1152]{1,0:T(8,128)(2,1)S(1)}, bf16[48,1152]{1,0:T(8,128)(2,1)S(1)}, u32[]{:S(2)}, u32[]{:S(2)}) collective-permute-start(bf16[48,1152]{1,0:T(8,128)(2,1)S(1)} %reshape.215), channel_id=1, source_target_pairs={{0,16},{1,17},{2,18},{3,19},{4,20},{5,21},{6,22},{7,23},{8,24},{9,... | collective-permute-start | bytes 331784 | tf_op jit(solution)/shard_map/ppermute | solution.py:370
  7.0 9.3 %collective-permute-start.1 = (bf16[48,1152]{1,0:T(8,128)(2,1)S(1)}, bf16[48,1152]{1,0:T(8,128)(2,1)S(1)}, u32[]{:S(2)}, u32[]{:S(2)}) collective-permute-start(bf16[48,1152]{1,0:T(8,128)(2,1)S(1)} %reshape.215), channel_id=1, source_target_pairs={{0,8},{1,9},{2,10},{3,11},{4,12},{5,13},{6,14},{7,15},{8,0},{9,1},... | collective-permute-start | bytes 331784 | tf_op jit(solution)/shard_map/ppermute | solution.py:370
  18.0 25.8 %collective-permute-start = (bf16[768,768]{1,0:T(8,128)(2,1)}, bf16[768,768]{1,0:T(8,128)(2,1)}, u32[]{:S(2)}, u32[]{:S(2)}) collective-permute-start(bf16[768,768]{1,0:T(8,128)(2,1)} %param.16), channel_id=1, source_target_pairs={{0,1},{1,0},{2,3},{3,2},{4,5},{5,4},{6,7},{7,6},{8,9},{9,8},{10,11... | collective-permute-start | bytes 3538952 | tf_op jit(solution)/shard_map/ppermute | solution.py:382
  25.9 20.6 %collective-permute-start.8 = (bf16[2,4,48,1152]{3,2,1,0:T(8,128)(2,1)}, bf16[2,4,48,1152]{3,2,1,0:T(8,128)(2,1)}, u32[]{:S(2)}, u32[]{:S(2)}) collective-permute-start(bf16[2,4,48,1152]{3,2,1,0:T(8,128)(2,1)} %pad_maximum_fusion.10), channel_id=1, source_target_pairs={{0,4},{1,3},{2,6},{3,1},{4,0},{5,7},{6,2},{7,5},{8,12},{9,11},{10,... | collective-permute-start | bytes 2654216 | tf_op jit(solution)/shard_map/ppermute | solution.py:370
  27.4 9.4 %collective-permute-start.6 = (bf16[48,1920]{1,0:T(8,128)(2,1)S(1)}, bf16[48,1920]{1,0:T(8,128)(2,1)S(1)}, u32[]{:S(2)}, u32[]{:S(2)}) collective-permute-start(bf16[48,1920]{1,0:T(8,128)(2,1)S(1)} %pad_maximum_fusion.22), channel_id=1, source_target_pairs={{0,24},{1,25},{2,26},{3,27},{4,28},{5,29},{6,30},{7,31},{8,16},{9,... | collective-permute-start | bytes 552968 | tf_op jit(solution)/shard_map/ppermute | solution.py:370
  29.9 13.7 %collective-permute-start.5 = (bf16[48,1920]{1,0:T(8,128)(2,1)S(1)}, bf16[48,1920]{1,0:T(8,128)(2,1)S(1)}, u32[]{:S(2)}, u32[]{:S(2)}) collective-permute-start(bf16[48,1920]{1,0:T(8,128)(2,1)S(1)} %pad_maximum_fusion.22), channel_id=1, source_target_pairs={{0,16},{1,17},{2,18},{3,19},{4,20},{5,21},{6,22},{7,23},{8,24},{9,... | collective-permute-start | bytes 552968 | tf_op jit(solution)/shard_map/ppermute | solution.py:370
  29.9 13.7 %collective-permute-start.4 = (bf16[48,1920]{1,0:T(8,128)(2,1)S(1)}, bf16[48,1920]{1,0:T(8,128)(2,1)S(1)}, u32[]{:S(2)}, u32[]{:S(2)}) collective-permute-start(bf16[48,1920]{1,0:T(8,128)(2,1)S(1)} %pad_maximum_fusion.22), channel_id=1, source_target_pairs={{0,8},{1,9},{2,10},{3,11},{4,12},{5,13},{6,14},{7,15},{8,0},{9,1},... | collective-permute-start | bytes 552968 | tf_op jit(solution)/shard_map/ppermute | solution.py:370
  49.3 12.1 %collective-permute-start.12 = (bf16[48,1536]{1,0:T(8,128)(2,1)S(1)}, bf16[48,1536]{1,0:T(8,128)(2,1)S(1)}, u32[]{:S(2)}, u32[]{:S(2)}) collective-permute-start(bf16[48,1536]{1,0:T(8,128)(2,1)S(1)} %copy-done.34), channel_id=1, source_target_pairs={{0,24},{1,25},{2,26},{3,27},{4,28},{5,29},{6,30},{7,31},{8,16},{9,... | collective-permute-start | bytes 442376 | tf_op jit(solution)/shard_map/ppermute | solution.py:370
  51.6 11.2 %collective-permute-start.11 = (bf16[48,1536]{1,0:T(8,128)(2,1)S(1)}, bf16[48,1536]{1,0:T(8,128)(2,1)S(1)}, u32[]{:S(2)}, u32[]{:S(2)}) collective-permute-start(bf16[48,1536]{1,0:T(8,128)(2,1)S(1)} %copy-done.34), channel_id=1, source_target_pairs={{0,16},{1,17},{2,18},{3,19},{4,20},{5,21},{6,22},{7,23},{8,24},{9,... | collective-permute-start | bytes 442376 | tf_op jit(solution)/shard_map/ppermute | solution.py:370
  51.6 11.2 %collective-permute-start.10 = (bf16[48,1536]{1,0:T(8,128)(2,1)S(1)}, bf16[48,1536]{1,0:T(8,128)(2,1)S(1)}, u32[]{:S(2)}, u32[]{:S(2)}) collective-permute-start(bf16[48,1536]{1,0:T(8,128)(2,1)S(1)} %copy-done.34), channel_id=1, source_target_pairs={{0,8},{1,9},{2,10},{3,11},{4,12},{5,13},{6,14},{7,15},{8,0},{9,1},... | collective-permute-start | bytes 442376 | tf_op jit(solution)/shard_map/ppermute | solution.py:370
  53.7 11.5 %collective-permute-start.9 = (bf16[4,48,1920]{2,1,0:T(8,128)(2,1)S(1)}, bf16[4,48,1920]{2,1,0:T(8,128)(2,1)S(1)}, u32[]{:S(2)}, u32[]{:S(2)}) collective-permute-start(bf16[4,48,1920]{2,1,0:T(8,128)(2,1)S(1)} %pad_maximum_fusion.11.refs_0_), channel_id=1, source_target_pairs={{0,2},{1,5},{2,0},{3,7},{4,6},{5,1},{6,4},{7,3},{8,10},{9,13},{10,... | collective-permute-start | bytes 2211848 | tf_op jit(solution)/shard_map/ppermute | solution.py:370
  66.5 29.8 %collective-permute-start.13 = (bf16[2,4,48,1920]{3,2,1,0:T(8,128)(2,1)}, bf16[2,4,48,1920]{3,2,1,0:T(8,128)(2,1)S(1)}, u32[]{:S(2)}, u32[]{:S(2)}) collective-permute-start(bf16[2,4,48,1920]{3,2,1,0:T(8,128)(2,1)} %pad_maximum_fusion.5), channel_id=1, source_target_pairs={{0,4},{1,3},{2,6},{3,1},{4,0},{5,7},{6,2},{7,5},{8,12},{9,11},{10,... | collective-permute-start | bytes 4423688 | tf_op jit(solution)/shard_map/ppermute | solution.py:370
  68.7 27.6 %collective-permute-start.14 = (bf16[4,48,1536]{2,1,0:T(8,128)(2,1)S(1)}, bf16[4,48,1536]{2,1,0:T(8,128)(2,1)S(1)}, u32[]{:S(2)}, u32[]{:S(2)}) collective-permute-start(bf16[4,48,1536]{2,1,0:T(8,128)(2,1)S(1)} %pad_maximum_fusion.12.refs_0_), channel_id=1, source_target_pairs={{0,2},{1,5},{2,0},{3,7},{4,6},{5,1},{6,4},{7,3},{8,10},{9,13},{10,... | collective-permute-start | bytes 1769480 | tf_op jit(solution)/shard_map/ppermute | solution.py:370
  109.8 16.3 %collective-permute-start.17 = (bf16[2,4,48,1536]{3,2,1,0:T(8,128)(2,1)S(1)}, bf16[2,4,48,1536]{3,2,1,0:T(8,128)(2,1)S(1)}, u32[]{:S(2)}, u32[]{:S(2)}) collective-permute-start(bf16[2,4,48,1536]{3,2,1,0:T(8,128)(2,1)S(1)} %pad_maximum_fusion.8), channel_id=1, source_target_pairs={{0,4},{1,3},{2,6},{3,1},{4,0},{5,7},{6,2},{7,5},{8,12},{9,11},{10,... | collective-permute-start | bytes 3538952 | tf_op jit(solution)/shard_map/ppermute | solution.py:370
  170.7 31.0 %collective-permute-start.22 = (bf16[384,1536]{1,0:T(8,128)(2,1)}, bf16[384,1536]{1,0:T(8,128)(2,1)}, u32[]{:S(2)}, u32[]{:S(2)}) collective-permute-start(bf16[384,1536]{1,0:T(8,128)(2,1)} %pad_maximum_fusion.9), channel_id=1, source_target_pairs={{0,2},{1,5},{2,0},{3,7},{4,6},{5,1},{6,4},{7,3},{8,10},{9,13},{10,... | collective-permute-start | bytes 3538952 | tf_op jit(solution)/shard_map/ppermute | solution.py:370
  183.9 10.1 %collective-permute-start.21 = (bf16[768,768]{1,0:T(8,128)(2,1)}, bf16[768,768]{1,0:T(8,128)(2,1)}, u32[]{:S(2)}, u32[]{:S(2)}) collective-permute-start(bf16[768,768]{1,0:T(8,128)(2,1)} %convert_element_type.302), channel_id=1, source_target_pairs={{0,1},{1,0},{2,3},{3,2},{4,5},{5,4},{6,7},{7,6},{8,9},{9,8},{10,11... | collective-permute-start | bytes 3538952 | tf_op jit(solution)/shard_map/ppermute | solution.py:382
  203.8 40.5 %collective-permute-start.24 = (bf16[192,1536]{1,0:T(8,128)(2,1)}, bf16[192,1536]{1,0:T(8,128)(2,1)}, u32[]{:S(2)}, u32[]{:S(2)}) collective-permute-start(bf16[192,1536]{1,0:T(8,128)(2,1)} %fusion.41), channel_id=1, source_target_pairs={{0,4},{1,3},{2,6},{3,1},{4,0},{5,7},{6,2},{7,5},{8,12},{9,11},{10,... | collective-permute-start | bytes 1769480 | tf_op jit(solution)/shard_map/ppermute | solution.py:370
  205.7 38.6 %collective-permute-start.23 = (bf16[384,1920]{1,0:T(8,128)(2,1)}, bf16[384,1920]{1,0:T(8,128)(2,1)S(1)}, u32[]{:S(2)}, u32[]{:S(2)}) collective-permute-start(bf16[384,1920]{1,0:T(8,128)(2,1)} %maximum_maximum_fusion), channel_id=1, source_target_pairs={{0,2},{1,5},{2,0},{3,7},{4,6},{5,1},{6,4},{7,3},{8,10},{9,13},{10,... | collective-permute-start | bytes 4423688 | tf_op jit(solution)/shard_map/ppermute | solution.py:370
  247.8 37.5 %collective-permute-start.29 = (bf16[48,1536]{1,0:T(8,128)(2,1)}, bf16[48,1536]{1,0:T(8,128)(2,1)}, u32[]{:S(2)}, u32[]{:S(2)}) collective-permute-start(bf16[48,1536]{1,0:T(8,128)(2,1)} %get-tuple-element.153), channel_id=1, source_target_pairs={{0,24},{1,25},{2,26},{3,27},{4,28},{5,29},{6,30},{7,31},{8,16},{9,... | collective-permute-start | bytes 442376 | tf_op jit(solution)/shard_map/ppermute | solution.py:370
  251.5 33.8 %collective-permute-start.28 = (bf16[48,1536]{1,0:T(8,128)(2,1)}, bf16[48,1536]{1,0:T(8,128)(2,1)}, u32[]{:S(2)}, u32[]{:S(2)}) collective-permute-start(bf16[48,1536]{1,0:T(8,128)(2,1)} %get-tuple-element.154), channel_id=1, source_target_pairs={{0,16},{1,17},{2,18},{3,19},{4,20},{5,21},{6,22},{7,23},{8,24},{9,... | collective-permute-start | bytes 442376 | tf_op jit(solution)/shard_map/ppermute | solution.py:370
  251.5 33.8 %collective-permute-start.27 = (bf16[48,1536]{1,0:T(8,128)(2,1)}, bf16[48,1536]{1,0:T(8,128)(2,1)}, u32[]{:S(2)}, u32[]{:S(2)}) collective-permute-start(bf16[48,1536]{1,0:T(8,128)(2,1)} %get-tuple-element.155), channel_id=1, source_target_pairs={{0,8},{1,9},{2,10},{3,11},{4,12},{5,13},{6,14},{7,15},{8,0},{9,1},... | collective-permute-start | bytes 442376 | tf_op jit(solution)/shard_map/ppermute | solution.py:370
  253.3 32.0 %collective-permute-start.26 = (bf16[192,1920]{1,0:T(8,128)(2,1)}, bf16[192,1920]{1,0:T(8,128)(2,1)}, u32[]{:S(2)}, u32[]{:S(2)}) collective-permute-start(bf16[192,1920]{1,0:T(8,128)(2,1)} %add_convert_fusion.4), channel_id=1, source_target_pairs={{0,4},{1,3},{2,6},{3,1},{4,0},{5,7},{6,2},{7,5},{8,12},{9,11},{10,... | collective-permute-start | bytes 2211848 | tf_op jit(solution)/shard_map/ppermute | solution.py:370
  259.6 25.7 %collective-permute-start.25 = (bf16[384,768]{1,0:T(8,128)(2,1)}, bf16[384,768]{1,0:T(8,128)(2,1)}, u32[]{:S(2)}, u32[]{:S(2)}) collective-permute-start(bf16[384,768]{1,0:T(8,128)(2,1)} %pad_maximum_fusion.13), channel_id=1, source_target_pairs={{0,2},{1,5},{2,0},{3,7},{4,6},{5,1},{6,4},{7,3},{8,10},{9,13},{10,... | collective-permute-start | bytes 1769480 | tf_op jit(solution)/shard_map/ppermute | solution.py:370
  294.0 11.3 %collective-permute-start.33 = (bf16[192,768]{1,0:T(8,128)(2,1)S(1)}, bf16[192,768]{1,0:T(8,128)(2,1)S(1)}, u32[]{:S(2)}, u32[]{:S(2)}) collective-permute-start(bf16[192,768]{1,0:T(8,128)(2,1)S(1)} %fusion.49), channel_id=1, source_target_pairs={{0,4},{1,3},{2,6},{3,1},{4,0},{5,7},{6,2},{7,5},{8,12},{9,11},{10,... | collective-permute-start | bytes 884744 | tf_op jit(solution)/shard_map/ppermute | solution.py:370
  294.7 9.7 %collective-permute-start.32 = (bf16[420,384]{1,0:T(8,128)(2,1)S(1)}, bf16[420,384]{1,0:T(8,128)(2,1)S(1)}, u32[]{:S(2)}, u32[]{:S(2)}) collective-permute-start(bf16[420,384]{1,0:T(8,128)(2,1)S(1)} %pad_maximum_fusion.15), channel_id=1, source_target_pairs={{0,2},{1,5},{2,0},{3,7},{4,6},{5,1},{6,4},{7,3},{8,10},{9,13},{10,... | collective-permute-start | bytes 967688 | tf_op jit(solution)/shard_map/ppermute | solution.py:370
  295.7 18.3 %collective-permute-start.35 = (bf16[48,1920]{1,0:T(8,128)(2,1)}, bf16[48,1920]{1,0:T(8,128)(2,1)}, u32[]{:S(2)}, u32[]{:S(2)}) collective-permute-start(bf16[48,1920]{1,0:T(8,128)(2,1)} %get-tuple-element.148), channel_id=1, source_target_pairs={{0,8},{1,9},{2,10},{3,11},{4,12},{5,13},{6,14},{7,15},{8,0},{9,1},... | collective-permute-start | bytes 552968 | tf_op jit(solution)/shard_map/ppermute | solution.py:370
  297.0 18.7 %collective-permute-start.37 = (bf16[48,1920]{1,0:T(8,128)(2,1)}, bf16[48,1920]{1,0:T(8,128)(2,1)}, u32[]{:S(2)}, u32[]{:S(2)}) collective-permute-start(bf16[48,1920]{1,0:T(8,128)(2,1)} %get-tuple-element.149), channel_id=1, source_target_pairs={{0,24},{1,25},{2,26},{3,27},{4,28},{5,29},{6,30},{7,31},{8,16},{9,... | collective-permute-start | bytes 552968 | tf_op jit(solution)/shard_map/ppermute | solution.py:370
  304.4 19.1 %collective-permute-start.36 = (bf16[48,1920]{1,0:T(8,128)(2,1)}, bf16[48,1920]{1,0:T(8,128)(2,1)}, u32[]{:S(2)}, u32[]{:S(2)}) collective-permute-start(bf16[48,1920]{1,0:T(8,128)(2,1)} %get-tuple-element.150), channel_id=1, source_target_pairs={{0,16},{1,17},{2,18},{3,19},{4,20},{5,21},{6,22},{7,23},{8,24},{9,... | collective-permute-start | bytes 552968 | tf_op jit(solution)/shard_map/ppermute | solution.py:370
  311.3 13.3 %collective-permute-start.40 = (bf16[60,1152]{1,0:T(8,128)(2,1)S(1)}, bf16[60,1152]{1,0:T(8,128)(2,1)S(1)}, u32[]{:S(2)}, u32[]{:S(2)}) collective-permute-start(bf16[60,1152]{1,0:T(8,128)(2,1)S(1)} %get-tuple-element.171), channel_id=1, source_target_pairs={{0,24},{1,25},{2,26},{3,27},{4,28},{5,29},{6,30},{7,31},{8,16},{9,... | collective-permute-start | bytes 414728 | tf_op jit(solution)/shard_map/ppermute | solution.py:370
  314.0 15.4 %collective-permute-start.39 = (bf16[60,1152]{1,0:T(8,128)(2,1)S(1)}, bf16[60,1152]{1,0:T(8,128)(2,1)S(1)}, u32[]{:S(2)}, u32[]{:S(2)}) collective-permute-start(bf16[60,1152]{1,0:T(8,128)(2,1)S(1)} %get-tuple-element.172), channel_id=1, source_target_pairs={{0,16},{1,17},{2,18},{3,19},{4,20},{5,21},{6,22},{7,23},{8,24},{9,... | collective-permute-start | bytes 414728 | tf_op jit(solution)/shard_map/ppermute | solution.py:370
  314.0 15.3 %collective-permute-start.38 = (bf16[60,1152]{1,0:T(8,128)(2,1)S(1)}, bf16[60,1152]{1,0:T(8,128)(2,1)S(1)}, u32[]{:S(2)}, u32[]{:S(2)}) collective-permute-start(bf16[60,1152]{1,0:T(8,128)(2,1)S(1)} %get-tuple-element.173), channel_id=1, source_target_pairs={{0,8},{1,9},{2,10},{3,11},{4,12},{5,13},{6,14},{7,15},{8,0},{9,1},... | collective-permute-start | bytes 414728 | tf_op jit(solution)/shard_map/ppermute | solution.py:370
  (66 other events, 515.6 us)
